TPU v7x, 32 devices: a whole 2x2x4 slice. The times are simulated.
32 devices in a mesh: dp: 8 (over y, x, core), tensor: 4 (over z).
Axes of the slice: x: 2, y: 2, z: 4, core: 2. Of those that a mesh axis runs over, the one named last changes fastest.
Arguments:
- tokens: bfloat16 [32, 1024, 768], P('dp', 'tensor'), may hold values from -6 to 6
- segment_ids: int32 [32, 1024], P('dp'), may hold values from 0 to 3, never falling along the last dimension, each value on 1 to 512 neighbouring positions
- drop_flags: int32 [32], P('dp'), may hold values 0 or 1
- query_key_value_weight: bfloat16 [3, 768, 768], P(None, 'dp', 'tensor'), may hold values from -0.21875 to 0.21875
- query_value_bias: float32 [2, 768], replicated, may hold values from -3 to 3
- attention_output_weight: bfloat16 [768, 768], P('tensor', 'dp'), may hold values from -0.875 to 0.875
- attention_output_bias: float32 [768], replicated, may hold values from -2 to 2
- gain_one: float32 [768], replicated, may hold values from 0.5 to 1.5
- shift_one: float32 [768], replicated, may hold values from -2 to 2
- up_projection_weight: bfloat16 [768, 3072], P('dp', 'tensor'), may hold values from -0.21875 to 0.21875
- hidden_layer_bias: float32 [3072], replicated, may hold values from -3 to 3
- down_projection_weight: bfloat16 [3072, 768], P('tensor', 'dp'), may hold values from -0.109375 to 0.109375
- down_projection_bias: float32 [768], replicated, may hold values from -2 to 2
- gain_two: float32 [768], replicated, may hold values from 0.5 to 1.5
- shift_two: float32 [768], replicated, may hold values from -2 to 2
- cotangent: bfloat16 [32, 1024, 768], P('dp', 'tensor'), may hold values from -6 to 6
Outputs:
- layer_out: bfloat16 [32, 1024, 768], P('dp', 'tensor')
- grad_tokens: float32 [32, 1024, 768], P('dp', 'tensor')
- grad_w_qkv: float32 [3, 768, 768], P(None, 'dp', 'tensor')
- grad_bias_qv: float32 [2, 768], replicated
- grad_w_out: float32 [768, 768], P('tensor', 'dp')
- grad_bias_out: float32 [768], replicated
- grad_gain_one: float32 [768], replicated
- grad_shift_one: float32 [768], replicated
- expansion_factor_sensitivity: float32 [768, 3072], P('dp', 'tensor')
- grad_bias_in: float32 [3072], replicated
- grad_w_back: float32 [3072, 768], P('tensor', 'dp')
- grad_bias_back: float32 [768], replicated
- grad_gain_two: float32 [768], replicated
- grad_shift_two: float32 [768], replicated
Inputs may be any that keep to these rules, and one draw needn't show every extreme that they name: `segment_ids`: along each sequence the ids never fall and every id from 0 to 3 appears; a document holds at most 512 positions. `drop_flags`: A 1 makes the layer the identity for that sequence.
All inputs are finite; a program needn't handle non-finite values. No bound on the sum of `drop_flags` on one device may be relied on, other than what follows from the above.
Results may differ from a plain program's by a relative error of at most 0.017.
Values may be sent and summed in bfloat16 or wider, within the bound.
A program may use at most 192 MiB of HBM per device.

v0:
```python
import jax
import jax.numpy as jnp
from jax import lax
from jax.sharding import PartitionSpec as P

HD = 64


norm_eps = 1e-05
mask_value = -1000000000.0
root_half = 0.7071067811865476
inv_root_two_pi = 0.3989422804014327


def gelu_value(preactivation):
    return 0.5 * preactivation * (1.0 + lax.erf(preactivation * root_half))


def gelu_slope(preactivation):
    return (
        0.5 * (1.0 + lax.erf(preactivation * root_half))
        + preactivation * jnp.exp(-0.5 * preactivation * preactivation) * inv_root_two_pi
    )


def norm_forward(rows_in, gain_vec, shift_vec):
    row_mean = jnp.mean(rows_in, axis=-1, keepdims=True)
    mean_shifted_entries = rows_in - row_mean
    inv_std = lax.rsqrt(
        jnp.mean(mean_shifted_entries * mean_shifted_entries, axis=-1, keepdims=True) + norm_eps
    )
    normed = mean_shifted_entries * inv_std
    return (normed * gain_vec + shift_vec, normed, inv_std)


def norm_backward(grad_out, normed, inv_std, gain_vec):
    grad_norm = grad_out * gain_vec
    return inv_std * (
        grad_norm
        - jnp.mean(grad_norm, axis=-1, keepdims=True)
        - normed * jnp.mean(grad_norm * normed, axis=-1, keepdims=True)
    )


def doc_scores(query_matrix, key_matrix, document_label_line):
    same_doc = document_label_line[:, None] == document_label_line[None, :]
    scores = (
        jnp.einsum("qhd,khd->hqk", query_matrix, key_matrix, preferred_element_type=jnp.float32)
        * 0.125
    )
    return jnp.where(same_doc[None], scores, mask_value)


def attend_forward(input_rows):
    query_matrix, key_matrix, value_matrix, document_label_line = input_rows
    scores = doc_scores(query_matrix, key_matrix, document_label_line)
    top_score = jnp.max(scores, axis=-1, keepdims=True)
    weights = jnp.exp(scores - top_score)
    totals = jnp.sum(weights, axis=-1, keepdims=True)
    probs = (weights / totals).astype(jnp.bfloat16)
    attended_rows = jnp.einsum(
        "hqk,khd->qhd", probs, value_matrix, preferred_element_type=jnp.float32
    )
    return (attended_rows.astype(jnp.bfloat16), (top_score + jnp.log(totals))[..., 0])


def attend_backward(input_rows):
    query_matrix, key_matrix, value_matrix, grad_att, log_total, document_label_line = input_rows
    scores = doc_scores(query_matrix, key_matrix, document_label_line)
    probs = jnp.exp(scores - log_total[..., None])
    probs_low = probs.astype(jnp.bfloat16)
    grad_values = jnp.einsum(
        "hqk,qhd->khd", probs_low, grad_att, preferred_element_type=jnp.float32
    )
    grad_probs = jnp.einsum(
        "qhd,khd->hqk", grad_att, value_matrix, preferred_element_type=jnp.float32
    )
    inner = jnp.sum(probs * grad_probs, axis=-1, keepdims=True)
    grad_scores = (probs * (grad_probs - inner)).astype(jnp.bfloat16)
    grad_queries = (
        jnp.einsum("hqk,khd->qhd", grad_scores, key_matrix, preferred_element_type=jnp.float32)
        * 0.125
    )
    grad_keys = (
        jnp.einsum("hqk,qhd->khd", grad_scores, query_matrix, preferred_element_type=jnp.float32)
        * 0.125
    )
    return (
        grad_queries.astype(jnp.bfloat16),
        grad_keys.astype(jnp.bfloat16),
        grad_values.astype(jnp.bfloat16),
    )


def on_device(
    tokens,
    segment_ids,
    drop_flags,
    query_key_value_weight,
    query_value_bias,
    attention_output_weight,
    attention_output_bias,
    gain_one,
    shift_one,
    up_projection_weight,
    hidden_layer_bias,
    down_projection_weight,
    down_projection_bias,
    gain_two,
    shift_two,
    cotangent,
):
    tensor_index = lax.axis_index("tensor")
    zero_index = jnp.zeros((), jnp.int32)
    seq_count = tokens.shape[0]
    width_local = query_key_value_weight.shape[2]
    hidden_local = up_projection_weight.shape[1]
    heads_local = width_local // HD
    rows_local = tokens.shape[1]
    row_start = tensor_index * rows_local
    (
        query_key_value_complete,
        output_weight_complete,
        up_weight_complete,
        contraction_factor_entire,
    ) = (
        lax.all_gather(query_key_value_weight, "dp", axis=1, tiled=True),
        lax.all_gather(attention_output_weight, "dp", axis=1, tiled=True),
        lax.all_gather(up_projection_weight, "dp", axis=0, tiled=True),
        lax.all_gather(down_projection_weight, "dp", axis=1, tiled=True),
    )
    bias_cols = lax.dynamic_slice_in_dim(
        query_value_bias, tensor_index * width_local, width_local, 1
    )
    collected_rows = lax.all_gather(tokens, "tensor", axis=1, tiled=True)
    length = collected_rows.shape[1]
    projected_rows = jnp.einsum(
        "tnu,wue->wtne",
        collected_rows,
        query_key_value_complete,
        preferred_element_type=jnp.float32,
    )
    query_matrix = (
        (projected_rows[0] + bias_cols[0])
        .astype(jnp.bfloat16)
        .reshape(seq_count, length, heads_local, HD)
    )
    key_matrix = projected_rows[1].astype(jnp.bfloat16).reshape(seq_count, length, heads_local, HD)
    value_matrix = (
        (projected_rows[2] + bias_cols[1])
        .astype(jnp.bfloat16)
        .reshape(seq_count, length, heads_local, HD)
    )
    attended_rows, log_total = lax.map(
        attend_forward, (query_matrix, key_matrix, value_matrix, segment_ids)
    )
    attended_rows = attended_rows.reshape(seq_count, length, width_local)
    partial_value = jnp.einsum(
        "qbp,pz->qbz", attended_rows, output_weight_complete, preferred_element_type=jnp.float32
    )
    summed = lax.psum(partial_value, "tensor")
    hidden_full, normed_full, inv_full = norm_forward(
        collected_rows.astype(jnp.float32) + summed + attention_output_bias, gain_one, shift_one
    )
    hidden_narrow_complete = hidden_full.astype(jnp.bfloat16)
    hidden = lax.dynamic_slice_in_dim(hidden_full, row_start, rows_local, 1)
    normed_one = lax.dynamic_slice_in_dim(normed_full, row_start, rows_local, 1)
    inv_one = lax.dynamic_slice_in_dim(inv_full, row_start, rows_local, 1)
    token_float = tokens.astype(jnp.float32)
    bias_up = lax.dynamic_slice_in_dim(hidden_layer_bias, tensor_index * hidden_local, hidden_local)
    preactivation = (
        jnp.einsum(
            "jxq,qz->jxz",
            hidden_narrow_complete,
            up_weight_complete,
            preferred_element_type=jnp.float32,
        )
        + bias_up
    )
    activation_narrow = gelu_value(preactivation).astype(jnp.bfloat16)
    feedforward_portion = jnp.einsum(
        "obq,qg->obg",
        activation_narrow,
        contraction_factor_entire,
        preferred_element_type=jnp.float32,
    )
    ffn_sum = lax.psum_scatter(
        feedforward_portion.astype(jnp.bfloat16), "tensor", scatter_dimension=1, tiled=True
    ).astype(jnp.float32)
    final, normed_two, inv_two = norm_forward(
        hidden + ffn_sum + down_projection_bias, gain_two, shift_two
    )
    dropped = drop_flags[:, None, None] == 1
    layer_out = jnp.where(dropped, token_float, final).astype(jnp.bfloat16)
    cot_float = cotangent.astype(jnp.float32)
    grad_final = jnp.where(dropped, 0.0, cot_float)
    grad_tokens = jnp.where(dropped, cot_float, 0.0)
    grad_gain_two = jnp.sum(grad_final * normed_two, axis=(0, 1))
    grad_shift_two = jnp.sum(grad_final, axis=(0, 1))
    grad_fpre = norm_backward(grad_final, normed_two, inv_two, gain_two)
    grad_branch_two = grad_fpre.astype(jnp.bfloat16)
    grad_bias_back = jnp.sum(grad_branch_two.astype(jnp.float32), axis=(0, 1))
    token_line_sensitivity = lax.all_gather(grad_branch_two, "tensor", axis=1, tiled=True)
    down_projection_gradient = jnp.einsum(
        "euj,euv->jv", activation_narrow, token_line_sensitivity, preferred_element_type=jnp.float32
    )
    activation_gradient = jnp.einsum(
        "eli,si->els",
        token_line_sensitivity,
        contraction_factor_entire,
        preferred_element_type=jnp.float32,
    )
    pregelu_sensitivity_entries = (activation_gradient * gelu_slope(preactivation)).astype(
        jnp.bfloat16
    )
    grad_bias_up = jnp.sum(pregelu_sensitivity_entries.astype(jnp.float32), axis=(0, 1))
    grad_up = jnp.einsum(
        "azt,azu->tu",
        hidden_narrow_complete,
        pregelu_sensitivity_entries,
        preferred_element_type=jnp.float32,
    )
    input_portion_gradient = jnp.einsum(
        "jtz,rz->jtr",
        pregelu_sensitivity_entries,
        up_weight_complete,
        preferred_element_type=jnp.float32,
    )
    grad_h_ffn = lax.psum_scatter(
        input_portion_gradient.astype(jnp.bfloat16), "tensor", scatter_dimension=1, tiled=True
    ).astype(jnp.float32)
    inner_grads = lax.dynamic_update_slice(
        jnp.zeros(hidden_layer_bias.shape, jnp.float32),
        grad_bias_up,
        (tensor_index * hidden_local,),
    )
    grad_hidden = grad_fpre + grad_h_ffn
    grad_gain_one = jnp.sum(grad_hidden * normed_one, axis=(0, 1))
    grad_shift_one = jnp.sum(grad_hidden, axis=(0, 1))
    sensitivity_before_gelu = norm_backward(grad_hidden, normed_one, inv_one, gain_one)
    grad_branch = sensitivity_before_gelu.astype(jnp.bfloat16)
    grad_bias_out = jnp.sum(grad_branch.astype(jnp.float32), axis=(0, 1))
    grad_tokens = grad_tokens + sensitivity_before_gelu
    branch_row_gradient = lax.all_gather(grad_branch, "tensor", axis=1, tiled=True)
    grad_out_w = jnp.einsum(
        "xpj,xpa->ja", attended_rows, branch_row_gradient, preferred_element_type=jnp.float32
    )
    grad_att = jnp.einsum(
        "qca,ia->qci",
        branch_row_gradient,
        output_weight_complete,
        preferred_element_type=jnp.float32,
    )
    grad_att = grad_att.astype(jnp.bfloat16).reshape(seq_count, length, heads_local, HD)
    grad_queries, grad_keys, grad_values = lax.map(
        attend_backward, (query_matrix, key_matrix, value_matrix, grad_att, log_total, segment_ids)
    )
    projected_gradient = jnp.stack((grad_queries, grad_keys, grad_values)).reshape(
        3, seq_count, length, width_local
    )
    grad_qkv = jnp.einsum(
        "rvt,frvg->ftg", collected_rows, projected_gradient, preferred_element_type=jnp.float32
    )
    grad_cols = jnp.sum(projected_gradient.astype(jnp.float32), axis=(1, 2))
    grad_cols = jnp.stack((grad_cols[0], grad_cols[2]))
    grad_x_part = jnp.einsum(
        "nrxy,nay->rxa",
        projected_gradient,
        query_key_value_complete,
        preferred_element_type=jnp.float32,
    )
    grad_tokens = grad_tokens + lax.psum_scatter(
        grad_x_part.astype(jnp.bfloat16), "tensor", scatter_dimension=1, tiled=True
    ).astype(jnp.float32)
    grad_qkv, grad_out_w, grad_up, down_projection_gradient = (
        lax.psum_scatter(grad_qkv, "dp", scatter_dimension=1, tiled=True),
        lax.psum_scatter(grad_out_w, "dp", scatter_dimension=1, tiled=True),
        lax.psum_scatter(grad_up, "dp", scatter_dimension=0, tiled=True),
        lax.psum_scatter(down_projection_gradient, "dp", scatter_dimension=1, tiled=True),
    )
    column_grads = lax.dynamic_update_slice(
        jnp.zeros(query_value_bias.shape, jnp.float32),
        grad_cols,
        (zero_index, tensor_index * width_local),
    )
    row_grads = jnp.stack(
        (
            grad_bias_out,
            grad_gain_one,
            grad_shift_one,
            grad_bias_back,
            grad_gain_two,
            grad_shift_two,
        )
    )
    column_grads, inner_grads, row_grads = lax.psum(
        (column_grads, inner_grads, row_grads), ("dp", "tensor")
    )
    return (
        layer_out,
        grad_tokens,
        grad_qkv,
        column_grads,
        grad_out_w,
        row_grads[0],
        row_grads[1],
        row_grads[2],
        grad_up,
        inner_grads,
        down_projection_gradient,
        row_grads[3],
        row_grads[4],
        row_grads[5],
    )


def solution(mesh):
    return jax.shard_map(
        on_device,
        mesh=mesh,
        in_specs=(
            P("dp", "tensor", None),
            P("dp", None),
            P("dp"),
            P(None, "dp", "tensor"),
            P(),
            P("tensor", "dp"),
            P(),
            P(),
            P(),
            P("dp", "tensor"),
            P(),
            P("tensor", "dp"),
            P(),
            P(),
            P(),
            P("dp", "tensor", None),
        ),
        out_specs=(
            P("dp", "tensor", None),
            P("dp", "tensor", None),
            P(None, "dp", "tensor"),
            P(),
            P("tensor", "dp"),
            P(),
            P(),
            P(),
            P("dp", "tensor"),
            P(),
            P("tensor", "dp"),
            P(),
            P(),
            P(),
        ),
        check_vma=False,
    )
```

profile of v0, /device:TPU:0, one launch (start us, length us, event | category | flops | bytes accessed | tf_op | source)
XLA Modules:
  0.0 1582.3 jit_solution(16759258541925945061)
XLA Ops:
  11.8 11.0 all_gather.23
  22.8 13.5 all_gather.22
  36.3 92.2 %all-gather.6.cloned.1.call-done = bf16[4,1024,768]{2,1,0:T(8,128)(2,1)} async-done(((bf16[4,256,768]{2,1,0:T(8,128)(2,1)}), bf16[4,1024,768]{2,1,0:T(8,128)(2,1)}) %all-gather.6.cloned.1.call-update) | async-done | bytes 6291472 | tf_op jit(solution)/shard_map/all_gather | solution.py:135
  141.8 60.5 %while.26 = (s32[]{:T(128)}, bf16[4,1024,3,64]{1,3,2,0:T(8,128)(2,1)}, f32[4,3,1024]{2,1,0:T(4,128)}, bf16[4,1024,3,64]{1,3,2,0:T(8,128)(2,1)}, s32[4,1024]{1,0:...) while((s32[]{:T(128)}, ...), condition=%wide.region_3.4_spmd, body=%wide.region_0.3_spmd.sunk | while | flops 844297216 | bytes 47827572 | solution.py:154
  212.3 422.2 %all-reduce.3.cloned.1.call-done = f32[4,1024,768]{2,1,0:T(8,128)} async-done(((f32[4,1024,768]{2,1,0:T(8,128)}), f32[4,1024,768]{2,1,0:T(8,128)}) %all-reduce.3.cloned.1.call-update) | async-done | bytes 12582928 | tf_op jit(solution)/shard_map/psum | solution.py:161
  642.7 8.6 multiply_reduce_fusion.1
  652.7 11.1 multiply_add_fusion
  663.8 13.1 multiply_convert_fusion.1
  676.9 9.2 convolution_convert_fusion.1
  687.2 108.7 %reduce-scatter.12.cloned.1.call-done = bf16[4,256,768]{2,1,0:T(8,128)(2,1)} async-done(((bf16[4,1024,768]{2,1,0:T(8,128)(2,1)}), bf16[4,256,768]{2,1,0:T(8,128)(2,1)}) %reduce-scatter.12.cloned.1.call-update) | async-done | bytes 1572880 | tf_op jit(solution)/shard_map/reduce_scatter | solution.py:187
  806.0 115.6 %all-gather.12.cloned.1.call-done = bf16[4,1024,768]{2,1,0:T(8,128)(2,1)} async-done(((bf16[4,256,768]{2,1,0:T(8,128)(2,1)}), bf16[4,1024,768]{2,1,0:T(8,128)(2,1)}) %all-gather.12.cloned.1.call-update) | async-done | bytes 6291472 | tf_op jit(solution)/shard_map/all_gather | solution.py:203
  921.6 12.9 convert_reduce_fusion
  945.6 107.8 %reduce-scatter.14.cloned.1.call-done = bf16[4,256,768]{2,1,0:T(8,128)(2,1)} async-done(((bf16[4,1024,768]{2,1,0:T(8,128)(2,1)}), bf16[4,256,768]{2,1,0:T(8,128)(2,1)}) %reduce-scatter.14.cloned.1.call-update) | async-done | bytes 1572880 | tf_op jit(solution)/shard_map/reduce_scatter | solution.py:229
  1065.4 116.2 %all-gather.14.cloned.1.call-done = bf16[4,1024,768]{2,1,0:T(8,128)(2,1)} async-done(((bf16[4,256,768]{2,1,0:T(8,128)(2,1)}), bf16[4,1024,768]{2,1,0:T(8,128)(2,1)}) %all-gather.14.cloned.1.call-update) | async-done | bytes 6291472 | tf_op jit(solution)/shard_map/all_gather | solution.py:244
  1198.4 115.1 %while.27 = (s32[]{:T(128)}, bf16[4,1024,3,64]{1,3,2,0:T(8,128)(2,1)}, bf16[4,1024,3,64]{1,3,2,0:T(8,128)(2,1)}, bf16[4,1024,3,64]{1,3,2,0:T(8,128)(2,1)}, bf16[...) while((s32[]{:T(128)}, ...), condition=%wide.region_17.18_spmd, body=%wide.region_15.17_spmd.sunk | while | flops 2062480384 | bytes 102601840 | solution.py:255
  1230.4 8.3 multiply_reduce_fusion.7
  1313.5 9.3 fusion.92
  1328.6 9.3 bitcast_convert_fusion
  1338.0 10.2 convolution_bitcast_fusion
  1348.4 11.2 fusion.89
  1363.4 45.8 %all-reduce = (f32[2,768]{1,0:T(2,128)}, f32[6,768]{1,0:T(8,128)S(1)}, f32[3072]{0:T(1024)}) all-reduce(f32[2,768]{1,0:T(2,128)S(1)} %dynamic_update_slice.23, f32[6,768]{1,0:T(8,128)S(1)} %stack.47, f32[3072]{0:T(1024)S(1)} %dynamic_update_slice.24), channel_id=1, replica_groups=mesh['dp'=8,'tensor'=4] {'dp','tensor'}, use_global_device_ids=true, to_apply=%region_21.22 | all-reduce | flops 9216 | bytes 73728 | tf_op jit(solution)/shard_map/psum | solution.py:296
  1413.4 67.8 %reduce-scatter.16.cloned.1.call-done = bf16[4,256,768]{2,1,0:T(8,128)(2,1)} async-done(((bf16[4,1024,768]{2,1,0:T(8,128)(2,1)}), bf16[4,256,768]{2,1,0:T(8,128)(2,1)}) %reduce-scatter.16.cloned.1.call-update) | async-done | bytes 1572880 | tf_op jit(solution)/shard_map/reduce_scatter | solution.py:272
  1485.9 42.4 %reduce-scatter.20.cloned.1.call-done = f32[768,96]{0,1:T(8,128)} async-done(((f32[768,768]{0,1:T(8,128)}), f32[768,96]{0,1:T(8,128)}) %reduce-scatter.20.cloned.1.call-update) | async-done | bytes 294928 | tf_op jit(solution)/shard_map/reduce_scatter | solution.py:279
  1528.3 46.1 %reduce-scatter.18.cloned.1.call-done = f32[96,768]{1,0:T(8,128)} async-done(((f32[768,768]{1,0:T(8,128)}), f32[96,768]{1,0:T(8,128)}) %reduce-scatter.18.cloned.1.call-update) | async-done | bytes 294928 | tf_op jit(solution)/shard_map/reduce_scatter | solution.py:278
  (230 shorter events, 272.6 us)
Async XLA Ops:
  8.0 120.5 %all-gather.6.cloned.1.call-start = ((), (), s32[]{:S(2)}) async-start(), calls=%async_computation.7 | async-start | bytes 7864320 | tf_op jit(solution)/shard_map/all_gather | solution.py:135
  8.7 625.8 %all-reduce.3.cloned.1.call-start = ((), (), s32[]{:S(2)}) async-start(), calls=%async_computation.8 | async-start | bytes 25165824 | tf_op jit(solution)/shard_map/psum | solution.py:161
  36.3 99.4 %copy-start.9 = (bf16[3,768,192]{2,0,1:T(4,128)(2,1)}, bf16[3,768,192]{2,0,1:T(4,128)(2,1)S(1)}, u32[]{:S(2)}) copy-start(bf16[3,768,192]{2,0,1:T(4,128)(2,1)S(1)} %all_gather.22) | copy-start | bytes 2654212
  210.1 424.5 %copy-start.23 = (f32[768]{0:T(1024)S(1)}, f32[768]{0:T(1024)}, u32[]{:S(2)}) copy-start(f32[768]{0:T(1024)} %param.26) | copy-start | bytes 9220
  210.1 453.7 %all-gather.8.cloned.1.call-start = ((), (), s32[]{:S(2)}) async-start(), calls=%async_computation.9 | async-start | bytes 1327104 | tf_op jit(solution)/shard_map/all_gather | solution.py:129
  210.7 466.2 %all-gather.10.cloned.1.call-start = ((), (), s32[]{:S(2)}) async-start(), calls=%async_computation.10 | async-start | bytes 1327104 | tf_op jit(solution)/shard_map/all_gather | solution.py:130
  211.3 584.7 %reduce-scatter.12.cloned.1.call-start = ((), (), s32[]{:S(2)}) async-start(), calls=%async_computation.11 | async-start | bytes 7864320 | tf_op jit(solution)/shard_map/reduce_scatter | solution.py:187
  212.3 451.5 %copy-start.36 = (f32[768]{0:T(1024)}, f32[768]{0:T(1024)S(1)}, u32[]{:S(2)}) copy-start(f32[768]{0:T(1024)S(1)} %dynamic_slice.48) | copy-start | bytes 9220
  686.1 235.5 %all-gather.12.cloned.1.call-start = ((), (), s32[]{:S(2)}) async-start(), calls=%async_computation.12 | async-start | bytes 7864320 | tf_op jit(solution)/shard_map/all_gather | solution.py:203
  805.5 247.8 %reduce-scatter.14.cloned.1.call-start = ((), (), s32[]{:S(2)}) async-start(), calls=%async_computation.13 | async-start | bytes 7864320 | tf_op jit(solution)/shard_map/reduce_scatter | solution.py:229
  921.6 15.5 copy-start.37
  944.2 237.4 %all-gather.14.cloned.1.call-start = ((), (), s32[]{:S(2)}) async-start(), calls=%async_computation.14 | async-start | bytes 7864320 | tf_op jit(solution)/shard_map/all_gather | solution.py:244
  1060.4 121.3 %copy-start.7 = (bf16[4,1024,3,64]{1,3,2,0:T(8,128)(2,1)S(1)}, bf16[4,1024,3,64]{1,3,2,0:T(8,128)(2,1)}, u32[]{:S(2)}) copy-start(bf16[4,1024,3,64]{1,3,2,0:T(8,128)(2,1)} %get-tuple-element.106) | copy-start | bytes 4718596
  1065.4 344.5 %reduce-scatter.24.cloned.1.call-start = ((), (), s32[]{:S(2)}) async-start(), calls=%async_computation.19 | async-start | bytes 884736
  1187.9 223.6 %reduce-scatter.22.cloned.1.call-start = ((), (), s32[]{:S(2)}) async-start(), calls=%async_computation.18 | async-start | bytes 2211840
  1328.6 152.6 %reduce-scatter.16.cloned.1.call-start = ((), (), s32[]{:S(2)}) async-start(), calls=%async_computation.15 | async-start | bytes 7864320 | tf_op jit(solution)/shard_map/reduce_scatter | solution.py:272
  1337.9 190.3 %reduce-scatter.20.cloned.1.call-start = ((), (), s32[]{:S(2)}) async-start(), calls=%async_computation.17 | async-start | bytes 2654208 | tf_op jit(solution)/shard_map/reduce_scatter | solution.py:279
  1348.3 11.7 copy-start.31
  1348.3 226.1 %reduce-scatter.18.cloned.1.call-start = ((), (), s32[]{:S(2)}) async-start(), calls=%async_computation.16 | async-start | bytes 2654208 | tf_op jit(solution)/shard_map/reduce_scatter | solution.py:278
  1360.1 121.1 %copy-start.3 = (f32[4,256,768]{2,1,0:T(8,128)S(1)}, f32[4,256,768]{2,1,0:T(8,128)}, u32[]{:S(2)}) copy-start(f32[4,256,768]{2,1,0:T(8,128)} %copy-done.2) | copy-start | bytes 9437188
  1360.1 121.1 %copy-start.15 = (f32[768]{0:T(1024)S(1)}, f32[768]{0:T(1024)}, u32[]{:S(2)}) copy-start(f32[768]{0:T(1024)} %param.27) | copy-start | bytes 9220
  1360.1 121.1 %copy-start.18 = (f32[4,256]{1,0:T(4,128)S(1)}, f32[4,256]{1,0:T(4,128)}, u32[]{:S(2)}) copy-start(f32[4,256]{1,0:T(4,128)} %constant_dynamic-slice_fusion.2) | copy-start | bytes 12292
  1360.1 121.1 %copy-start.20 = (f32[4,256]{1,0:T(4,128)S(1)}, f32[4,256]{1,0:T(4,128)}, u32[]{:S(2)}) copy-start(f32[4,256]{1,0:T(4,128)} %copy-done.19) | copy-start | bytes 12292
  1360.1 121.1 %copy-start.22 = (f32[4,256]{1,0:T(4,128)S(1)}, f32[4,256]{1,0:T(4,128)}, u32[]{:S(2)}) copy-start(f32[4,256]{1,0:T(4,128)} %copy-done.21) | copy-start | bytes 12292
  (31 other events, 180.5 us)
Sparse Core Ops, SparseCore 0:
  10.4 118.0 all-gather.5
  210.2 424.2 all-reduce.2
  686.2 109.6 reduce-scatter.11
  805.6 115.8 all-gather.11
  944.3 108.9 reduce-scatter.13
  1065.5 116.0 all-gather.13
Sparse Core Ops, SparseCore 1:
  212.5 22.0 all-gather.7
  236.3 23.9 all-gather.9
  1188.0 33.1 reduce-scatter.23
  1328.6 38.3 reduce-scatter.21
  1369.4 111.7 reduce-scatter.15
  1485.5 42.7 reduce-scatter.19
  1532.1 42.3 reduce-scatter.17
where the time goes:
time: 1590 us; the launch traced here: 1580 us
  waiting for transfers between devices  1120 us (70%)
  matrix products  231 us (15%)
  other arithmetic  110 us (7%)
  blocking collectives  70.4 us (4%)
  local copies, waits for them, and re-layouts  31.5 us (2%)
  between operations  16.6 us (1%)
    psum x1, waiting for transfers between devices, on_device(): summed = lax.psum(partial_value, 'tensor')  422 us
    all_gather x1, waiting for transfers between devices, on_device(): lax.all_gather(grad_branch, 'tensor', axis=1, tiled=True)  116 us
    all_gather x1, waiting for transfers between devices, on_device(): lax.all_gather(grad_branch_two, 'tensor', axis=1, tiled=True)  116 us
    reduce_scatter x1, waiting for transfers between devices, on_device(): lax.psum_scatter(feedforward_portion.astype(jnp.bfloat16), 'tensor', scat...  109 us
    reduce_scatter x1, waiting for transfers between devices, on_device(): lax.psum_scatter(input_portion_gradient.astype(jnp.bfloat16), 'tensor', s...  108 us
    all_gather x1, waiting for transfers between devices, on_device(): collected_rows = lax.all_gather(tokens, 'tensor', axis=1, tiled=True)  92.2 us
    reduce_scatter x1, waiting for transfers between devices, on_device(): lax.psum_scatter(grad_x_part.astype(jnp.bfloat16), 'tensor', scatter_dime...  67.8 us
    reduce_scatter x1, waiting for transfers between devices, on_device(): lax.psum_scatter(grad_up, 'dp', scatter_dimension=0, tiled=True)  46.1 us
  transfers between devices with their start and end apart: 13, of which 9 were waited for; matrix products, arithmetic and copies ran while one was open for 15% of the time, Pallas kernels for 0%

commit v1 on v0

v1 whole, which is shorter than its diff:
```python
import functools
import jax
import jax.numpy as jnp
from jax import lax
from jax.experimental import pallas as pl
from jax.experimental.pallas import tpu as pltpu
from jax.sharding import PartitionSpec as P

HD = 64
EPS = 1e-05
NEG = -1000000000.0
BF = jnp.bfloat16
F32 = jnp.float32
VMEM_LIMIT = 60 * 1024 * 1024
BLK = 256


def dot_nn(a, b):
    return jnp.dot(a, b, preferred_element_type=F32)


def dot_nt(a, b):
    return lax.dot_general(a, b, (((1,), (1,)), ((), ())), preferred_element_type=F32)


def dot_tn(a, b):
    return lax.dot_general(a, b, (((0,), (0,)), ((), ())), preferred_element_type=F32)


def half_masks(shape):
    lane = lax.broadcasted_iota(jnp.int32, shape, 1)
    return lane < HD


def attend_kernel(lo_ref, hi_ref, q_ref, k_ref, v_ref, segc_ref, segr_ref, o_ref, lse_ref, s_scr):
    n = q_ref.shape[0] // BLK
    first = half_masks((BLK, 2 * HD))
    zero = jnp.zeros((), BF)

    def rows(i):
        return pl.ds(pl.multiple_of(i * BLK, BLK), BLK)

    def q_block(i, carry):
        q = q_ref[rows(i), :]
        qs = (jnp.where(first, q, zero), jnp.where(first, zero, q))
        segq = segc_ref[rows(i), :]
        segq = jnp.concatenate([segq] * (BLK // 128), axis=1)
        lo, hi = lo_ref[i], hi_ref[i]

        def score(j, tops):
            k = k_ref[rows(j), :]
            same = segq == segr_ref[j]
            new = []
            for h in range(2):
                s = jnp.where(same, dot_nt(qs[h], k) * 0.125, NEG)
                s_scr[h, j] = s
                top = tops[h]
                for c in range(BLK // 128):
                    top = jnp.maximum(top, s[:, c * 128 : (c + 1) * 128])
                new.append(top)
            return tuple(new)

        start = jnp.full((BLK, 128), NEG, F32)
        tops = lax.fori_loop(lo, hi, score, (start, start))
        tops = [jnp.max(t, axis=1, keepdims=True) for t in tops]

        def weigh(j, state):
            v = v_ref[rows(j), :]
            new = []
            for h in range(2):
                total, acc = state[h]
                p = jnp.exp(s_scr[h, j] - tops[h])
                for c in range(BLK // 128):
                    total = total + p[:, c * 128 : (c + 1) * 128]
                acc = acc + dot_nn(p.astype(BF), v)
                new.append((total, acc))
            return tuple(new)

        zeros = jnp.zeros((BLK, 128), F32)
        state = lax.fori_loop(lo, hi, weigh, ((zeros, zeros), (zeros, zeros)))
        outs = []
        for h in range(2):
            total = jnp.sum(state[h][0], axis=1, keepdims=True)
            outs.append(state[h][1] / total)
            lse = tops[h] + jnp.log(total)
            lse_ref[h : h + 1, rows(i)] = jnp.transpose(jnp.broadcast_to(lse, (BLK, 128)))[0:1, :]
        o_ref[rows(i), :] = jnp.where(first, outs[0], outs[1]).astype(BF)
        return carry

    lax.fori_loop(0, n, q_block, 0)


def attend(qkv, lo, hi, segc, segr):
    length, wide = qkv.shape
    d = wide // 3
    pairs = d // (2 * HD)
    n = length // BLK
    col = lambda off: pl.BlockSpec((length, 2 * HD), lambda p, *_: (0, off + p))
    return pl.pallas_call(
        attend_kernel,
        out_shape=(
            jax.ShapeDtypeStruct((length, d), BF),
            jax.ShapeDtypeStruct((pairs, 2, length), F32),
        ),
        grid_spec=pltpu.PrefetchScalarGridSpec(
            num_scalar_prefetch=2,
            grid=(pairs,),
            in_specs=[
                col(0),
                col(pairs),
                col(2 * pairs),
                pl.BlockSpec((length, 128), lambda p, *_: (0, 0)),
                pl.BlockSpec((n, 1, BLK), lambda p, *_: (0, 0, 0)),
            ],
            out_specs=[col(0), pl.BlockSpec((None, 2, length), lambda p, *_: (p, 0, 0))],
            scratch_shapes=[pltpu.VMEM((2, n, BLK, BLK), F32)],
        ),
        compiler_params=pltpu.CompilerParams(vmem_limit_bytes=VMEM_LIMIT),
        cost_estimate=pl.CostEstimate(
            flops=4 * length * length * d // 2,
            bytes_accessed=8 * length * d,
            transcendentals=length * length * d // HD // 2,
        ),
        name="attend_forward",
    )(lo, hi, qkv, qkv, qkv, segc, segr)


def attend_back_kernel(
    lo_ref, hi_ref, q_ref, k_ref, v_ref, att_ref, g_ref, lse_ref, segc_ref, segr_ref,
    gq_ref, gk_ref, gv_ref, dq_scr, delta_scr,
):
    length = q_ref.shape[0]
    n = length // BLK
    first = half_masks((BLK, 2 * HD))
    zero = jnp.zeros((), BF)

    def rows(i):
        return pl.ds(pl.multiple_of(i * BLK, BLK), BLK)

    sub = lax.broadcasted_iota(jnp.int32, (8, 2 * HD), 0)
    lane = lax.broadcasted_iota(jnp.int32, (8, 2 * HD), 1)
    pick = jnp.where(lane // HD == sub, 1.0, 0.0).astype(F32)
    prod = g_ref[...].astype(F32) * att_ref[...].astype(F32)
    delta_scr[...] = lax.dot_general(
        pick, prod, (((1,), (1,)), ((), ())),
        preferred_element_type=F32, precision=lax.Precision.HIGHEST,
    )
    dq_scr[...] = jnp.zeros_like(dq_scr)

    def k_block(j, carry):
        k = k_ref[rows(j), :]
        v = v_ref[rows(j), :]
        ks = (jnp.where(first, k, zero), jnp.where(first, zero, k))
        vs = (jnp.where(first, v, zero), jnp.where(first, zero, v))
        kcat = jnp.concatenate(ks, axis=0)
        segk = segc_ref[rows(j), :]
        segk = jnp.concatenate([segk] * (BLK // 128), axis=1)

        def q_step(i, state):
            q = q_ref[rows(i), :]
            g = g_ref[rows(i), :]
            same = segk == segr_ref[i]
            new, both = [], []
            for h in range(2):
                dk, dv = state[h]
                st = dot_nt(ks[h], q) * 0.125
                pt = jnp.where(same, jnp.exp(st - lse_ref[h : h + 1, rows(i)]), 0.0)
                dv = dv + dot_nn(pt.astype(BF), g)
                dpt = dot_nt(vs[h], g)
                dst = (pt * (dpt - delta_scr[h : h + 1, rows(i)])).astype(BF)
                dk = dk + dot_nn(dst, q)
                both.append(dst)
                new.append((dk, dv))
            dq_scr[rows(i), :] += dot_tn(jnp.concatenate(both, axis=0), kcat)
            return tuple(new)

        zeros = jnp.zeros((BLK, 2 * HD), F32)
        state = lax.fori_loop(lo_ref[j], hi_ref[j], q_step, ((zeros, zeros), (zeros, zeros)))
        gk_ref[rows(j), :] = (jnp.where(first, state[0][0], state[1][0]) * 0.125).astype(BF)
        gv_ref[rows(j), :] = jnp.where(first, state[0][1], state[1][1]).astype(BF)
        return carry

    lax.fori_loop(0, n, k_block, 0)
    gq_ref[...] = (dq_scr[...] * 0.125).astype(BF)


def attend_back(qkv, att, g_att, lse, lo, hi, segc, segr):
    length, wide = qkv.shape
    d = wide // 3
    pairs = d // (2 * HD)
    n = length // BLK
    col = lambda off: pl.BlockSpec((length, 2 * HD), lambda p, *_: (0, off + p))
    return pl.pallas_call(
        attend_back_kernel,
        out_shape=[jax.ShapeDtypeStruct((length, d), BF)] * 3,
        grid_spec=pltpu.PrefetchScalarGridSpec(
            num_scalar_prefetch=2,
            grid=(pairs,),
            in_specs=[
                col(0),
                col(pairs),
                col(2 * pairs),
                col(0),
                col(0),
                pl.BlockSpec((None, 2, length), lambda p, *_: (p, 0, 0)),
                pl.BlockSpec((length, 128), lambda p, *_: (0, 0)),
                pl.BlockSpec((n, 1, BLK), lambda p, *_: (0, 0, 0)),
            ],
            out_specs=[col(0)] * 3,
            scratch_shapes=[
                pltpu.VMEM((length, 2 * HD), F32),
                pltpu.VMEM((8, length), F32),
            ],
        ),
        compiler_params=pltpu.CompilerParams(vmem_limit_bytes=VMEM_LIMIT),
        cost_estimate=pl.CostEstimate(
            flops=10 * length * length * d // 2,
            bytes_accessed=16 * length * d,
            transcendentals=length * length * d // HD // 2,
        ),
        name="attend_backward",
    )(lo, hi, qkv, qkv, qkv, att, g_att, lse, segc, segr)


def gelu_parts(u):
    e = jnp.exp(-0.5 * u * u)
    t = 1.0 / (1.0 + (0.3275911 * 0.7071067811865476) * jnp.abs(u))
    poly = t * (
        0.5 * 0.254829592
        + t * (0.5 * -0.284496736 + t * (0.5 * 1.421413741 + t * (0.5 * -1.453152027 + t * (0.5 * 1.061405429))))
    )
    tail = poly * e
    cdf = jnp.where(u < 0.0, tail, 1.0 - tail)
    return u * cdf, cdf + u * e * 0.3989422804014327


def norm_rows(v):
    mean = jnp.mean(v, axis=-1, keepdims=True)
    c = v - mean
    inv = lax.rsqrt(jnp.mean(c * c, axis=-1, keepdims=True) + EPS)
    return c * inv, inv


def norm_back(g, normed, inv, gain):
    gn = g * gain
    return inv * (
        gn
        - jnp.mean(gn, axis=-1, keepdims=True)
        - normed * jnp.mean(gn * normed, axis=-1, keepdims=True)
    )


def middle_kernel(
    row_steps, drop_ref, att_ref, x_ref, cot_ref, wo_ref, up_ref, dn_ref, vec_ref, bin_ref,
    lo_ref, gatt_ref, ghpre_ref, gup_ref, gdn_ref, gwo_ref, vecg_ref, bing_ref,
    att_s, act_s, gpre_s, slope_s, ht_s, gb2t_s, gbt_s,
):
    step = pl.program_id(0)
    parts = up_ref.shape[0]

    @pl.when(step == 0)
    def _():
        vecg_ref[...] = jnp.zeros_like(vecg_ref)
        bing_ref[...] = jnp.zeros_like(bing_ref)

    @pl.when(step < row_steps)
    def _():
        at = pl.ds(pl.multiple_of(step * BLK, BLK), BLK)
        vec = lambda r: vec_ref[r : r + 1, :]
        dropped = drop_ref[0] == 1
        att = att_ref[...]
        att_s[at, :] = att
        x = x_ref[...].astype(F32)
        branch = dot_nt(att, wo_ref[...]) + vec(0)
        n1, inv1 = norm_rows(x + branch)
        hidden = n1 * vec(1) + vec(2)
        low = hidden.astype(BF)
        ht_s[:, at] = jnp.transpose(low)
        ffn = hidden + vec(3)
        for t in range(parts):
            pre = dot_nn(low, up_ref[t]) + bin_ref[t : t + 1, :]
            act, slope = gelu_parts(pre)
            act = act.astype(BF)
            act_s[t, at, :] = act
            slope_s[t] = slope
            ffn = ffn + dot_nt(act, dn_ref[t])
        n2, inv2 = norm_rows(ffn)
        final = n2 * vec(4) + vec(5)
        lo_ref[...] = jnp.where(dropped, x, final).astype(BF)
        g_final = jnp.where(dropped, 0.0, cot_ref[...].astype(F32))
        g_fpre = norm_back(g_final, n2, inv2, vec(4))
        gb2 = g_fpre.astype(BF)
        gb2t_s[:, at] = jnp.transpose(gb2)
        g_hidden = g_fpre
        for t in range(parts):
            gpre = (dot_nn(gb2, dn_ref[t]) * slope_s[t]).astype(BF)
            gpre_s[t, at, :] = gpre
            bing_ref[t : t + 1, :] += jnp.sum(gpre.astype(F32), axis=0, keepdims=True)
            g_hidden = g_hidden + dot_nt(gpre, up_ref[t])
        g_hpre = norm_back(g_hidden, n1, inv1, vec(1))
        gb = g_hpre.astype(BF)
        gbt_s[:, at] = jnp.transpose(gb)
        gatt_ref[...] = dot_nn(gb, wo_ref[...]).astype(BF)
        ghpre_ref[...] = g_hpre
        for r, v in enumerate(
            (gb.astype(F32), g_hidden * n1, g_hidden, gb2.astype(F32), g_final * n2, g_final)
        ):
            vecg_ref[r : r + 1, :] += jnp.sum(v, axis=0, keepdims=True)

    for t in range(parts):

        @pl.when(step == row_steps + t)
        def _():
            gup_ref[...] = dot_nn(ht_s[...], gpre_s[t]).astype(BF)
            gdn_ref[...] = dot_nn(gb2t_s[...], act_s[t]).astype(BF)

    @pl.when(step == row_steps + parts)
    def _():
        gwo_ref[...] = dot_nn(gbt_s[...], att_s[...]).astype(BF)


def middle(drop, att, x, cot, wo, up, dn, vec, bias_in):
    length, d = att.shape
    parts, _, fl = up.shape
    nr = length // BLK
    rows = pl.BlockSpec((BLK, d), lambda i: (jnp.minimum(i, nr - 1), 0))
    once = lambda shape: pl.BlockSpec(
        shape, lambda i: (0,) * len(shape), pipeline_mode=pl.Buffered(1)
    )
    part = pl.BlockSpec((None, d, fl), lambda i: (jnp.clip(i - nr, 0, parts - 1), 0, 0))
    whole = lambda shape: pl.BlockSpec(shape, lambda i: (0,) * len(shape))
    return pl.pallas_call(
        functools.partial(middle_kernel, nr),
        grid=(nr + parts + 1,),
        out_shape=(
            jax.ShapeDtypeStruct((length, d), BF),
            jax.ShapeDtypeStruct((length, d), BF),
            jax.ShapeDtypeStruct((length, d), F32),
            jax.ShapeDtypeStruct((parts, d, fl), BF),
            jax.ShapeDtypeStruct((parts, d, fl), BF),
            jax.ShapeDtypeStruct((d, d), BF),
            jax.ShapeDtypeStruct((8, d), F32),
            jax.ShapeDtypeStruct((parts, fl), F32),
        ),
        in_specs=[
            pl.BlockSpec(memory_space=pltpu.SMEM),
            rows,
            rows,
            rows,
            once((d, d)),
            once((parts, d, fl)),
            once((parts, d, fl)),
            once((8, d)),
            once((parts, fl)),
        ],
        out_specs=(rows, rows, rows, part, part, whole((d, d)), whole((8, d)), whole((parts, fl))),
        scratch_shapes=[
            pltpu.VMEM((length, d), BF),
            pltpu.VMEM((parts, length, fl), BF),
            pltpu.VMEM((parts, length, fl), BF),
            pltpu.VMEM((parts, BLK, fl), F32),
            pltpu.VMEM((d, length), BF),
            pltpu.VMEM((d, length), BF),
            pltpu.VMEM((d, length), BF),
        ],
        compiler_params=pltpu.CompilerParams(vmem_limit_bytes=VMEM_LIMIT),
        cost_estimate=pl.CostEstimate(
            flops=6 * length * d * (d + 2 * parts * fl),
            bytes_accessed=4 * length * d * 3 + 8 * parts * d * fl,
            transcendentals=2 * length * parts * fl,
        ),
        name="middle",
    )(drop, att, x, cot, wo, up, dn, vec, bias_in)


def block_range(seg):
    length = seg.shape[0]
    n = length // BLK
    blocks = seg.reshape(n, BLK)
    start = jnp.sum(seg[None, :] < blocks[:, :1], axis=1)
    end = jnp.sum(seg[None, :] <= blocks[:, -1:], axis=1)
    return (start // BLK).astype(jnp.int32), ((end + BLK - 1) // BLK).astype(jnp.int32)


def on_device(
    tokens, segment_ids, drop_flags, qkv_w, qv_b, wo_w, wo_b, gain1, shift1,
    up_w, up_b, dn_w, dn_b, gain2, shift2, cotangent,
):
    axes = ("tensor", "dp")
    me = lax.axis_index("tensor")
    nt = lax.axis_size("tensor")
    seqs, rows_local, d = tokens.shape
    length = segment_ids.shape[1]
    rw, wl = qkv_w.shape[1], qkv_w.shape[2]
    fl = up_w.shape[1]
    per = seqs // nt

    def to_seq(a):
        return lax.all_to_all(a, "tensor", 0, 1, tiled=True)

    def to_rows(a):
        return lax.all_to_all(a, "tensor", 1, 0, tiled=True)

    x_all = to_seq(tokens)
    cot_all = to_seq(cotangent)
    w1 = lax.all_gather(
        jnp.transpose(qkv_w, (1, 0, 2)).reshape(rw, 3 * wl), axes, axis=0, tiled=True
    )
    w2 = lax.all_gather(
        jnp.concatenate((up_w, dn_w.T, wo_w.T), axis=1), axes, axis=0, tiled=True
    ).reshape(nt, d, 2 * fl + wl)
    wqkv = w1.reshape(nt, d, 3, wl).transpose(1, 2, 0, 3).reshape(d, 3 * d)
    up = w2[:, :, :fl]
    dn = w2[:, :, fl : 2 * fl]
    wo = w2[:, :, 2 * fl :].transpose(1, 0, 2).reshape(d, d)
    bias = jnp.concatenate((qv_b[0], jnp.zeros((d,), F32), qv_b[1]))
    zero_row = jnp.zeros((d,), F32)
    vec = jnp.stack((wo_b, gain1, shift1, dn_b, gain2, shift2, zero_row, zero_row))
    bias_in = up_b.reshape(nt, fl)

    gw1 = gw2 = None
    outs, gxs = [], []
    vecg = bing = qvg = 0.0
    for s in range(per):
        x, cot = x_all[s], cot_all[s]
        seg = lax.dynamic_index_in_dim(segment_ids, me * per + s, 0, keepdims=False)
        drop = lax.dynamic_slice_in_dim(drop_flags, me * per + s, 1)
        lo, hi = block_range(seg)
        segc = jnp.broadcast_to(seg[:, None], (length, 128))
        segr = seg.reshape(length // BLK, 1, BLK)
        qkv = (dot_nn(x, wqkv) + bias).astype(BF)
        att, lse = attend(qkv, lo, hi, segc, segr)
        layer, g_att, g_hpre, gup, gdn, gwo, vg, bg = middle(
            drop, att, x, cot, wo, up, dn, vec, bias_in
        )
        gq, gk, gv = attend_back(qkv, att, g_att, lse, lo, hi, segc, segr)
        gqkv = jnp.concatenate((gq, gk, gv), axis=1)
        gx = g_hpre + dot_nt(gqkv, wqkv)
        gx = gx + jnp.where(drop[0] == 1, cot.astype(F32), 0.0)
        gwq = dot_tn(x, gqkv)
        g1 = gwq.astype(BF).reshape(d, 3, nt, wl).transpose(2, 0, 1, 3).reshape(nt * d, 3 * wl)
        g2 = jnp.concatenate(
            (gup, gdn, gwo.reshape(d, nt, wl).transpose(1, 0, 2)), axis=2
        ).reshape(nt * d, 2 * fl + wl)
        gw1 = g1 if gw1 is None else gw1 + g1
        gw2 = g2 if gw2 is None else gw2 + g2
        outs.append(layer)
        gxs.append(gx.astype(BF))
        vecg, bing = vecg + vg, bing + bg
        qvg = qvg + jnp.stack(
            (jnp.sum(gq.astype(F32), axis=0), jnp.sum(gv.astype(F32), axis=0))
        )
    layer_out = to_rows(jnp.stack(outs))
    g2 = lax.psum_scatter(gw2, axes, scatter_dimension=0, tiled=True).astype(F32)
    g1 = lax.psum_scatter(gw1, axes, scatter_dimension=0, tiled=True).astype(F32)
    grad_tokens = to_rows(jnp.stack(gxs)).astype(F32)
    vecg, bing, qvg = lax.psum((vecg, bing, qvg), axes)
    return (
        layer_out,
        grad_tokens,
        g1.reshape(rw, 3, wl).transpose(1, 0, 2),
        qvg,
        g2[:, 2 * fl :].T,
        vecg[0],
        vecg[1],
        vecg[2],
        g2[:, :fl],
        bing.reshape(-1),
        g2[:, fl : 2 * fl].T,
        vecg[3],
        vecg[4],
        vecg[5],
    )


def solution(mesh):
    rows = P("dp", "tensor", None)
    return jax.shard_map(
        on_device,
        mesh=mesh,
        in_specs=(
            rows, P("dp", None), P("dp"), P(None, "dp", "tensor"), P(), P("tensor", "dp"), P(), P(), P(),
            P("dp", "tensor"), P(), P("tensor", "dp"), P(), P(), P(), rows,
        ),
        out_specs=(
            rows, rows, P(None, "dp", "tensor"), P(), P("tensor", "dp"), P(), P(), P(),
            P("dp", "tensor"), P(), P("tensor", "dp"), P(), P(), P(),
        ),
        check_vma=False,
    )
```

time: 1590 us -> 653 us (0.41)
  waiting for transfers between devices: 1120 us -> 255 us
  matrix products: 231 us -> 16.9 us
  Pallas kernels: 0 us -> 147 us
  other arithmetic: 110 us -> 36.5 us
  local copies, waits for them, and re-layouts: 31.5 us -> 73.6 us
  starting transfers between devices: 1.34 us -> 38.3 us
    psum x1 -> x0, waiting for transfers between devices: 422 us -> none  [on_device(): summed = lax.psum(partial_value, 'tensor')]
    reduce_scatter x5 -> x1, waiting for transfers between devices: 373 us -> 116 us  [on_device(): lax.psum_scatter(gw2, axes, scatter_dimension=0, tiled=True).astype(F32)]
    all_gather x5 -> x2, waiting for transfers between devices: 324 us -> 81 us  [the longest x1 45.1 us: on_device(): lax.all_gather(jnp.transpose(qkv_w, (1, 0, 2)).reshape(rw, 3 * wl), axes,...]
    dot_general x40 -> x3, matrix products: 231 us -> 16.9 us  [the longest x1 7.19 us: dot_nt(): lax.dot_general(a, b, (((1,), (1,)), ((), ())), preferred_element_type=F32)]
    pallas_call x0 -> x3, Pallas kernels: none -> 147 us  [the longest x1 57.4 us: middle(): pl.pallas_call(functools.partial(middle_kernel, nr), grid=(nr + parts + 1...]
    all_to_all x0 -> x4, waiting for transfers between devices: none -> 57.9 us  [the longest x2 35.7 us: to_seq(): return lax.all_to_all(a, 'tensor', 0, 1, tiled=True)]
    reduce_sum x13 -> x3, other arithmetic: 55.7 us -> 0.79 us  [the longest x1 0.28 us: on_device(): jnp.sum(gv.astype(F32), axis=0)]
    all_to_all x0 -> x4, starting transfers between devices: none -> 38.1 us  [the longest x2 27.4 us: to_rows(): return lax.all_to_all(a, 'tensor', 1, 0, tiled=True)]
  transfers between devices with their start and end apart: 13 -> 8, of which waited for: 9 -> 5; matrix products, arithmetic and copies ran while one was open for 15% -> 16% of each run, Pallas kernels for 0% -> 6%
where the time goes in v1:
time: 653 us; the launch traced here: 647 us
  waiting for transfers between devices  255 us (39%)
  Pallas kernels  147 us (23%)
  local copies, waits for them, and re-layouts  73.6 us (11%)
  blocking collectives  64.1 us (10%)
  starting transfers between devices  38.3 us (6%)
  other arithmetic  36.5 us (6%)
  matrix products  16.9 us (3%)
  between operations  15.4 us (2%)
    reduce_scatter x1, waiting for transfers between devices, on_device(): lax.psum_scatter(gw2, axes, scatter_dimension=0, tiled=True).astype(F32)  116 us
    psum x1, blocking collectives, on_device(): vecg, bing, qvg = lax.psum((vecg, bing, qvg), axes)  64.1 us
    pallas_call x1, Pallas kernels, middle(): pl.pallas_call(functools.partial(middle_kernel, nr), grid=(nr + parts + 1...  57.4 us
    pallas_call x1, Pallas kernels, attend_back(): pl.pallas_call(attend_back_kernel, out_shape=[jax.ShapeDtypeStruct((lengt...  50.6 us
    all_gather x1, waiting for transfers between devices, on_device(): lax.all_gather(jnp.transpose(qkv_w, (1, 0, 2)).reshape(rw, 3 * wl), axes,...  45.1 us
    pallas_call x1, Pallas kernels, attend(): pl.pallas_call(attend_kernel, out_shape=(jax.ShapeDtypeStruct((length, d)...  38.7 us
    all_gather x1, waiting for transfers between devices, on_device(): lax.all_gather(jnp.concatenate((up_w, dn_w.T, wo_w.T), axis=1), axes, axi...  35.9 us
    all_to_all x2, waiting for transfers between devices, to_seq(): return lax.all_to_all(a, 'tensor', 0, 1, tiled=True)  35.7 us
  transfers between devices with their start and end apart: 8, of which 5 were waited for; matrix products, arithmetic and copies ran while one was open for 16% of the time, Pallas kernels for 6%

profile of v1, /device:TPU:0, one launch (start us, length us, event | category | flops | bytes accessed | tf_op | source)
XLA Modules:
  0.0 646.7 jit_solution(17013014708090359455)
XLA Ops:
  11.9 6.3 all-to-all-start
  22.2 35.7 %all-to-all-done = bf16[4,256,768]{2,1,0:T(8,128)(2,1)S(1)} async-done(((bf16[4,256,768]{2,1,0:T(8,128)(2,1)}), bf16[4,256,768]{2,1,0:T(8,128)(2,1)S(1)}, u32[]{:S(2)}, u32[]{:S(2)}) %all-to-all-start) | async-done | bytes 1572896 | tf_op jit(solution)/shard_map/all_to_all | solution.py:399
  57.9 4.3 all-to-all-start.1
  63.3 45.1 %all-gather.3.cloned.1.call-done = bf16[3072,576]{1,0:T(8,128)(2,1)} async-done(((bf16[96,576]{1,0:T(8,128)(2,1)}), bf16[3072,576]{1,0:T(8,128)(2,1)}) %all-gather.3.cloned.1.call-update) | async-done | bytes 3538960 | tf_op jit(solution)/shard_map/all_gather | solution.py:406
  108.4 4.4 copy.83
  112.8 4.3 reshape.96
  119.7 5.5 add_convert_fusion.q_ref.k_ref.v_ref
  126.3 38.7 %attend_forward.1 = (bf16[1024,768]{1,0:T(8,128)(2,1)}, f32[6,2,1024]{2,1,0:T(2,128)}) custom-call(s32[4]{0:T(128)} %get-tuple-element.144.lo_ref, s32[4]{0:T(128)} %get-tuple-element.143.hi_ref, bf16[1024,2304]{1,0:T(8,128)(2,1)} %add_convert_fusion.q_ref.k_ref.v_ref, bf16[1024,2304]{1,0:T(8,128)(2,1)} %add_convert_fusion.q_ref.k_ref.v_ref, ...), custom_call_target="tpu_custom_call" | custom-call | flops 1610612736 | bytes 6291456 | tf_op jit(solution)/shard_map/attend_forward/pallas_call | solution.py:99
  164.9 35.9 %all-gather.5.cloned.1.call-done = bf16[3072,1728]{1,0:T(8,128)(2,1)} async-done(((bf16[96,1728]{1,0:T(8,128)(2,1)}), bf16[3072,1728]{1,0:T(8,128)(2,1)}) %all-gather.5.cloned.1.call-update) | async-done | bytes 10616848 | tf_op jit(solution)/shard_map/all_gather | solution.py:409
  204.5 8.1 %fusion.2 = (bf16[4,768,768]{2,1,0:T(8,128)(2,1)}, bf16[4,768,768]{2,1,0:T(8,128)(2,1)}) fusion(bf16[4,768,1728]{2,1,0:T(8,128)(2,1)} %bitcast.66), kind=kLoop, calls=%fused_computation.39 | loop fusion | bytes 18874368 | tf_op jit(solution)/shard_map/slice | solution.py:414
  212.6 57.4 %middle.1 = (bf16[1024,768]{1,0:T(8,128)(2,1)}, bf16[1024,768]{1,0:T(8,128)(2,1)}, f32[1024,768]{1,0:T(8,128)}, bf16[4,768,768]{2,1,0:T(8,128)(2,1)}, bf16[4,768...) custom-call(s32[1]{0:T(128)} %dynamic_slice.7.drop_ref, ...), custom_call_target="tpu_custom_call" | custom-call | flops 32614907904 | bytes 28311552 | tf_op jit(solution)/shard_map/middle/pallas_call | solution.py:332
  270.0 50.6 %attend_backward.1 = (bf16[1024,768]{1,0:T(8,128)(2,1)}, bf16[1024,768]{1,0:T(8,128)(2,1)}, bf16[1024,768]{1,0:T(8,128)(2,1)}) custom-call(s32[4]{0:T(128)} %get-tuple-element.144.lo_ref, s32[4]{0:T(128)} %get-tuple-element.143.hi_ref, bf16[1024,2304]{1,0:T(8,128)(2,1)} %add_convert_fusion.q_ref.k_ref.v_ref, ...), custom_call_target="tpu_custom_call" | custom-call | flops 4026531840 | bytes 12582912 | tf_op jit(solution)/shard_map/attend_backward/pallas_call | solution.py:193
  323.9 4.2 convolution_convert_fusion
  331.6 3.9 copy.95
  338.0 9.1 %pad_maximum_fusion = bf16[4,768,1728]{2,1,0:T(8,128)(2,1)} fusion(bf16[4,768,192]{2,1,0:T(8,128)(2,1)S(1)} %bitcast.67, bf16[4,768,768]{2,1,0:T(8,128)(2,1)} %get-tuple-element.36, bf16[4,768,768]{2,1,0:T(8,128)(2,1)} %get-tuple-element.35), kind=kLoop, calls=%fused_computation | loop fusion | flops 31850496 | bytes 21233664 | tf_op jit(solution)/shard_map/concatenate | solution.py:442
  351.6 11.6 %reduce.25 = bf16[1024,768]{1,0:T(8,128)(2,1)} reduce(bf16[1024,1,768]{2,1,0:T(2,128)(2,1)S(1)} %bitcast.61, bf16[]{:T(256)} %broadcast.45), dimensions={1}, to_apply=%bitcast.56.reduce_sub_computation | reduce | bytes 3145730
  367.0 23.1 %all-to-all-start.2 = ((bf16[4,2,98304]{2,1,0:T(2,128)(2,1)}), bf16[4,2,98304]{2,1,0:T(2,128)(2,1)}, u32[]{:S(2)}, u32[]{:S(2)}) async-start(bf16[4,2,98304]{2,1,0:T(2,128)(2,1)} %reshape.133), calls=%async_computation.2 | async-start | bytes 3145728 | tf_op jit(solution)/shard_map/all_to_all | solution.py:402
  390.8 7.2 %fusion = bf16[1,1024,768]{2,1,0:T(8,128)(2,1)S(1)} fusion(bf16[1024,768]{1,0:T(8,128)(2,1)} %bitcast.7.cot_ref, pred[]{:T(512)} %bitcast.14, f32[1024,768]{1,0:T(8,128)} %get-tuple-element.29, bf16[1024,2304]{1,0:T(8,128)(2,1)} %copy-done.10, bf16[768,2304]{0,1:T(8,128)(2,1)S(1)} %bitcast.71), kind=kOutput, calls=%fused_computation.7 | convolution fusion | flops 3627810816 | bytes 14548993 | tf_op jit(solution)/shard_map/dot_general | solution.py:23
  400.4 11.6 %reduce.26 = bf16[1024,768]{1,0:T(8,128)(2,1)} reduce(bf16[1024,1,768]{2,1,0:T(2,128)(2,1)S(1)} %bitcast.62, bf16[]{:T(256)} %broadcast.45), dimensions={1}, to_apply=%bitcast.55.reduce_sub_computation | reduce | bytes 3145730
  412.1 3.9 reshape.131
  415.9 22.2 %all-to-all-done.2 = bf16[4,2,98304]{2,1,0:T(2,128)(2,1)} async-done(((bf16[4,2,98304]{2,1,0:T(2,128)(2,1)}), bf16[4,2,98304]{2,1,0:T(2,128)(2,1)}, u32[]{:S(2)}, u32[]{:S(2)}) %all-to-all-start.2) | async-done | bytes 1572896 | tf_op jit(solution)/shard_map/all_to_all | solution.py:402
  438.1 4.3 all-to-all-start.3
  443.1 64.1 %all-reduce = (f32[2,768]{1,0:T(2,128)}, f32[8,768]{1,0:T(8,128)S(1)}, f32[3072]{0:T(1024)}) all-reduce(f32[2,768]{1,0:T(2,128)S(1)} %pad_maximum_fusion.3, f32[8,768]{1,0:T(8,128)S(1)} %copy-done.12, f32[3072]{0:T(1024)S(1)} %reshape.107), channel_id=1, replica_groups=mesh['dp'=8,'tensor'=4] {'tensor','dp'}, use_global_device_ids=true, to_apply=%region_5.6 | all-reduce | flops 10752 | bytes 86016 | tf_op jit(solution)/shard_map/psum | solution.py:457
  519.2 116.4 %reduce-scatter.5.cloned.1.call-done = bf16[96,1728]{1,0:T(8,128)(2,1)} async-done(((bf16[3072,1728]{1,0:T(8,128)(2,1)}), bf16[96,1728]{1,0:T(8,128)(2,1)}) %reduce-scatter.5.cloned.1.call-update) | async-done | bytes 331792 | tf_op jit(solution)/shard_map/reduce_scatter | solution.py:454
  (115 shorter events, 53.5 us)
Async XLA Ops:
  7.2 11.1 %copy-start.22 = (s32[4]{0:T(128)S(1)}, s32[4]{0:T(128)}, u32[]{:S(2)}) copy-start(s32[4]{0:T(128)} %param.18) | copy-start | bytes 52
  7.2 13.6 %copy-start.16 = (f32[768]{0:T(1024)S(1)}, f32[768]{0:T(1024)}, u32[]{:S(2)}) copy-start(f32[768]{0:T(1024)} %param.22) | copy-start | bytes 9220
  7.2 13.6 %copy-start.17 = (f32[768]{0:T(1024)S(1)}, f32[768]{0:T(1024)}, u32[]{:S(2)}) copy-start(f32[768]{0:T(1024)} %param.23) | copy-start | bytes 9220
  7.2 13.6 %copy-start.18 = (f32[768]{0:T(1024)S(1)}, f32[768]{0:T(1024)}, u32[]{:S(2)}) copy-start(f32[768]{0:T(1024)} %param.24) | copy-start | bytes 9220
  7.2 13.6 %copy-start.19 = (f32[768]{0:T(1024)S(1)}, f32[768]{0:T(1024)}, u32[]{:S(2)}) copy-start(f32[768]{0:T(1024)} %param.28) | copy-start | bytes 9220
  7.2 13.6 %copy-start.20 = (f32[768]{0:T(1024)S(1)}, f32[768]{0:T(1024)}, u32[]{:S(2)}) copy-start(f32[768]{0:T(1024)} %param.29) | copy-start | bytes 9220
  7.2 13.6 %copy-start.21 = (f32[768]{0:T(1024)S(1)}, f32[768]{0:T(1024)}, u32[]{:S(2)}) copy-start(f32[768]{0:T(1024)} %param.30) | copy-start | bytes 9220
  7.3 13.6 %copy-start.13 = (f32[3072]{0:T(1024)S(1)}, f32[3072]{0:T(1024)}, u32[]{:S(2)}) copy-start(f32[3072]{0:T(1024)} %param.26) | copy-start | bytes 36868
  7.3 14.9 %copy-start.15 = (f32[2,768]{1,0:T(2,128)S(1)}, f32[2,768]{1,0:T(2,128)}, u32[]{:S(2)}) copy-start(f32[2,768]{1,0:T(2,128)} %param.20) | copy-start | bytes 18436
  7.3 101.1 %all-gather.3.cloned.1.call-start = ((), (), s32[]{:S(2)}) async-start(), calls=%async_computation.6 | async-start | bytes 4055040 | tf_op jit(solution)/shard_map/all_gather | solution.py:406
  9.2 191.6 %all-gather.5.cloned.1.call-start = ((), (), s32[]{:S(2)}) async-start(), calls=%async_computation.7 | async-start | bytes 11354112 | tf_op jit(solution)/shard_map/all_gather | solution.py:409
  11.9 46.0 %all-to-all-start = ((bf16[4,256,768]{2,1,0:T(8,128)(2,1)}), bf16[4,256,768]{2,1,0:T(8,128)(2,1)S(1)}, u32[]{:S(2)}, u32[]{:S(2)}) async-start(bf16[4,256,768]{2,1,0:T(8,128)(2,1)} %param.16), calls=%async_computation | async-start | bytes 3145728 | tf_op jit(solution)/shard_map/all_to_all | solution.py:399
  20.7 104.5 %copy-start.11 = (s32[1,1024]{1,0:T(1,128)}, s32[1,1024]{1,0:T(1,128)S(1)}, u32[]{:S(2)}) copy-start(s32[1,1024]{1,0:T(1,128)S(1)} %get-tuple-element.140) | copy-start | bytes 12292
  57.9 154.6 %all-to-all-start.1 = ((bf16[4,256,768]{2,1,0:T(8,128)(2,1)}), bf16[4,256,768]{2,1,0:T(8,128)(2,1)}, u32[]{:S(2)}, u32[]{:S(2)}) async-start(bf16[4,256,768]{2,1,0:T(8,128)(2,1)} %param.31), calls=%async_computation.1 | async-start | bytes 3145728 | tf_op jit(solution)/shard_map/all_to_all | solution.py:399
  62.3 455.0 %reduce-scatter.7.cloned.1.call-start = ((), (), s32[]{:S(2)}) async-start(), calls=%async_computation.9 | async-start | bytes 4055040
  119.7 5.6 copy-start.3
  335.5 300.1 %reduce-scatter.5.cloned.1.call-start = ((), (), s32[]{:S(2)}) async-start(), calls=%async_computation.8 | async-start | bytes 11354112 | tf_op jit(solution)/shard_map/reduce_scatter | solution.py:454
  363.2 27.6 %copy-start.4 = (bf16[768,3,4,192]{0,3,2,1:T(8,128)(2,1)S(1)}, bf16[768,3,4,192]{0,3,2,1:T(8,128)(2,1)}, u32[]{:S(2)}) copy-start(bf16[768,3,4,192]{0,3,2,1:T(8,128)(2,1)} %copy-done.3) | copy-start | bytes 10616836
  367.0 71.1 %all-to-all-start.2 = ((bf16[4,2,98304]{2,1,0:T(2,128)(2,1)}), bf16[4,2,98304]{2,1,0:T(2,128)(2,1)}, u32[]{:S(2)}, u32[]{:S(2)}) async-start(bf16[4,2,98304]{2,1,0:T(2,128)(2,1)} %reshape.133), calls=%async_computation.2 | async-start | bytes 3145728 | tf_op jit(solution)/shard_map/all_to_all | solution.py:402
  412.1 30.4 %copy-start.2 = (bf16[1024,768]{1,0:T(8,128)(2,1)S(1)}, bf16[1024,768]{1,0:T(8,128)(2,1)}, u32[]{:S(2)}) copy-start(bf16[1024,768]{1,0:T(8,128)(2,1)} %get-tuple-element.34) | copy-start | bytes 4718596
  412.1 30.7 %copy-start = (bf16[1024,768]{1,0:T(8,128)(2,1)S(1)}, bf16[1024,768]{1,0:T(8,128)(2,1)}, u32[]{:S(2)}) copy-start(bf16[1024,768]{1,0:T(8,128)(2,1)} %get-tuple-element.32) | copy-start | bytes 4718596
  415.9 27.1 %copy-start.14 = (f32[4,768]{1,0:T(4,128)S(1)}, f32[4,768]{1,0:T(4,128)}, u32[]{:S(2)}) copy-start(f32[4,768]{1,0:T(4,128)} %get-tuple-element.39) | copy-start | bytes 36868
  415.9 27.1 %copy-start.12 = (f32[8,768]{1,0:T(8,128)S(1)}, f32[8,768]{1,0:T(8,128)}, u32[]{:S(2)}) copy-start(f32[8,768]{1,0:T(8,128)} %get-tuple-element.38) | copy-start | bytes 73732
  438.1 74.2 %all-to-all-start.3 = ((bf16[4,2,98304]{2,1,0:T(2,128)(2,1)}), bf16[4,2,98304]{2,1,0:T(2,128)(2,1)}, u32[]{:S(2)}, u32[]{:S(2)}) async-start(bf16[4,2,98304]{2,1,0:T(2,128)(2,1)} %reshape.131), calls=%async_computation.3 | async-start | bytes 3145728 | tf_op jit(solution)/shard_map/all_to_all | solution.py:402
  (7 other events, 19.2 us)
Sparse Core Ops, SparseCore 0:
  11.6 96.7 all-gather.2
  111.8 88.9 all-gather.4
  335.6 151.6 reduce-scatter.6
  493.2 142.3 reduce-scatter.4

commit v2 on v1

--- a/solution.py
+++ b/solution.py
@@ -319,13 +319,16 @@
         gwo_ref[...] = dot_nn(gbt_s[...], att_s[...]).astype(BF)
 
 
-def middle(drop, att, x, cot, wo, up, dn, vec, bias_in):
+def middle(drop, att, x, cot, wo, w, vec, bias_in):
     length, d = att.shape
-    parts, _, fl = up.shape
+    _, parts, _, fl = w.shape
     nr = length // BLK
     rows = pl.BlockSpec((BLK, d), lambda i: (jnp.minimum(i, nr - 1), 0))
     once = lambda shape: pl.BlockSpec(
         shape, lambda i: (0,) * len(shape), pipeline_mode=pl.Buffered(1)
+    )
+    weight = lambda a: pl.BlockSpec(
+        (None, parts, d, fl), lambda i: (a, 0, 0, 0), pipeline_mode=pl.Buffered(1)
     )
     part = pl.BlockSpec((None, d, fl), lambda i: (jnp.clip(i - nr, 0, parts - 1), 0, 0))
     whole = lambda shape: pl.BlockSpec(shape, lambda i: (0,) * len(shape))
@@ -348,8 +351,8 @@
             rows,
             rows,
             once((d, d)),
-            once((parts, d, fl)),
-            once((parts, d, fl)),
+            weight(1),
+            weight(2),
             once((8, d)),
             once((parts, fl)),
         ],
@@ -370,7 +373,582 @@
             transcendentals=2 * length * parts * fl,
         ),
         name="middle",
-    )(drop, att, x, cot, wo, up, dn, vec, bias_in)
+    )(drop, att, x, cot, wo, w, w, vec, bias_in)
+
+
+def place(dp):
+    yx, core = dp // 2, dp % 2
+    y, x = yx // 2, yx % 2
+    return yx, core, y * 2 + 1 - x, (1 - y) * 2 + x, 3 - yx
+
+
+def remote(src, dst, send, recv, dp, z):
+    return pltpu.make_async_remote_copy(
+        src_ref=src,
+        dst_ref=dst,
+        send_sem=send,
+        recv_sem=recv,
+        device_id=(dp, z),
+        device_id_type=pl.DeviceIdType.MESH,
+    )
+
+
+def greet(dp, z, yx, core, yx_x, yx_y, nz):
+    barrier = pltpu.get_barrier_semaphore()
+    others = [(yx_x * 2 + core, z), (yx_y * 2 + core, z), (yx * 2 + 1 - core, z)]
+    others += [(dp, (z + k) % nz) for k in range(1, nz)]
+    for dev in others:
+        pl.semaphore_signal(
+            barrier, inc=1, device_id=dev, device_id_type=pl.DeviceIdType.MESH
+        )
+    pl.semaphore_wait(barrier, len(others))
+
+
+def inbound_kernel(tok_ref, sh_ref, x_ref, w_ref, send, recv, tsend, trecv, local):
+    na, nz = w_ref.shape[0], w_ref.shape[1]
+    half = w_ref.shape[4] // 2
+    dp, z = lax.axis_index("dp"), lax.axis_index("tensor")
+    yx, core, yx_x, yx_y, yx_d = place(dp)
+    dev_x, dev_y, dev_c = yx_x * 2 + core, yx_y * 2 + core, yx * 2 + 1 - core
+    low, high = pl.ds(0, half), pl.ds(half, half)
+    greet(dp, z, yx, core, yx_x, yx_y, nz)
+
+    def blk(a, t, where):
+        return w_ref.at[a, t, where, core]
+
+    def mine(a, t, own):
+        return sh_ref.at[a] if own else blk(a, t, yx)
+
+    def x_own(a, t, own):
+        return remote(mine(a, t, own), blk(a, t, yx), send.at[a, t, 0], recv.at[a, t, 0], dev_x, z)
+
+    def y_own(a, t, own):
+        return remote(mine(a, t, own), blk(a, t, yx), send.at[a, t, 1], recv.at[a, t, 1], dev_y, z)
+
+    def c_own(a, t, own):
+        return remote(mine(a, t, own), blk(a, t, yx), send.at[a, t, 2], recv.at[a, t, 5], dev_c, z)
+
+    def right(a, t, own):
+        return remote(
+            mine(a, t, own), blk(a, t, yx), send.at[a, t, 8], recv.at[a, t, 4], dp, (z + 1) % nz
+        )
+
+    def left(a, t, own):
+        return remote(
+            mine(a, t, own), blk(a, t, yx), send.at[a, t, 9], recv.at[a, t, 4], dp, (z + nz - 1) % nz
+        )
+
+    def fwd_y(a, t):
+        b = blk(a, t, yx_x).at[low]
+        return remote(b, b, send.at[a, t, 3], recv.at[a, t, 2], dev_y, z)
+
+    def fwd_x(a, t):
+        b = blk(a, t, yx_y).at[high]
+        return remote(b, b, send.at[a, t, 4], recv.at[a, t, 3], dev_x, z)
+
+    def c_fwd(a, t, where, kind):
+        b = blk(a, t, where)
+        return remote(b, b, send.at[a, t, kind], recv.at[a, t, 5], dev_c, z)
+
+    def landed(ref, sem):
+        pltpu.make_async_copy(ref, ref, sem).wait()
+
+    def each(body):
+        def run(a, carry):
+            body(a)
+            return carry
+
+        lax.fori_loop(0, na, run, 0)
+
+    def sides(s, body):
+        if s == 0:
+            body(z, None)
+            return
+
+        @pl.when(z >= s)
+        def _():
+            body(z - s, True)
+
+        @pl.when(z + s < nz)
+        def _():
+            body(z + s, False)
+
+    def stage1(s, a, t, from_left):
+        own = s == 0
+        if own:
+            pltpu.make_async_copy(sh_ref.at[a], blk(a, t, yx), local.at[a]).start()
+        else:
+            landed(blk(a, t, yx), recv.at[a, t, 4])
+        if own or from_left:
+
+            @pl.when(z < nz - 1)
+            def _():
+                right(a, t, own).start()
+
+        if own or not from_left:
+
+            @pl.when(z > 0)
+            def _():
+                left(a, t, own).start()
+
+        x_own(a, t, own).start()
+        y_own(a, t, own).start()
+        c_own(a, t, own).start()
+
+    def stage2(a, t):
+        landed(blk(a, t, yx_x), recv.at[a, t, 0])
+        fwd_y(a, t).start()
+        c_fwd(a, t, yx_x, 5).start()
+        landed(blk(a, t, yx_y), recv.at[a, t, 1])
+        fwd_x(a, t).start()
+        c_fwd(a, t, yx_y, 6).start()
+
+    def stage3(a, t):
+        landed(blk(a, t, yx_d).at[low], recv.at[a, t, 2])
+        landed(blk(a, t, yx_d).at[high], recv.at[a, t, 3])
+        c_fwd(a, t, yx_d, 7).start()
+
+    def tokens(k):
+        to = (z + k) % nz
+        return remote(tok_ref.at[to], x_ref.at[z], tsend.at[k], trecv.at[k], dp, to)
+
+    own_tokens = pltpu.make_async_copy(tok_ref.at[z], x_ref.at[z], tsend.at[0])
+    own_tokens.start()
+    for s in range(nz + 2):
+        if s < nz:
+            each(lambda a: sides(s, lambda t, fl: stage1(s, a, t, fl)))
+        if s == TOKENS_AT:
+            for k in range(1, nz):
+                tokens(k).start()
+        if 1 <= s <= nz:
+            each(lambda a: sides(s - 1, lambda t, fl: stage2(a, t)))
+        if 2 <= s:
+            each(lambda a: sides(s - 2, lambda t, fl: stage3(a, t)))
+
+    def drain(s, a, t, from_left):
+        own = s == 0
+        landed(w_ref.at[a, t, :, 1 - core], recv.at[a, t, 5])
+        if own:
+            pltpu.make_async_copy(sh_ref.at[a], blk(a, t, yx), local.at[a]).wait()
+        if own or from_left:
+
+            @pl.when(z < nz - 1)
+            def _():
+                right(a, t, own).wait_send()
+
+        if own or not from_left:
+
+            @pl.when(z > 0)
+            def _():
+                left(a, t, own).wait_send()
+
+        x_own(a, t, own).wait_send()
+        y_own(a, t, own).wait_send()
+        c_own(a, t, own).wait_send()
+        fwd_y(a, t).wait_send()
+        fwd_x(a, t).wait_send()
+        c_fwd(a, t, yx_x, 5).wait_send()
+        c_fwd(a, t, yx_y, 6).wait_send()
+        c_fwd(a, t, yx_d, 7).wait_send()
+
+    for s in range(nz):
+        each(lambda a: sides(s, lambda t, fl: drain(s, a, t, fl)))
+    own_tokens.wait()
+    for k in range(1, nz):
+        copy = tokens(k)
+        copy.wait_send()
+        landed(x_ref.at[(z + nz - k) % nz], trecv.at[k])
+
+
+TOKENS_AT = 0
+
+
+def inbound(tokens, shards):
+    nz, nd = lax.axis_size("tensor"), lax.axis_size("dp")
+    na, rw, wide = shards.shape
+    if (nz, nd) != (4, 8):
+        x = lax.all_to_all(tokens, "tensor", 0, 0)
+        w = lax.all_gather(shards, ("tensor", "dp"), axis=1, tiled=True)
+        return x.reshape(-1, x.shape[2]), w.reshape(na, nz, nd * rw, wide)
+    x, w = pl.pallas_call(
+        inbound_kernel,
+        out_shape=(
+            jax.ShapeDtypeStruct(tokens.shape, tokens.dtype),
+            jax.ShapeDtypeStruct((na, nz, nd // 2, 2, rw, wide), shards.dtype),
+        ),
+        in_specs=[pl.BlockSpec(memory_space=pl.ANY)] * 2,
+        out_specs=(pl.BlockSpec(memory_space=pl.ANY),) * 2,
+        scratch_shapes=[
+            pltpu.SemaphoreType.DMA((na, nz, 10)),
+            pltpu.SemaphoreType.DMA((na, nz, 6)),
+            pltpu.SemaphoreType.DMA((nz,)),
+            pltpu.SemaphoreType.DMA((nz,)),
+            pltpu.SemaphoreType.DMA((na,)),
+        ],
+        compiler_params=pltpu.CompilerParams(collective_id=0, has_side_effects=True),
+        name="inbound",
+    )(tokens, shards)
+    return x.reshape(-1, x.shape[2]), w.reshape(na, nz, nd * rw, wide)
+
+
+def outbound_kernel(
+    gx_ref, g0_ref, g1_ref, g2_ref, vec_ref, rows_ref, out_ref, vsum_ref,
+    own, rc, rda, rdb, rx, ry, rz, vbuf, send, recv, load, tsend, trecv, vsend, vrecv,
+):
+    na, nz = own.shape[0], own.shape[1]
+    half = own.shape[4] // 2
+    dp, z = lax.axis_index("dp"), lax.axis_index("tensor")
+    yx, core, yx_x, yx_y, yx_d = place(dp)
+    dev_x, dev_y, dev_c = yx_x * 2 + core, yx_y * 2 + core, yx * 2 + 1 - core
+    low, high = pl.ds(0, half), pl.ds(half, half)
+    order = [3 * (1 - z // 2), (2 + 3 * z) % 5, 1 + z % 2, z]
+
+    def loads(a, t):
+        g = (g0_ref, g1_ref, g2_ref)[a]
+        return pltpu.make_async_copy(g.at[t], own.at[a, t], load.at[a, t])
+
+    for t in order:
+        for a in range(na):
+            loads(a, t).start()
+    vsum_ref[...] = vec_ref[...]
+    greet(dp, z, yx, core, yx_x, yx_y, nz)
+
+    def each(body):
+        def run(a, carry):
+            body(a)
+            return carry
+
+        lax.fori_loop(0, na, run, 0)
+
+    def landed(ref, sem):
+        pltpu.make_async_copy(ref, ref, sem).wait()
+
+    def add(dst, src):
+        dst[...] = (dst[...].astype(F32) + src[...].astype(F32)).astype(BF)
+
+    def c_copy(a, t):
+        return remote(
+            own.at[a, t, :, 1 - core], rc.at[a, t], send.at[a, t, 0], recv.at[a, t, 0], dev_c, z
+        )
+
+    def da_copy(a, t):
+        return remote(
+            own.at[a, t, yx_d, core, low], rda.at[a, t], send.at[a, t, 1], recv.at[a, t, 1], dev_x, z
+        )
+
+    def db_copy(a, t):
+        return remote(
+            own.at[a, t, yx_d, core, high], rdb.at[a, t], send.at[a, t, 2], recv.at[a, t, 2], dev_y, z
+        )
+
+    def x_copy(a, t):
+        return remote(
+            own.at[a, t, yx_x, core], rx.at[a, t], send.at[a, t, 3], recv.at[a, t, 3], dev_x, z
+        )
+
+    def y_copy(a, t):
+        return remote(
+            own.at[a, t, yx_y, core], ry.at[a, t], send.at[a, t, 4], recv.at[a, t, 4], dev_y, z
+        )
+
+    def right(a, t):
+        return remote(
+            own.at[a, t, yx, core], rz.at[0, a, t], send.at[a, t, 5], recv.at[a, t, 5], dp, (z + 1) % nz
+        )
+
+    def left(a, t):
+        return remote(
+            own.at[a, t, yx, core], rz.at[1, a, t], send.at[a, t, 6], recv.at[a, t, 6], dp,
+            (z + nz - 1) % nz,
+        )
+
+    def stage1(t):
+        for a in range(na):
+            loads(a, t).wait()
+            c_copy(a, t).start()
+
+    def stage2(a, t):
+        landed(rc.at[a, t], recv.at[a, t, 0])
+        for q in range(4):
+            add(own.at[a, t, q, core], rc.at[a, t, q])
+        da_copy(a, t).start()
+        db_copy(a, t).start()
+
+    def stage3(a, t):
+        landed(rda.at[a, t], recv.at[a, t, 1])
+        add(own.at[a, t, yx_y, core, low], rda.at[a, t])
+        landed(rdb.at[a, t], recv.at[a, t, 2])
+        add(own.at[a, t, yx_x, core, high], rdb.at[a, t])
+        x_copy(a, t).start()
+        y_copy(a, t).start()
+
+    def stage4(a, t):
+        landed(rx.at[a, t], recv.at[a, t, 3])
+        landed(ry.at[a, t], recv.at[a, t, 4])
+        here = own.at[a, t, yx, core]
+        here[...] = (
+            here[...].astype(F32) + rx[a, t].astype(F32) + ry[a, t].astype(F32)
+        ).astype(BF)
+
+    def pass_right(a, t):
+        @pl.when(z > 0)
+        def _():
+            landed(rz.at[0, a, t], recv.at[a, t, 5])
+            add(own.at[a, t, yx, core], rz.at[0, a, t])
+
+        right(a, t).start()
+
+    def pass_left(a, t):
+        @pl.when(z < nz - 1)
+        def _():
+            landed(rz.at[1, a, t], recv.at[a, t, 6])
+            add(own.at[a, t, yx, core], rz.at[1, a, t])
+
+        left(a, t).start()
+
+    def stage5(a, t):
+        @pl.when(t > z)
+        def _():
+            pass_right(a, t)
+
+        @pl.when(t < z)
+        def _():
+            pass_left(a, t)
+
+    def finish(a):
+        out_ref[a] = own[a, z, yx, core].astype(F32)
+
+        @pl.when(z > 0)
+        def _():
+            landed(rz.at[0, a, z], recv.at[a, z, 5])
+            out_ref[a] += rz[0, a, z].astype(F32)
+
+        @pl.when(z < nz - 1)
+        def _():
+            landed(rz.at[1, a, z], recv.at[a, z, 6])
+            out_ref[a] += rz[1, a, z].astype(F32)
+
+    def rows(k):
+        to = (z + k) % nz
+        return remote(gx_ref.at[to], rows_ref.at[z], tsend.at[k], trecv.at[k], dp, to)
+
+    partners = [(dev_c, z), (dev_x, z), (dev_y, z)]
+    partners += [(dp, z + 1 - 2 * (z % 2)), (dp, (z + 2) % nz)]
+
+    def vec_copy(k):
+        return remote(vbuf.at[0, k], vbuf.at[1, k], vsend.at[k], vrecv.at[k], *partners[k])
+
+    def vec_start(k):
+        vbuf[0, k] = vsum_ref[...]
+        vec_copy(k).start()
+
+    def vec_finish(k):
+        landed(vbuf.at[1, k], vrecv.at[k])
+        vsum_ref[...] += vbuf[1, k]
+
+    own_rows = pltpu.make_async_copy(gx_ref.at[z], rows_ref.at[z], tsend.at[0])
+    own_rows.start()
+    for k in range(1, nz):
+        rows(k).start()
+    vec_start(0)
+    for k in range(nz):
+        stage1(order[k])
+    for k in range(nz + 3):
+        if k < nz:
+            each(lambda a: stage2(a, order[k]))
+        if 1 <= k <= nz:
+            each(lambda a: stage3(a, order[k - 1]))
+        if k < len(partners):
+            vec_finish(k)
+            if k + 1 < len(partners):
+                vec_start(k + 1)
+        if 2 <= k <= nz + 1:
+            each(lambda a: stage4(a, order[k - 2]))
+        if 3 <= k <= nz + 1:
+            each(lambda a: stage5(a, order[k - 3]))
+    each(finish)
+
+    def drain(k):
+        t = order[k]
+
+        def body(a):
+            c_copy(a, t).wait_send()
+            da_copy(a, t).wait_send()
+            db_copy(a, t).wait_send()
+            x_copy(a, t).wait_send()
+            y_copy(a, t).wait_send()
+
+            @pl.when(t > z)
+            def _():
+                right(a, t).wait_send()
+
+            @pl.when(t < z)
+            def _():
+                left(a, t).wait_send()
+
+        each(body)
+
+    for k in range(nz):
+        drain(k)
+    for k in range(len(partners)):
+        vec_copy(k).wait_send()
+    own_rows.wait()
+    for k in range(1, nz):
+        rows(k).wait_send()
+        landed(rows_ref.at[(z + nz - k) % nz], trecv.at[k])
+
+
+def outbound(gx, grads, vec):
+    nz, nd = lax.axis_size("tensor"), lax.axis_size("dp")
+    length, d = gx.shape
+    gx = gx.reshape(nz, length // nz, d)
+    rw, wide = d // nd, grads[0].shape[2]
+    if (nz, nd) != (4, 8):
+        axes = ("tensor", "dp")
+        rows = lax.all_to_all(gx, "tensor", 0, 0)
+        parts = [
+            lax.psum_scatter(g.reshape(nz * d, wide), axes, scatter_dimension=0, tiled=True)
+            for g in grads
+        ]
+        return rows, [p.astype(F32) for p in parts], lax.psum(vec, axes)
+    na = len(grads)
+    unit = (nd // 2, 2, rw, wide)
+    any_ = pl.BlockSpec(memory_space=pl.ANY)
+    vmem = pl.BlockSpec(memory_space=pltpu.VMEM)
+    dma = pltpu.SemaphoreType.DMA
+    steps = 5
+    rows, out, vsum = pl.pallas_call(
+        outbound_kernel,
+        out_shape=(
+            jax.ShapeDtypeStruct(gx.shape, gx.dtype),
+            jax.ShapeDtypeStruct((na, rw, wide), F32),
+            jax.ShapeDtypeStruct(vec.shape, F32),
+        ),
+        in_specs=[any_] * 4 + [vmem],
+        out_specs=(any_, vmem, vmem),
+        scratch_shapes=[
+            pltpu.VMEM((na, nz) + unit, BF),
+            pltpu.VMEM((na, nz, nd // 2, rw, wide), BF),
+            pltpu.VMEM((na, nz, rw // 2, wide), BF),
+            pltpu.VMEM((na, nz, rw // 2, wide), BF),
+            pltpu.VMEM((na, nz, rw, wide), BF),
+            pltpu.VMEM((na, nz, rw, wide), BF),
+            pltpu.VMEM((2, na, nz, rw, wide), BF),
+            pltpu.VMEM((2, steps) + vec.shape, F32),
+            dma((na, nz, 7)),
+            dma((na, nz, 7)),
+            dma((na, nz)),
+            dma((nz,)),
+            dma((nz,)),
+            dma((steps,)),
+            dma((steps,)),
+        ],
+        compiler_params=pltpu.CompilerParams(
+            collective_id=1, has_side_effects=True, vmem_limit_bytes=VMEM_LIMIT
+        ),
+        name="outbound",
+    )(gx, *(g.reshape((nz,) + unit) for g in grads), vec)
+    return rows, [out[a] for a in range(na)], vsum
+
+
+def project_kernel(x_ref, mix_ref, bias_ref, qkv_ref, w_ref, wo_ref):
+    nz, d, wide = mix_ref.shape
+    wl = wide // 4
+    for j in range(4):
+        whole = jnp.concatenate(
+            [mix_ref[t, :, j * wl : (j + 1) * wl] for t in range(nz)], axis=1
+        )
+        if j < 3:
+            w_ref[:, j * d : (j + 1) * d] = whole
+        else:
+            wo_ref[...] = whole
+    n = x_ref.shape[0] // BLK
+
+    def body(i, carry):
+        at = pl.ds(pl.multiple_of(i * BLK, BLK), BLK)
+        qkv_ref[at, :] = (dot_nn(x_ref[at, :], w_ref[...]) + bias_ref[...]).astype(BF)
+        return carry
+
+    lax.fori_loop(0, n, body, 0)
+
+
+def project(x, w, bias):
+    length, d = x.shape
+    na, nz, _, wide = w.shape
+    full = lambda shape: pl.BlockSpec(shape, lambda i: (0,) * len(shape))
+    return pl.pallas_call(
+        project_kernel,
+        grid=(1,),
+        out_shape=(
+            jax.ShapeDtypeStruct((length, 3 * d), BF),
+            jax.ShapeDtypeStruct((d, 3 * d), BF),
+            jax.ShapeDtypeStruct((d, d), BF),
+        ),
+        in_specs=[
+            full((length, d)),
+            pl.BlockSpec((None, nz, d, wide), lambda i: (0, 0, 0, 0)),
+            full((1, 3 * d)),
+        ],
+        out_specs=(full((length, 3 * d)), full((d, 3 * d)), full((d, d))),
+        compiler_params=pltpu.CompilerParams(vmem_limit_bytes=VMEM_LIMIT),
+        cost_estimate=pl.CostEstimate(
+            flops=6 * length * d * d, bytes_accessed=10 * length * d + 14 * d * d, transcendentals=0
+        ),
+        name="project",
+    )(x, w, bias)
+
+
+def project_back_kernel(
+    drop_ref, x_ref, cot_ref, ghpre_ref, gq_ref, gk_ref, gv_ref, w_ref, gwo_ref,
+    gx_ref, gmix_ref, sums_ref, xt,
+):
+    nz, d, wide = gmix_ref.shape
+    wl = wide // 4
+    n = x_ref.shape[0] // BLK
+    grads = (gq_ref, gk_ref, gv_ref)
+    dropped = drop_ref[0] == 1
+
+    def body(i, carry):
+        at = pl.ds(pl.multiple_of(i * BLK, BLK), BLK)
+        total = ghpre_ref[at, :] + jnp.where(dropped, cot_ref[at, :].astype(F32), 0.0)
+        for j, g in enumerate(grads):
+            total = total + dot_nt(g[at, :], w_ref[:, j * d : (j + 1) * d])
+        gx_ref[at, :] = total.astype(BF)
+        return carry
+
+    lax.fori_loop(0, n, body, 0)
+    for i in range(n):
+        xt[:, i * BLK : (i + 1) * BLK] = jnp.transpose(x_ref[i * BLK : (i + 1) * BLK, :])
+    sums_ref[...] = jnp.zeros_like(sums_ref)
+    for j, g in enumerate(grads):
+        grad = dot_nn(xt[...], g[...]).astype(BF)
+        for t in range(nz):
+            gmix_ref[t, :, j * wl : (j + 1) * wl] = grad[:, t * wl : (t + 1) * wl]
+        sums_ref[j : j + 1, :] = jnp.sum(g[...].astype(F32), axis=0, keepdims=True)
+    for t in range(nz):
+        gmix_ref[t, :, 3 * wl :] = gwo_ref[:, t * wl : (t + 1) * wl]
+
+
+def project_back(drop, x, cot, g_hpre, gq, gk, gv, wqkv, gwo, nz):
+    length, d = x.shape
+    wide = 4 * d // nz
+    vmem = pl.BlockSpec(memory_space=pltpu.VMEM)
+    return pl.pallas_call(
+        project_back_kernel,
+        out_shape=(
+            jax.ShapeDtypeStruct((length, d), BF),
+            jax.ShapeDtypeStruct((nz, d, wide), BF),
+            jax.ShapeDtypeStruct((8, d), F32),
+        ),
+        in_specs=[pl.BlockSpec(memory_space=pltpu.SMEM)] + [vmem] * 8,
+        out_specs=(vmem,) * 3,
+        scratch_shapes=[pltpu.VMEM((d, length), BF)],
+        compiler_params=pltpu.CompilerParams(vmem_limit_bytes=VMEM_LIMIT),
+        cost_estimate=pl.CostEstimate(
+            flops=12 * length * d * d, bytes_accessed=18 * length * d + 14 * d * d, transcendentals=0
+        ),
+        name="project_back",
+    )(drop, x, cot, g_hpre, gq, gk, gv, wqkv, gwo)
 
 
 def block_range(seg):
@@ -386,90 +964,61 @@
     tokens, segment_ids, drop_flags, qkv_w, qv_b, wo_w, wo_b, gain1, shift1,
     up_w, up_b, dn_w, dn_b, gain2, shift2, cotangent,
 ):
-    axes = ("tensor", "dp")
     me = lax.axis_index("tensor")
     nt = lax.axis_size("tensor")
-    seqs, rows_local, d = tokens.shape
+    d = tokens.shape[2]
     length = segment_ids.shape[1]
     rw, wl = qkv_w.shape[1], qkv_w.shape[2]
     fl = up_w.shape[1]
-    per = seqs // nt
-
-    def to_seq(a):
-        return lax.all_to_all(a, "tensor", 0, 1, tiled=True)
-
-    def to_rows(a):
-        return lax.all_to_all(a, "tensor", 1, 0, tiled=True)
-
-    x_all = to_seq(tokens)
-    cot_all = to_seq(cotangent)
-    w1 = lax.all_gather(
-        jnp.transpose(qkv_w, (1, 0, 2)).reshape(rw, 3 * wl), axes, axis=0, tiled=True
-    )
-    w2 = lax.all_gather(
-        jnp.concatenate((up_w, dn_w.T, wo_w.T), axis=1), axes, axis=0, tiled=True
-    ).reshape(nt, d, 2 * fl + wl)
-    wqkv = w1.reshape(nt, d, 3, wl).transpose(1, 2, 0, 3).reshape(d, 3 * d)
-    up = w2[:, :, :fl]
-    dn = w2[:, :, fl : 2 * fl]
-    wo = w2[:, :, 2 * fl :].transpose(1, 0, 2).reshape(d, d)
+    n = length // BLK
+
+    mix = jnp.concatenate((qkv_w[0], qkv_w[1], qkv_w[2], wo_w.T), axis=1)
+    x, w = inbound(tokens, jnp.stack((mix, up_w, dn_w.T)))
+    cotangent, x = lax.optimization_barrier((cotangent, x))
+    cot = lax.all_to_all(cotangent, "tensor", 0, 0).reshape(length, d)
+
+    seg = lax.dynamic_index_in_dim(segment_ids, me, 0, keepdims=False)
+    drop = lax.dynamic_slice_in_dim(drop_flags, me, 1)
+    lo, hi = block_range(seg)
+    segc = jnp.broadcast_to(seg[:, None], (length, 128))
+    segr = seg.reshape(n, 1, BLK)
     bias = jnp.concatenate((qv_b[0], jnp.zeros((d,), F32), qv_b[1]))
     zero_row = jnp.zeros((d,), F32)
     vec = jnp.stack((wo_b, gain1, shift1, dn_b, gain2, shift2, zero_row, zero_row))
-    bias_in = up_b.reshape(nt, fl)
-
-    gw1 = gw2 = None
-    outs, gxs = [], []
-    vecg = bing = qvg = 0.0
-    for s in range(per):
-        x, cot = x_all[s], cot_all[s]
-        seg = lax.dynamic_index_in_dim(segment_ids, me * per + s, 0, keepdims=False)
-        drop = lax.dynamic_slice_in_dim(drop_flags, me * per + s, 1)
-        lo, hi = block_range(seg)
-        segc = jnp.broadcast_to(seg[:, None], (length, 128))
-        segr = seg.reshape(length // BLK, 1, BLK)
-        qkv = (dot_nn(x, wqkv) + bias).astype(BF)
-        att, lse = attend(qkv, lo, hi, segc, segr)
-        layer, g_att, g_hpre, gup, gdn, gwo, vg, bg = middle(
-            drop, att, x, cot, wo, up, dn, vec, bias_in
-        )
-        gq, gk, gv = attend_back(qkv, att, g_att, lse, lo, hi, segc, segr)
-        gqkv = jnp.concatenate((gq, gk, gv), axis=1)
-        gx = g_hpre + dot_nt(gqkv, wqkv)
-        gx = gx + jnp.where(drop[0] == 1, cot.astype(F32), 0.0)
-        gwq = dot_tn(x, gqkv)
-        g1 = gwq.astype(BF).reshape(d, 3, nt, wl).transpose(2, 0, 1, 3).reshape(nt * d, 3 * wl)
-        g2 = jnp.concatenate(
-            (gup, gdn, gwo.reshape(d, nt, wl).transpose(1, 0, 2)), axis=2
-        ).reshape(nt * d, 2 * fl + wl)
-        gw1 = g1 if gw1 is None else gw1 + g1
-        gw2 = g2 if gw2 is None else gw2 + g2
-        outs.append(layer)
-        gxs.append(gx.astype(BF))
-        vecg, bing = vecg + vg, bing + bg
-        qvg = qvg + jnp.stack(
-            (jnp.sum(gq.astype(F32), axis=0), jnp.sum(gv.astype(F32), axis=0))
-        )
-    layer_out = to_rows(jnp.stack(outs))
-    g2 = lax.psum_scatter(gw2, axes, scatter_dimension=0, tiled=True).astype(F32)
-    g1 = lax.psum_scatter(gw1, axes, scatter_dimension=0, tiled=True).astype(F32)
-    grad_tokens = to_rows(jnp.stack(gxs)).astype(F32)
-    vecg, bing, qvg = lax.psum((vecg, bing, qvg), axes)
+
+    qkv, wqkv, wo = project(x, w, bias[None])
+    att, lse = attend(qkv, lo, hi, segc, segr)
+    layer, g_att, g_hpre, gup, gdn, gwo, vecg, bing = middle(
+        drop, att, x, cot, wo, w, vec, up_b.reshape(nt, fl)
+    )
+    layer_out = lax.all_to_all(layer.reshape(nt, length // nt, d), "tensor", 0, 0)
+    gq, gk, gv = attend_back(qkv, att, g_att, lse, lo, hi, segc, segr)
+    gx, gmix, sums = project_back(drop, x, cot, g_hpre, gq, gk, gv, wqkv, gwo, nt)
+    flat = jnp.concatenate(
+        (vecg[:6].reshape(-1), bing.reshape(-1), sums[0], sums[2])
+    )
+    pad = -flat.shape[0] % (8 * 128)
+    flat_size = flat.shape[0]
+    flat = jnp.concatenate((flat, jnp.zeros((pad,), F32))).reshape(-1, 128)
+    rows, (g_mix, g_up, g_dn), total = outbound(gx, (gmix, gup, gdn), flat)
+    total = total.reshape(-1)[:flat_size]
+    vecs = total[: 6 * d].reshape(6, d)
+    g_bin = total[6 * d : 6 * d + nt * fl]
     return (
         layer_out,
-        grad_tokens,
-        g1.reshape(rw, 3, wl).transpose(1, 0, 2),
-        qvg,
-        g2[:, 2 * fl :].T,
-        vecg[0],
-        vecg[1],
-        vecg[2],
-        g2[:, :fl],
-        bing.reshape(-1),
-        g2[:, fl : 2 * fl].T,
-        vecg[3],
-        vecg[4],
-        vecg[5],
+        rows.astype(F32),
+        jnp.stack([g_mix[:, j * wl : (j + 1) * wl] for j in range(3)]),
+        total[6 * d + nt * fl :].reshape(2, d),
+        g_mix[:, 3 * wl :].T,
+        vecs[0],
+        vecs[1],
+        vecs[2],
+        g_up,
+        g_bin,
+        g_dn.T,
+        vecs[3],
+        vecs[4],
+        vecs[5],
     )
 
 

time: 653 us -> 402 us (0.62)
  waiting for transfers between devices: 255 us -> 0.01 us
  Pallas kernels: 147 us -> 369 us
  blocking collectives: 64.1 us -> 0 us
  local copies, waits for them, and re-layouts: 73.6 us -> 16 us
  other arithmetic: 36.5 us -> 5.95 us
  starting transfers between devices: 38.3 us -> 8.77 us
  matrix products: 16.9 us -> 0 us
  between operations: 15.4 us -> 0.99 us
    pallas_call x0 -> x4, Pallas kernels: none -> 191 us  [the longest x1 83.6 us: inbound(): pl.pallas_call(inbound_kernel, out_shape=(jax.ShapeDtypeStruct(tokens.sha...]
    reduce_scatter x1 -> x0, waiting for transfers between devices: 116 us -> none  [on_device(): lax.psum_scatter(gw2, axes, scatter_dimension=0, tiled=True).astype(F32)]
    all_gather x2 -> x0, waiting for transfers between devices: 81 us -> none  [the longest x1 45.1 us: on_device(): lax.all_gather(jnp.transpose(qkv_w, (1, 0, 2)).reshape(rw, 3 * wl), axes,...]
    psum x1 -> x0, blocking collectives: 64.1 us -> none  [on_device(): vecg, bing, qvg = lax.psum((vecg, bing, qvg), axes)]
    all_to_all x4 -> x2, waiting for transfers between devices: 57.9 us -> 0.01 us  [the longest x1 0.01 us: on_device(): lax.all_to_all(layer.reshape(nt, length // nt, d), 'tensor', 0, 0)]
    all_to_all x4 -> x2, starting transfers between devices: 38.1 us -> 8.77 us  [the longest x1 5.06 us: on_device(): lax.all_to_all(layer.reshape(nt, length // nt, d), 'tensor', 0, 0)]
    unnamed x61 -> x33, local copies, waits for them, and re-layouts: 30.3 us -> 4 us
    unnamed x2 -> x0, other arithmetic: 23.2 us -> none
  transfers between devices with their start and end apart: 8 -> 2, of which waited for: 5 -> 0; matrix products, arithmetic and copies ran while one was open for 16% -> 4% of each run, Pallas kernels for 6% -> 57%
where the time goes in v2:
time: 402 us; the launch traced here: 401 us
  Pallas kernels  369 us (92%)
  local copies, waits for them, and re-layouts  16 us (4%)
  starting transfers between devices  8.77 us (2%)
  other arithmetic  5.95 us (1%)
    pallas_call x1, Pallas kernels, inbound(): pl.pallas_call(inbound_kernel, out_shape=(jax.ShapeDtypeStruct(tokens.sha...  83.6 us
    pallas_call x1, Pallas kernels, outbound(): pl.pallas_call(outbound_kernel, out_shape=(jax.ShapeDtypeStruct(gx.shape,...  79.7 us
    pallas_call x1, Pallas kernels, attend_back(): pl.pallas_call(attend_back_kernel, out_shape=[jax.ShapeDtypeStruct((lengt...  70.6 us
    pallas_call x1, Pallas kernels, middle(): pl.pallas_call(functools.partial(middle_kernel, nr), grid=(nr + parts + 1...  56.8 us
    pallas_call x1, Pallas kernels, attend(): pl.pallas_call(attend_kernel, out_shape=(jax.ShapeDtypeStruct((length, d)...  51 us
    pallas_call x1, Pallas kernels, project_back(): pl.pallas_call(project_back_kernel, out_shape=(jax.ShapeDtypeStruct((leng...  16.8 us
    pallas_call x1, Pallas kernels, project(): pl.pallas_call(project_kernel, grid=(1,), out_shape=(jax.ShapeDtypeStruct...  10.6 us
  transfers between devices with their start and end apart: 2, of which 0 were waited for; matrix products, arithmetic and copies ran while one was open for 4% of the time, Pallas kernels for 57%

profile of v2, /device:TPU:0, one launch (start us, length us, event | category | flops | bytes accessed | tf_op | source)
XLA Modules:
  0.0 400.8 jit_solution(3643899381361818720)
XLA Ops:
  0.6 0.9 copy.36
  1.5 0.9 slice_bitcast_fusion.9
  2.5 1.8 pad_maximum_fusion.sh_ref
  4.3 83.6 %inbound.1 = (bf16[4,256,768]{2,1,0:T(8,128)(2,1)}, bf16[3,4,4,2,96,768]{5,4,3,2,1,0:T(8,128)(2,1)}) custom-call(bf16[4,256,768]{2,1,0:T(8,128)(2,1)} %tok_ref.1, bf16[3,96,768]{2,1,0:T(8,128)(2,1)} %pad_maximum_fusion.sh_ref), custom_call_target="tpu_custom_call" | custom-call | tf_op jit(solution)/shard_map/inbound/pallas_call | solution.py:573
  88.0 3.7 all-to-all-start
  93.0 1.4 fusion
  95.7 0.6 stack.59.vec_ref
  97.3 10.6 %project.1 = (bf16[1024,2304]{1,0:T(8,128)(2,1)}, bf16[768,2304]{1,0:T(8,128)(2,1)}, bf16[768,768]{1,0:T(8,128)(2,1)}) custom-call(bf16[1024,768]{1,0:T(8,128)(2,1)} %bitcast.62, bf16[3,4,768,768]{3,2,1,0:T(8,128)(2,1)} %bitcast.56, f32[1,2304]{1,0:T(1,128)} %broadcast_in_dim.7.bias_ref), custom_call_target="tpu_custom_call" | custom-call | flops 3623878656 | bytes 16121856 | tf_op jit(solution)/shard_map/project/pallas_call | solution.py:879
  107.9 1.0 broadcast_in_dim.16.segc_ref
  108.9 51.0 %attend_forward.1 = (bf16[1024,768]{1,0:T(8,128)(2,1)}, f32[6,2,1024]{2,1,0:T(2,128)}) custom-call(s32[4]{0:T(128)} %get-tuple-element.149.lo_ref, s32[4]{0:T(128)} %get-tuple-element.148.hi_ref, bf16[1024,2304]{1,0:T(8,128)(2,1)} %get-tuple-element.43.q_ref.k_ref.v_ref, bf16[1024,2304]{1,0:T(8,128)(2,1)} %get-tuple-element.43.q_ref.k_ref.v_ref, ...), custom_call_target="tpu_custom_call" | custom-call | flops 1610612736 | bytes 6291456 | tf_op jit(solution)/shard_map/attend_forward/pallas_call | solution.py:99
  160.0 1.1 copy-done
  161.1 56.8 %middle.1 = (bf16[1024,768]{1,0:T(8,128)(2,1)}, bf16[1024,768]{1,0:T(8,128)(2,1)}, f32[1024,768]{1,0:T(8,128)}, bf16[4,768,768]{2,1,0:T(8,128)(2,1)}, bf16[4,768...) custom-call(s32[1]{0:T(128)} %dynamic_slice.7.drop_ref, ...), custom_call_target="tpu_custom_call" | custom-call | flops 32614907904 | bytes 28311552 | tf_op jit(solution)/shard_map/middle/pallas_call | solution.py:335
  217.9 5.1 %all-to-all-start.1 = ((bf16[4,256,768]{2,1,0:T(8,128)(2,1)}), bf16[4,256,768]{2,1,0:T(8,128)(2,1)S(1)}, u32[]{:S(2)}, u32[]{:S(2)}) async-start(bf16[4,256,768]{2,1,0:T(8,128)(2,1)} %bitcast.68), calls=%async_computation.1 | async-start | bytes 3145728 | tf_op jit(solution)/shard_map/all_to_all | solution.py:994
  223.0 70.6 %attend_backward.1 = (bf16[1024,768]{1,0:T(8,128)(2,1)}, bf16[1024,768]{1,0:T(8,128)(2,1)}, bf16[1024,768]{1,0:T(8,128)(2,1)}) custom-call(s32[4]{0:T(128)} %get-tuple-element.149.lo_ref, s32[4]{0:T(128)} %get-tuple-element.148.hi_ref, bf16[1024,2304]{1,0:T(8,128)(2,1)} %get-tuple-element.43.q_ref.k_ref.v_ref, ...), custom_call_target="tpu_custom_call" | custom-call | flops 4026531840 | bytes 12582912 | tf_op jit(solution)/shard_map/attend_backward/pallas_call | solution.py:193
  293.6 16.8 %project_back.1 = (bf16[1024,768]{1,0:T(8,128)(2,1)}, bf16[4,768,768]{2,1,0:T(8,128)(2,1)}, f32[8,768]{1,0:T(8,128)}) custom-call(s32[1]{0:T(128)} %dynamic_slice.7.drop_ref, bf16[1024,768]{1,0:T(8,128)(2,1)} %bitcast.64, bf16[1024,768]{1,0:T(8,128)(2,1)} %bitcast.67, f32[1024,768]{1,0:T(8,128)} %get-tuple-element.48.ghpre_ref, ...), custom_call_target="tpu_custom_call" | custom-call | flops 7247757312 | bytes 22413312 | tf_op jit(solution)/shard_map/project_back/pallas_call | solution.py:936
  310.3 0.8 slice_reduce_fusion.1
  311.2 0.6 maximum_bitcast_fusion.1.vec_ref
  311.8 79.7 %outbound.1 = (bf16[4,256,768]{2,1,0:T(8,128)(2,1)}, f32[3,96,768]{2,1,0:T(8,128)}, f32[72,128]{1,0:T(8,128)}) custom-call(bf16[4,256,768]{2,1,0:T(8,128)(2,1)} %bitcast.65, bf16[4,4,2,96,768]{4,3,2,1,0:T(8,128)(2,1)} %bitcast.61, bf16[4,4,2,96,768]{4,3,2,1,0:T(8,128)(2,1)} %bitcast.59, bf16[4,4,2,96,768]{4,3,2,1,0:T(8,128)(2,1)} %bitcast.60, ...), custom_call_target="tpu_custom_call" | custom-call | tf_op jit(solution)/shard_map/outbound/pallas_call | solution.py:820
  391.5 0.8 slice.107
  392.9 2.0 slice_bitcast_fusion
  395.0 0.7 copy.37
  395.8 1.9 convert_element_type.11
  397.7 0.7 pad_maximum_fusion.1
  399.7 1.1 copy.39
  (56 shorter events, 5.5 us)
Async XLA Ops:
  87.9 3.8 copy-start.8
  87.9 3.8 copy-start.9
  88.0 3.9 copy-start.10
  88.0 3.9 copy-start.11
  88.0 3.9 copy-start.12
  88.0 3.9 copy-start.13
  88.0 3.9 copy-start.14
  88.0 6.4 %copy-start.7 = (f32[2,768]{1,0:T(2,128)S(1)}, f32[2,768]{1,0:T(2,128)}, u32[]{:S(2)}) copy-start(f32[2,768]{1,0:T(2,128)} %param.20) | copy-start | bytes 18436
  88.0 7.1 %copy-start.5 = (f32[3072]{0:T(1024)S(1)}, f32[3072]{0:T(1024)}, u32[]{:S(2)}) copy-start(f32[3072]{0:T(1024)} %param.26) | copy-start | bytes 36868
  88.0 71.9 %all-to-all-start = ((bf16[4,256,768]{2,1,0:T(8,128)(2,1)}), bf16[4,256,768]{2,1,0:T(8,128)(2,1)S(1)}, u32[]{:S(2)}, u32[]{:S(2)}) async-start(bf16[4,256,768]{2,1,0:T(8,128)(2,1)} %param.31), calls=%async_computation | async-start | bytes 3145728 | tf_op jit(solution)/shard_map/all_to_all | solution.py:978
  94.4 13.5 %copy-start.2 = (s32[1,1024]{1,0:T(1,128)}, s32[1,1024]{1,0:T(1,128)S(1)}, u32[]{:S(2)}) copy-start(s32[1,1024]{1,0:T(1,128)S(1)} %get-tuple-element.131) | copy-start | bytes 12292
  160.0 1.1 copy-start
  217.9 5.1 %copy-start.6 = (f32[4,768]{1,0:T(4,128)S(1)}, f32[4,768]{1,0:T(4,128)}, u32[]{:S(2)}) copy-start(f32[4,768]{1,0:T(4,128)} %get-tuple-element.61) | copy-start | bytes 36868
  217.9 5.1 %copy-start.4 = (f32[8,768]{1,0:T(8,128)S(1)}, f32[8,768]{1,0:T(8,128)}, u32[]{:S(2)}) copy-start(f32[8,768]{1,0:T(8,128)} %get-tuple-element.60) | copy-start | bytes 73732
  217.9 181.8 %all-to-all-start.1 = ((bf16[4,256,768]{2,1,0:T(8,128)(2,1)}), bf16[4,256,768]{2,1,0:T(8,128)(2,1)S(1)}, u32[]{:S(2)}, u32[]{:S(2)}) async-start(bf16[4,256,768]{2,1,0:T(8,128)(2,1)} %bitcast.68), calls=%async_computation.1 | async-start | bytes 3145728 | tf_op jit(solution)/shard_map/all_to_all | solution.py:994
  391.5 4.3 %copy-start.1 = (bf16[4,256,768]{2,1,0:T(8,128)(2,1)S(1)}, bf16[4,256,768]{2,1,0:T(8,128)(2,1)}, u32[]{:S(2)}) copy-start(bf16[4,256,768]{2,1,0:T(8,128)(2,1)} %get-tuple-element.63) | copy-start | bytes 4718596
  395.8 2.7 copy-start.3

commit v3 on v1

v3 whole, which is shorter than its diff:
```python
import functools
import jax
import jax.numpy as jnp
from jax import lax
from jax.experimental import pallas as pl
from jax.experimental.pallas import tpu as pltpu
from jax.sharding import PartitionSpec as P

HD = 64
EPS = 1e-05
NEG = -1000000000.0
BF = jnp.bfloat16
F32 = jnp.float32
VMEM_LIMIT = 60 * 1024 * 1024
BLK = 256
LANES = 128


def dot_nn(a, b):
    return jnp.dot(a, b, preferred_element_type=F32)


def dot_nt(a, b):
    return lax.dot_general(a, b, (((1,), (1,)), ((), ())), preferred_element_type=F32)


def dot_tn(a, b):
    return lax.dot_general(a, b, (((0,), (0,)), ((), ())), preferred_element_type=F32)


def doc_lanes(segc_ref, kx_s, qx_s):
    lane = lax.broadcasted_iota(jnp.int32, segc_ref.shape, 1)
    same = (segc_ref[...] == lane).astype(F32)
    kx_s[:, LANES:] = same.astype(BF)
    qx_s[:, LANES:] = ((1.0 - same) * NEG).astype(BF)


def split_heads(pair):
    first = lax.broadcasted_iota(jnp.int32, pair.shape, 1) % (2 * HD) < HD
    zero = jnp.zeros((), pair.dtype)
    return jnp.where(first, pair, zero), jnp.where(first, zero, pair)


def attend_pair(q, k, v, kx_s, qx_s, vt_s):
    kx_s[:, :LANES] = k
    qx_s[:, :LANES] = (q.astype(F32) * 0.125).astype(BF)
    vt = jnp.transpose(v)
    vt_s[0, :HD, :] = vt[:HD, :]
    vt_s[1, :HD, :] = vt[HD:, :]
    kx = kx_s[...]
    ext = qx_s[:, LANES:]
    outs, lses = [], []
    scores = [
        dot_nt(kx, jnp.concatenate((h, ext), axis=1)) for h in split_heads(qx_s[:, :LANES])
    ]
    for h in range(2):
        top = jnp.max(scores[h], axis=0, keepdims=True)
        p = jnp.exp(scores[h] - top).astype(BF)
        o = dot_nn(vt_s[h], p)
        total = o[HD : HD + 1, :]
        outs.append(o[:HD, :] / total)
        lses.append(top + jnp.log(total))
    return jnp.transpose(jnp.concatenate(outs, axis=0)).astype(BF), jnp.concatenate(lses, axis=0)


def attend_pair_back(q_ref, k_ref, v_ref, att_ref, g_ref, lse, kx_s, qx_s, kt_s, delta_s, dk_s, dv_s, put_q):
    length = q_ref.shape[0]
    kx_s[:, :LANES] = k_ref[...]
    qx_s[:, :LANES] = (q_ref[...].astype(F32) * 0.125).astype(BF)
    kt_s[...] = jnp.transpose(k_ref[...])
    sub = lax.broadcasted_iota(jnp.int32, (8, LANES), 0)
    lane = lax.broadcasted_iota(jnp.int32, (8, LANES), 1)
    pick = jnp.where(lane // HD == sub, 1.0, 0.0).astype(F32)
    prod = g_ref[...].astype(F32) * att_ref[...].astype(F32)
    delta_s[...] = lax.dot_general(
        pick, prod, (((1,), (1,)), ((), ())),
        preferred_element_type=F32, precision=lax.Precision.HIGHEST,
    )
    for i in range(length // QB):
        at = slice(i * QB, (i + 1) * QB)
        kx = kx_s[...]
        v = v_ref[...]
        ext = qx_s[at, LANES:]
        qs = split_heads(qx_s[at, :LANES])
        gs = split_heads(g_ref[at, :])
        ps, ds, dq = [], [], []
        for h in range(2):
            s = dot_nt(kx, jnp.concatenate((qs[h], ext), axis=1))
            p = jnp.exp(s - lse[h : h + 1, at])
            dp = dot_nt(v, gs[h])
            d = (p * (dp - delta_s[h : h + 1, at])).astype(BF)
            ps.append(p.astype(BF))
            ds.append(d)
            dq.append(dot_nn(kt_s[h * HD : (h + 1) * HD, :], d))
        dv = dot_nn(jnp.concatenate(ps, axis=1), jnp.concatenate(gs, axis=0))
        dk = dot_nn(jnp.concatenate(ds, axis=1), jnp.concatenate(qs, axis=0))
        dv_s[...] = dv if i == 0 else dv_s[...] + dv
        dk_s[...] = dk if i == 0 else dk_s[...] + dk
        put_q(at, (jnp.transpose(jnp.concatenate(dq, axis=0)) * 0.125).astype(BF))


QB = 512


def gelu_parts(u):
    e = jnp.exp(-0.5 * u * u)
    t = 1.0 / (1.0 + (0.3275911 * 0.7071067811865476) * jnp.abs(u))
    poly = t * (
        0.5 * 0.254829592
        + t * (0.5 * -0.284496736 + t * (0.5 * 1.421413741 + t * (0.5 * -1.453152027 + t * (0.5 * 1.061405429))))
    )
    tail = poly * e
    cdf = jnp.where(u < 0.0, tail, 1.0 - tail)
    return u * cdf, cdf + u * e * 0.3989422804014327


def norm_rows(v):
    mean = jnp.mean(v, axis=-1, keepdims=True)
    c = v - mean
    inv = lax.rsqrt(jnp.mean(c * c, axis=-1, keepdims=True) + EPS)
    return c * inv, inv


def norm_back(g, normed, inv, gain):
    gn = g * gain
    return inv * (
        gn
        - jnp.mean(gn, axis=-1, keepdims=True)
        - normed * jnp.mean(gn * normed, axis=-1, keepdims=True)
    )


def middle_kernel(
    row_steps, drop_ref, att_ref, x_ref, cot_ref, wo_ref, up_ref, dn_ref, vec_ref, bin_ref,
    lo_ref, gatt_ref, ghpre_ref, gup_ref, gdn_ref, gwo_ref, vecg_ref, bing_ref,
    att_s, act_s, gpre_s, slope_s, ht_s, gb2t_s, gbt_s,
):
    step = pl.program_id(0)
    parts = up_ref.shape[0]

    @pl.when(step == 0)
    def _():
        vecg_ref[...] = jnp.zeros_like(vecg_ref)
        bing_ref[...] = jnp.zeros_like(bing_ref)

    @pl.when(step < row_steps)
    def _():
        at = pl.ds(pl.multiple_of(step * BLK, BLK), BLK)
        vec = lambda r: vec_ref[r : r + 1, :]
        dropped = drop_ref[0] == 1
        att = att_ref[...]
        att_s[at, :] = att
        x = x_ref[...].astype(F32)
        branch = dot_nt(att, wo_ref[...]) + vec(0)
        n1, inv1 = norm_rows(x + branch)
        hidden = n1 * vec(1) + vec(2)
        low = hidden.astype(BF)
        ht_s[:, at] = jnp.transpose(low)
        ffn = hidden + vec(3)
        for t in range(parts):
            pre = dot_nn(low, up_ref[t]) + bin_ref[t : t + 1, :]
            act, slope = gelu_parts(pre)
            act = act.astype(BF)
            act_s[t, at, :] = act
            slope_s[t] = slope
            ffn = ffn + dot_nt(act, dn_ref[t])
        n2, inv2 = norm_rows(ffn)
        final = n2 * vec(4) + vec(5)
        lo_ref[...] = jnp.where(dropped, x, final).astype(BF)
        g_final = jnp.where(dropped, 0.0, cot_ref[...].astype(F32))
        g_fpre = norm_back(g_final, n2, inv2, vec(4))
        gb2 = g_fpre.astype(BF)
        gb2t_s[:, at] = jnp.transpose(gb2)
        g_hidden = g_fpre
        for t in range(parts):
            gpre = (dot_nn(gb2, dn_ref[t]) * slope_s[t]).astype(BF)
            gpre_s[t, at, :] = gpre
            bing_ref[t : t + 1, :] += jnp.sum(gpre.astype(F32), axis=0, keepdims=True)
            g_hidden = g_hidden + dot_nt(gpre, up_ref[t])
        g_hpre = norm_back(g_hidden, n1, inv1, vec(1))
        gb = g_hpre.astype(BF)
        gbt_s[:, at] = jnp.transpose(gb)
        gatt_ref[...] = dot_nn(gb, wo_ref[...]).astype(BF)
        ghpre_ref[...] = g_hpre + jnp.where(dropped, cot_ref[...].astype(F32), 0.0)
        for r, v in enumerate(
            (gb.astype(F32), g_hidden * n1, g_hidden, gb2.astype(F32), g_final * n2, g_final)
        ):
            vecg_ref[r : r + 1, :] += jnp.sum(v, axis=0, keepdims=True)

    for t in range(parts):

        @pl.when(step == row_steps + t)
        def _():
            gup_ref[...] = dot_nn(ht_s[...], gpre_s[t]).astype(BF)
            gdn_ref[...] = dot_nn(gb2t_s[...], act_s[t]).astype(BF)

    @pl.when(step == row_steps + parts)
    def _():
        gwo_ref[...] = dot_nn(gbt_s[...], att_s[...]).astype(BF)


def middle(drop, att, x, cot, wo, w, vec, bias_in):
    length, d = att.shape
    _, parts, _, fl = w.shape
    nr = length // BLK
    rows = pl.BlockSpec((BLK, d), lambda i: (jnp.minimum(i, nr - 1), 0))
    once = lambda shape: pl.BlockSpec(
        shape, lambda i: (0,) * len(shape), pipeline_mode=pl.Buffered(1)
    )
    weight = lambda a: pl.BlockSpec(
        (None, parts, d, fl), lambda i: (a, 0, 0, 0), pipeline_mode=pl.Buffered(1)
    )
    part = pl.BlockSpec((None, d, fl), lambda i: (jnp.clip(i - nr, 0, parts - 1), 0, 0))
    whole = lambda shape: pl.BlockSpec(shape, lambda i: (0,) * len(shape))
    return pl.pallas_call(
        functools.partial(middle_kernel, nr),
        grid=(nr + parts + 1,),
        out_shape=(
            jax.ShapeDtypeStruct((length, d), BF),
            jax.ShapeDtypeStruct((length, d), BF),
            jax.ShapeDtypeStruct((length, d), F32),
            jax.ShapeDtypeStruct((parts, d, fl), BF),
            jax.ShapeDtypeStruct((parts, d, fl), BF),
            jax.ShapeDtypeStruct((d, d), BF),
            jax.ShapeDtypeStruct((8, d), F32),
            jax.ShapeDtypeStruct((parts, fl), F32),
        ),
        in_specs=[
            pl.BlockSpec(memory_space=pltpu.SMEM),
            rows,
            rows,
            rows,
            once((d, d)),
            weight(0),
            weight(1),
            once((8, d)),
            once((parts, fl)),
        ],
        out_specs=(rows, rows, rows, part, part, whole((d, d)), whole((8, d)), whole((parts, fl))),
        scratch_shapes=[
            pltpu.VMEM((length, d), BF),
            pltpu.VMEM((parts, length, fl), BF),
            pltpu.VMEM((parts, length, fl), BF),
            pltpu.VMEM((parts, BLK, fl), F32),
            pltpu.VMEM((d, length), BF),
            pltpu.VMEM((d, length), BF),
            pltpu.VMEM((d, length), BF),
        ],
        compiler_params=pltpu.CompilerParams(vmem_limit_bytes=VMEM_LIMIT),
        cost_estimate=pl.CostEstimate(
            flops=6 * length * d * (d + 2 * parts * fl),
            bytes_accessed=4 * length * d * 3 + 8 * parts * d * fl,
            transcendentals=2 * length * parts * fl,
        ),
        name="middle",
    )(drop, att, x, cot, wo, w, w, vec, bias_in)


def place(dp):
    yx, core = dp // 2, dp % 2
    y, x = yx // 2, yx % 2
    return yx, core, y * 2 + 1 - x, (1 - y) * 2 + x, 3 - yx


def remote(src, dst, send, recv, dp, z):
    return pltpu.make_async_remote_copy(
        src_ref=src,
        dst_ref=dst,
        send_sem=send,
        recv_sem=recv,
        device_id=(dp, z),
        device_id_type=pl.DeviceIdType.MESH,
    )


def greet(dp, z, yx, core, yx_x, yx_y, nz):
    barrier = pltpu.get_barrier_semaphore()
    others = [(yx_x * 2 + core, z), (yx_y * 2 + core, z), (yx * 2 + 1 - core, z)]
    others += [(dp, (z + k) % nz) for k in range(1, nz)]
    for dev in others:
        pl.semaphore_signal(
            barrier, inc=1, device_id=dev, device_id_type=pl.DeviceIdType.MESH
        )
    pl.semaphore_wait(barrier, len(others))


def landed(ref, sem):
    pltpu.make_async_copy(ref, ref, sem).wait()


class Here:
    def __init__(self, nz):
        self.nz = nz
        self.dp, self.z = lax.axis_index("dp"), lax.axis_index("tensor")
        self.yx, self.core, self.yx_x, self.yx_y, self.yx_d = place(self.dp)
        self.dev_x = self.yx_x * 2 + self.core
        self.dev_y = self.yx_y * 2 + self.core
        self.dev_c = self.yx * 2 + 1 - self.core

    def greet(self):
        greet(self.dp, self.z, self.yx, self.core, self.yx_x, self.yx_y, self.nz)

    def sides(self, s, body):
        if s == 0:
            body(self.z, None)
            return

        @pl.when(self.z >= s)
        def _():
            body(self.z - s, True)

        @pl.when(self.z + s < self.nz)
        def _():
            body(self.z + s, False)


class Exchange:
    def __init__(self, here, src, dst, send, recv):
        self.here, self.src, self.dst, self.send, self.recv = here, src, dst, send, recv

    def copy(self, k):
        h = self.here
        to = (h.z + k) % h.nz
        return remote(
            self.src.at[to], self.dst.at[h.z], self.send.at[k], self.recv.at[k], h.dp, to
        )

    def own(self):
        z = self.here.z
        return pltpu.make_async_copy(self.src.at[z], self.dst.at[z], self.send.at[0])

    def start(self):
        self.own().start()
        for k in range(1, self.here.nz):
            self.copy(k).start()

    def wait_recv(self):
        h = self.here
        self.own().wait()
        for k in range(1, h.nz):
            landed(self.dst.at[(h.z + h.nz - k) % h.nz], self.recv.at[k])

    def wait_send(self):
        for k in range(1, self.here.nz):
            self.copy(k).wait_send()


class Gather:
    def __init__(self, here, w_ref, sh_ref, first, count, send, recv, local):
        self.here, self.w, self.sh, self.first, self.count = here, w_ref, sh_ref, first, count
        self.send, self.recv, self.local = send, recv, local

    def blk(self, a, t, yx):
        return self.w.at[a, t, yx, self.here.core]

    def copy(self, src, dst, a, t, sender, receiver, dp, z):
        f = self.first + a
        return remote(src, dst, self.send.at[f, t, sender], self.recv.at[f, t, receiver], dp, z)

    def firsts(self, a, t, own):
        h = self.here
        dst = self.blk(a, t, h.yx)
        src = self.sh.at[self.first + a] if own else dst
        return (
            lambda: self.copy(src, dst, a, t, 0, 0, h.dev_x, h.z),
            lambda: self.copy(src, dst, a, t, 1, 1, h.dev_y, h.z),
            lambda: self.copy(src, dst, a, t, 2, 5, h.dev_c, h.z),
            lambda: self.copy(src, dst, a, t, 8, 4, h.dp, (h.z + 1) % h.nz),
            lambda: self.copy(src, dst, a, t, 9, 4, h.dp, (h.z + h.nz - 1) % h.nz),
        )

    def own_copy(self, a, t):
        return pltpu.make_async_copy(
            self.sh.at[self.first + a], self.blk(a, t, self.here.yx), self.local.at[self.first + a]
        )

    def halves(self, a, t):
        h = self.here
        half = self.w.shape[4] // 2
        to_y = self.blk(a, t, h.yx_x).at[pl.ds(0, half)]
        to_x = self.blk(a, t, h.yx_y).at[pl.ds(half, half)]
        return (
            self.copy(to_y, to_y, a, t, 3, 2, h.dev_y, h.z),
            self.copy(to_x, to_x, a, t, 4, 3, h.dev_x, h.z),
        )

    def to_core(self, a, t, yx, kind):
        b = self.blk(a, t, yx)
        return self.copy(b, b, a, t, kind, 5, self.here.dev_c, self.here.z)

    def each(self, s, body):
        def run(a, carry):
            self.here.sides(s, lambda t, from_left: body(a, t, from_left))
            return carry

        lax.fori_loop(0, self.count, run, 0)

    def along(self, own, from_left, right, left):
        h = self.here
        if own or from_left:
            pl.when(h.z < h.nz - 1)(right)
        if own or not from_left:
            pl.when(h.z > 0)(left)

    def stage1(self, s):
        h, own = self.here, s == 0

        def body(a, t, from_left):
            if own:
                self.own_copy(a, t).start()
            else:
                landed(self.blk(a, t, h.yx), self.recv.at[self.first + a, t, 4])
            x, y, c, right, left = self.firsts(a, t, own)
            self.along(own, from_left, lambda: right().start(), lambda: left().start())
            x().start()
            y().start()
            c().start()

        self.each(s, body)

    def stage2(self, s):
        h = self.here

        def body(a, t, from_left):
            f = self.first + a
            to_y, to_x = self.halves(a, t)
            landed(self.blk(a, t, h.yx_x), self.recv.at[f, t, 0])
            to_y.start()
            self.to_core(a, t, h.yx_x, 5).start()
            landed(self.blk(a, t, h.yx_y), self.recv.at[f, t, 1])
            to_x.start()
            self.to_core(a, t, h.yx_y, 6).start()

        self.each(s, body)

    def stage3(self, s):
        h = self.here
        half = self.w.shape[4] // 2

        def body(a, t, from_left):
            f = self.first + a
            b = self.blk(a, t, h.yx_d)
            landed(b.at[pl.ds(0, half)], self.recv.at[f, t, 2])
            landed(b.at[pl.ds(half, half)], self.recv.at[f, t, 3])
            self.to_core(a, t, h.yx_d, 7).start()

        self.each(s, body)

    def drain(self):
        h = self.here
        for s in range(h.nz):
            own = s == 0

            def body(a, t, from_left):
                landed(self.w.at[a, t, :, 1 - h.core], self.recv.at[self.first + a, t, 5])
                if own:
                    self.own_copy(a, t).wait()
                x, y, c, right, left = self.firsts(a, t, own)
                self.along(own, from_left, lambda: right().wait_send(), lambda: left().wait_send())
                for copy in (x(), y(), c(), *self.halves(a, t)):
                    copy.wait_send()
                for yx, kind in ((h.yx_x, 5), (h.yx_y, 6), (h.yx_d, 7)):
                    self.to_core(a, t, yx, kind).wait_send()

            self.each(s, body)


class Scatter:
    def __init__(self, here, own, rc, rda, rdb, rx, ry, rz, first, send, recv):
        self.here, self.own, self.first, self.count = here, own, first, own.shape[0]
        self.rc, self.rda, self.rdb, self.rx, self.ry, self.rz = rc, rda, rdb, rx, ry, rz
        self.send, self.recv = send, recv
        z = here.z
        self.order = [3 * (1 - z // 2), (2 + 3 * z) % 5, 1 + z % 2, z]

    def copies(self, a, t):
        h, own, f = self.here, self.own, self.first + a
        half = own.shape[4] // 2
        d = own.at[a, t, h.yx_d, h.core]
        mine = own.at[a, t, h.yx, h.core]
        sem = lambda k: (self.send.at[f, t, k], self.recv.at[f, t, k])
        return (
            lambda: remote(own.at[a, t, :, 1 - h.core], self.rc.at[a, t], *sem(0), h.dev_c, h.z),
            lambda: remote(d.at[pl.ds(0, half)], self.rda.at[a, t], *sem(1), h.dev_x, h.z),
            lambda: remote(d.at[pl.ds(half, half)], self.rdb.at[a, t], *sem(2), h.dev_y, h.z),
            lambda: remote(own.at[a, t, h.yx_x, h.core], self.rx.at[a, t], *sem(3), h.dev_x, h.z),
            lambda: remote(own.at[a, t, h.yx_y, h.core], self.ry.at[a, t], *sem(4), h.dev_y, h.z),
            lambda: remote(mine, self.rz.at[0, a, t], *sem(5), h.dp, (h.z + 1) % h.nz),
            lambda: remote(mine, self.rz.at[1, a, t], *sem(6), h.dp, (h.z + h.nz - 1) % h.nz),
        )

    def each(self, k, body):
        t = self.order[k]

        def run(a, carry):
            body(a, t, self.copies(a, t))
            return carry

        lax.fori_loop(0, self.count, run, 0)

    def got(self, ref, a, t, kind):
        landed(ref, self.recv.at[self.first + a, t, kind])

    def add(self, dst, src):
        dst[...] = (dst[...].astype(F32) + src[...].astype(F32)).astype(BF)

    def stage1(self, k):
        self.each(k, lambda a, t, copies: copies[0]().start())

    def stage2(self, k):
        h = self.here

        def body(a, t, copies):
            self.got(self.rc.at[a, t], a, t, 0)
            for q in range(4):
                self.add(self.own.at[a, t, q, h.core], self.rc.at[a, t, q])
            copies[1]().start()
            copies[2]().start()

        self.each(k, body)

    def stage3(self, k):
        h = self.here
        half = self.own.shape[4] // 2

        def body(a, t, copies):
            self.got(self.rda.at[a, t], a, t, 1)
            self.add(self.own.at[a, t, h.yx_y, h.core, pl.ds(0, half)], self.rda.at[a, t])
            copies[4]().start()
            self.got(self.rdb.at[a, t], a, t, 2)
            self.add(self.own.at[a, t, h.yx_x, h.core, pl.ds(half, half)], self.rdb.at[a, t])
            copies[3]().start()

        self.each(k, body)

    def stage4(self, k):
        h = self.here

        def body(a, t, copies):
            mine = self.own.at[a, t, h.yx, h.core]
            self.got(self.rx.at[a, t], a, t, 3)
            self.got(self.ry.at[a, t], a, t, 4)
            mine[...] = (
                mine[...].astype(F32) + self.rx[a, t].astype(F32) + self.ry[a, t].astype(F32)
            ).astype(BF)

        self.each(k, body)

    def stage5(self, k):
        h = self.here

        def body(a, t, copies):
            mine = self.own.at[a, t, h.yx, h.core]

            @pl.when(t > h.z)
            def _():
                @pl.when(h.z > 0)
                def _():
                    self.got(self.rz.at[0, a, t], a, t, 5)
                    self.add(mine, self.rz.at[0, a, t])

                copies[5]().start()

            @pl.when(t < h.z)
            def _():
                @pl.when(h.z < h.nz - 1)
                def _():
                    self.got(self.rz.at[1, a, t], a, t, 6)
                    self.add(mine, self.rz.at[1, a, t])

                copies[6]().start()

        self.each(k, body)

    def finish(self, out_ref):
        h = self.here

        def run(a, carry):
            f, z = self.first + a, h.z
            out_ref[f] = self.own[a, z, h.yx, h.core].astype(F32)

            @pl.when(z > 0)
            def _():
                self.got(self.rz.at[0, a, z], a, z, 5)
                out_ref[f] += self.rz[0, a, z].astype(F32)

            @pl.when(z < h.nz - 1)
            def _():
                self.got(self.rz.at[1, a, z], a, z, 6)
                out_ref[f] += self.rz[1, a, z].astype(F32)

            return carry

        lax.fori_loop(0, self.count, run, 0)

    def drain(self):
        h = self.here

        def body(a, t, copies):
            for copy in copies[:5]:
                copy().wait_send()
            pl.when(t > h.z)(lambda: copies[5]().wait_send())
            pl.when(t < h.z)(lambda: copies[6]().wait_send())

        for k in range(h.nz):
            self.each(k, body)


def scatter_scratch(na, nz, nd, rw, wide):
    return [
        pltpu.VMEM((na, nz, nd // 2, 2, rw, wide), BF),
        pltpu.VMEM((na, nz, nd // 2, rw, wide), BF),
        pltpu.VMEM((na, nz, rw // 2, wide), BF),
        pltpu.VMEM((na, nz, rw // 2, wide), BF),
        pltpu.VMEM((na, nz, rw, wide), BF),
        pltpu.VMEM((na, nz, rw, wide), BF),
        pltpu.VMEM((2, na, nz, rw, wide), BF),
    ]


def every_pair(pairs, work, between):
    def step(p, carry):
        work(p)
        for at, steps in enumerate(between):

            @pl.when(p == at)
            def _():
                for run in steps:
                    run()

        return carry

    lax.fori_loop(0, pairs, step, 0)


def columns(p, start=0):
    return pl.ds(pl.multiple_of(start + p * LANES, LANES), LANES)


def assemble(mix, nz, wqkv_ref, wo_ref):
    d = wo_ref.shape[0]
    wl = d // nz
    for j in range(4):
        whole = jnp.concatenate([mix(t)[:, j * wl : (j + 1) * wl] for t in range(nz)], axis=1)
        if j < 3:
            wqkv_ref[:, j * d : (j + 1) * d] = whole
        else:
            wo_ref[...] = whole


def first_kernel(
    comm, tok_ref, cot_ref, sh_ref, bias_ref, segc_ref,
    x_out, cot_out, wud_out, qkv_out, wqkv_out, xt_out, wo_ref, att_ref, lse_ref,
    mix_s, x_s, qkv_s, wqkv_s, xt_s, kx_s, qx_s, vt_s, out_sem, *sems,
):
    nz = mix_s.shape[1]
    length, d = att_ref.shape
    pairs = d // LANES
    blk = length // nz
    if comm:
        send, recv, local, tsend, trecv, csend, crecv = sems
        here = Here(nz)
        here.greet()
        mix = Gather(here, mix_s, sh_ref, 0, 1, send, recv, local)
        rest = Gather(here, wud_out, sh_ref, 1, 2, send, recv, local)
        tokens = Exchange(here, tok_ref, x_s, tsend, trecv)
        cots = Exchange(here, cot_ref, cot_out, csend, crecv)
        mix.stage1(0)
        tokens.start()
        doc_lanes(segc_ref, kx_s, qx_s)
        vt_s[:, HD:, :] = jnp.ones((2, vt_s.shape[1] - HD, length), BF)
        mix.stage1(1)
        mix.stage2(0)
        mix.stage1(2)
        mix.stage2(1)
        mix.stage3(0)
        rest.stage1(0)
        mix.stage1(3)
        mix.stage2(2)
        mix.stage3(1)
        mix.stage2(3)
        mix.stage3(2)
        mix.stage3(3)
        tokens.wait_recv()
        cots.start()
        rest.stage1(1)
        mix.drain()
        between = [
            [lambda: rest.stage2(0), lambda: rest.stage1(2)],
            [lambda: rest.stage3(0), lambda: rest.stage2(1), lambda: rest.stage1(3)],
            [lambda: rest.stage3(1), lambda: rest.stage2(2)],
            [lambda: rest.stage3(2), lambda: rest.stage2(3)],
            [lambda: rest.stage3(3)],
            [],
        ]
    out_x = pltpu.make_async_copy(x_s, x_out, out_sem.at[0])
    out_qkv = pltpu.make_async_copy(qkv_s, qkv_out, out_sem.at[1])
    out_w = pltpu.make_async_copy(wqkv_s, wqkv_out, out_sem.at[2])
    out_xt = pltpu.make_async_copy(xt_s, xt_out, out_sem.at[3])
    out_x.start()
    assemble(lambda t: mix_s[0, t].reshape(d, -1), nz, wqkv_s, wo_ref)
    out_w.start()

    def body(i, carry):
        at = pl.ds(pl.multiple_of(i * blk, blk), blk)
        qkv_s[at, :] = (dot_nn(x_s[i], wqkv_s[...]) + bias_ref[...]).astype(BF)
        return carry

    lax.fori_loop(0, nz, body, 0)
    out_qkv.start()
    for i in range(nz):
        xt_s[:, i * blk : (i + 1) * blk] = jnp.transpose(x_s[i])
    out_xt.start()

    def work(p):
        o, lse = attend_pair(
            qkv_s[:, columns(p)], qkv_s[:, columns(p, d)], qkv_s[:, columns(p, 2 * d)], kx_s, qx_s, vt_s
        )
        att_ref[:, columns(p)] = o
        lse_ref[p] = lse

    every_pair(pairs, work, between)
    rest.drain()
    tokens.wait_send()
    cots.wait_recv()
    cots.wait_send()
    for copy in (out_x, out_qkv, out_w, out_xt):
        copy.wait()


def first(tokens, cot, shards, bias, segc):
    nz, nd = lax.axis_size("tensor"), lax.axis_size("dp")
    na, rw, wide = shards.shape
    _, blk, d = tokens.shape
    length = segc.shape[0]
    pairs = d // LANES
    any_ = pl.BlockSpec(memory_space=pl.ANY)
    vmem = pl.BlockSpec(memory_space=pltpu.VMEM)
    dma = pltpu.SemaphoreType.DMA
    s = jax.ShapeDtypeStruct
    unit = (nz, nd // 2, 2, rw, wide)
    return pl.pallas_call(
        functools.partial(first_kernel, True),
        out_shape=(
            s(tokens.shape, BF),
            s(tokens.shape, BF),
            s((na - 1,) + unit, BF),
            s((length, 3 * d), BF),
            s((d, 3 * d), BF),
            s((d, length), BF),
            s((d, d), BF),
            s((length, d), BF),
            s((pairs, 2, length), F32),
        ),
        in_specs=[any_, any_, any_, vmem, vmem],
        out_specs=(any_,) * 6 + (vmem,) * 3,
        scratch_shapes=[
            pltpu.VMEM((1,) + unit, BF),
            pltpu.VMEM((nz, blk, d), BF),
            pltpu.VMEM((length, 3 * d), BF),
            pltpu.VMEM((d, 3 * d), BF),
            pltpu.VMEM((d, length), BF),
            pltpu.VMEM((length, 2 * LANES), BF),
            pltpu.VMEM((length, 2 * LANES), BF),
            pltpu.VMEM((2, HD + 16, length), BF),
            dma((4,)),
            dma((na, nz, 10)),
            dma((na, nz, 6)),
            dma((na,)),
            dma((nz,)),
            dma((nz,)),
            dma((nz,)),
            dma((nz,)),
        ],
        compiler_params=pltpu.CompilerParams(
            collective_id=0, has_side_effects=True, vmem_limit_bytes=VMEM_LIMIT
        ),
        name="first",
    )(tokens, cot, shards, bias, segc)


def last_kernel(
    layer_ref, gup_ref, gdn_ref, gwo_ref, ghpre_ref, qkv_ref, att_ref, gatt_ref, wqkv_ref, xt_ref,
    lse_ref, segc_ref, vec_ref,
    lrows_ref, grows_ref, out_ref, vsum_ref,
    pair_s, g_s, w_s, xt_s, hpre_s, gwo_s, gx_s, kx_s, qx_s, kt_s, delta_s, dk_s, dv_s, vbuf,
    u0, u1, u2, u3, u4, u5, u6, m0, m1, m2, m3, m4, m5, m6,
    psem, hsem, load, uload, send, recv, lsend, lrecv, xsend, xrecv, vsend, vrecv,
):
    nz = u0.shape[1]
    length, d = g_s.shape[1:]
    pairs = d // LANES
    blk = length // nz
    wl = d // nz
    here = Here(nz)
    z = here.z
    ud = Scatter(here, u0, u1, u2, u3, u4, u5, u6, 1, send, recv)
    mx = Scatter(here, m0, m1, m2, m3, m4, m5, m6, 0, send, recv)
    layer = Exchange(here, layer_ref, lrows_ref, lsend, lrecv)
    rows = Exchange(here, gx_s, grows_ref, xsend, xrecv)

    def pair_loads(p, slot):
        srcs = (
            qkv_ref.at[:, columns(p)], qkv_ref.at[:, columns(p, d)], qkv_ref.at[:, columns(p, 2 * d)],
            att_ref.at[:, columns(p)], gatt_ref.at[:, columns(p)],
        )
        return [
            pltpu.make_async_copy(src, pair_s.at[slot, j], psem.at[slot, j])
            for j, src in enumerate(srcs)
        ]

    def ud_loads(k):
        t = ud.order[k]
        return [
            pltpu.make_async_copy(g.at[t], u0.at[a, t], uload.at[a, t])
            for a, g in enumerate((gup_ref, gdn_ref))
        ]

    later = [
        pltpu.make_async_copy(src, dst, load.at[i])
        for i, (src, dst) in enumerate(((wqkv_ref, w_s), (xt_ref, xt_s), (gwo_ref, gwo_s)))
    ]

    def hpre_load(i, slot):
        return pltpu.make_async_copy(ghpre_ref.at[i], hpre_s.at[slot], hsem.at[slot])

    for copy in pair_loads(0, 0):
        copy.start()
    for k in range(nz):
        for copy in ud_loads(k):
            copy.start()
    here.greet()
    layer.start()
    doc_lanes(segc_ref, kx_s, qx_s)

    def work(p):
        slot = p % 2

        @pl.when(p + 1 < pairs)
        def _():
            for copy in pair_loads(p + 1, 1 - slot):
                copy.start()

        for copy in pair_loads(p, slot):
            copy.wait()
        q, k, v, att, g = [pair_s.at[slot, j] for j in range(5)]

        def put_q(at, value):
            g_s[0, at, columns(p)] = value

        attend_pair_back(q, k, v, att, g, lse_ref[p], kx_s, qx_s, kt_s, delta_s, dk_s, dv_s, put_q)
        g_s[1, :, columns(p)] = dk_s[...].astype(BF)
        g_s[2, :, columns(p)] = dv_s[...].astype(BF)

    def cores():
        for k in range(nz):
            for copy in ud_loads(k):
                copy.wait()
            ud.stage1(k)

    def start_later():
        for copy in later:
            copy.start()

    def run(*names):
        return [lambda name=name, k=k: getattr(ud, name)(k) for name, k in names]

    between = [
        [cores],
        run(("stage2", 0), ("stage2", 1)),
        run(("stage3", 0), ("stage2", 2), ("stage3", 1), ("stage2", 3)),
        run(("stage4", 0), ("stage5", 0), ("stage3", 2)) + [start_later],
        run(("stage3", 3), ("stage4", 1), ("stage5", 1)),
        run(("stage4", 2), ("stage5", 2), ("stage4", 3)),
    ]
    every_pair(pairs, work, between)

    place_of = [(z + k) % nz for k in (1, 2, 3, 0)]
    hpre_load(place_of[0], 0).start()
    for copy in later:
        copy.wait()
    for i, to in enumerate(place_of):
        if i + 1 < nz:
            hpre_load(place_of[i + 1], (i + 1) % 2).start()
        hpre_load(to, i % 2).wait()
        at = pl.ds(pl.multiple_of(to * blk, blk), blk)
        total = hpre_s[i % 2]
        for j in range(3):
            total = total + dot_nt(g_s[j, at, :], w_s[:, j * d : (j + 1) * d])
        gx_s[to] = total.astype(BF)
        if i + 1 < nz:
            rows.copy(i + 1).start()
        else:
            rows.own().start()

    vsum_ref[...] = vec_ref[...]
    xt = xt_s[...]
    for j in range(3):
        grad = dot_nn(xt, g_s[j]).astype(BF)
        for t in range(nz):
            part = grad[:, t * wl : (t + 1) * wl]
            m0[0, t, :, :, :, j * wl : (j + 1) * wl] = part.reshape(m0.shape[2:5] + (wl,))
        if j != 1:
            sums = jnp.sum(g_s[j].astype(F32), axis=0, keepdims=True)
            r = vec_ref.shape[0] - 2 + j // 2
            vsum_ref[r : r + 1, :] = sums
    for t in range(nz):
        part = gwo_s[:, t * wl : (t + 1) * wl]
        m0[0, t, :, :, :, 3 * wl :] = part.reshape(m0.shape[2:5] + (wl,))

    partners = [(here.dev_c, z), (here.dev_x, z), (here.dev_y, z)]
    partners += [(here.dp, z + 1 - 2 * (z % 2)), (here.dp, (z + 2) % nz)]

    def vec_copy(k):
        return remote(vbuf.at[0, k], vbuf.at[1, k], vsend.at[k], vrecv.at[k], *partners[k])

    def vec_start(k):
        vbuf[0, k] = vsum_ref[...]
        vec_copy(k).start()

    def vec_finish(k):
        landed(vbuf.at[1, k], vrecv.at[k])
        vsum_ref[...] += vbuf[1, k]

    for k in range(nz):
        mx.stage1(k)
    vec_start(0)
    for k in range(nz + 3):
        if k < nz:
            mx.stage2(k)
        if 1 <= k <= nz:
            mx.stage3(k - 1)
        if k < len(partners):
            vec_finish(k)
            if k + 1 < len(partners):
                vec_start(k + 1)
        if 2 <= k <= nz + 1:
            mx.stage4(k - 2)
        if 3 <= k <= nz + 1:
            mx.stage5(k - 3)
    ud.finish(out_ref)
    mx.finish(out_ref)
    ud.drain()
    mx.drain()
    for k in range(len(partners)):
        vec_copy(k).wait_send()
    layer.wait_recv()
    layer.wait_send()
    rows.wait_recv()
    rows.wait_send()


def last(layer, gup, gdn, gwo, ghpre, qkv, att, gatt, wqkv, xt, lse, segc, vec):
    nz, nd = lax.axis_size("tensor"), lax.axis_size("dp")
    length, d = att.shape
    rw, wide = d // nd, gup.shape[2]
    blk = length // nz
    unit = (nz, nd // 2, 2, rw, wide)
    any_ = pl.BlockSpec(memory_space=pl.ANY)
    vmem = pl.BlockSpec(memory_space=pltpu.VMEM)
    dma = pltpu.SemaphoreType.DMA
    s = jax.ShapeDtypeStruct
    steps = 5
    return pl.pallas_call(
        last_kernel,
        out_shape=(
            s((nz, blk, d), BF),
            s((nz, blk, d), BF),
            s((3, rw, wide), F32),
            s(vec.shape, F32),
        ),
        in_specs=[any_] * 10 + [vmem] * 3,
        out_specs=(any_, any_, vmem, vmem),
        scratch_shapes=[
            pltpu.VMEM((2, 5, length, LANES), BF),
            pltpu.VMEM((3, length, d), BF),
            pltpu.VMEM((d, 3 * d), BF),
            pltpu.VMEM((d, length), BF),
            pltpu.VMEM((2, blk, d), F32),
            pltpu.VMEM((d, d), BF),
            pltpu.VMEM((nz, blk, d), BF),
            pltpu.VMEM((length, 2 * LANES), BF),
            pltpu.VMEM((length, 2 * LANES), BF),
            pltpu.VMEM((LANES, length), BF),
            pltpu.VMEM((8, length), F32),
            pltpu.VMEM((length, LANES), F32),
            pltpu.VMEM((length, LANES), F32),
            pltpu.VMEM((2, steps) + vec.shape, F32),
        ]
        + scatter_scratch(2, nz, nd, rw, wide)
        + scatter_scratch(1, nz, nd, rw, wide)
        + [
            dma((2, 5)),
            dma((2,)),
            dma((3,)),
            dma((2, nz)),
            dma((3, nz, 7)),
            dma((3, nz, 7)),
            dma((nz,)),
            dma((nz,)),
            dma((nz,)),
            dma((nz,)),
            dma((steps,)),
            dma((steps,)),
        ],
        compiler_params=pltpu.CompilerParams(
            collective_id=1, has_side_effects=True, vmem_limit_bytes=LAST_LIMIT
        ),
        name="last",
    )(
        layer.reshape(nz, blk, d), gup.reshape(unit), gdn.reshape(unit), gwo,
        ghpre.reshape(nz, blk, d), qkv, att, gatt, wqkv, xt, lse, segc, vec,
    )


LAST_LIMIT = 61 * 1024 * 1024


def plain_attend_kernel(q_ref, k_ref, v_ref, segc_ref, o_ref, lse_ref, kx_s, qx_s, vt_s):
    doc_lanes(segc_ref, kx_s, qx_s)
    vt_s[:, HD:, :] = jnp.ones((2, vt_s.shape[1] - HD, vt_s.shape[2]), BF)
    o_ref[...], lse_ref[...] = attend_pair(q_ref[...], k_ref[...], v_ref[...], kx_s, qx_s, vt_s)


def plain_attend_back_kernel(
    q_ref, k_ref, v_ref, att_ref, g_ref, lse_ref, segc_ref, gq_ref, gk_ref, gv_ref,
    kx_s, qx_s, kt_s, delta_s, dk_s, dv_s,
):
    doc_lanes(segc_ref, kx_s, qx_s)

    def put_q(at, value):
        gq_ref[at, :] = value

    attend_pair_back(
        q_ref, k_ref, v_ref, att_ref, g_ref, lse_ref[...], kx_s, qx_s, kt_s, delta_s, dk_s, dv_s, put_q
    )
    gk_ref[...] = dk_s[...].astype(BF)
    gv_ref[...] = dv_s[...].astype(BF)


def plain_specs(length, d):
    col = lambda off: pl.BlockSpec((length, LANES), lambda p: (0, off + p))
    seg = pl.BlockSpec((length, LANES), lambda p: (0, 0))
    lse = pl.BlockSpec((None, 2, length), lambda p: (p, 0, 0))
    wide = pltpu.VMEM((length, 2 * LANES), BF)
    return d // LANES, col, seg, lse, wide


def plain_first(tokens, cot, shards, bias, segc):
    axes = ("tensor", "dp")
    nz = lax.axis_size("tensor")
    length, d = segc.shape[0], tokens.shape[2]
    pairs, col, seg, lse_spec, wide = plain_specs(length, d)
    x = lax.all_to_all(tokens, "tensor", 0, 0)
    cot = lax.all_to_all(cot, "tensor", 0, 0)
    w = lax.all_gather(shards, axes, axis=1, tiled=True).reshape(3, nz, d, shards.shape[2])
    parts = w[0].reshape(nz, d, 4, d // nz).transpose(1, 2, 0, 3).reshape(d, 4 * d)
    wqkv, wo = parts[:, : 3 * d], parts[:, 3 * d :]
    rows = x.reshape(length, d)
    qkv = (dot_nn(rows, wqkv) + bias).astype(BF)
    att, lse = pl.pallas_call(
        plain_attend_kernel,
        grid=(pairs,),
        out_shape=(
            jax.ShapeDtypeStruct((length, d), BF),
            jax.ShapeDtypeStruct((pairs, 2, length), F32),
        ),
        in_specs=[col(0), col(pairs), col(2 * pairs), seg],
        out_specs=(col(0), lse_spec),
        scratch_shapes=[wide, wide, pltpu.VMEM((2, HD + 16, length), BF)],
        compiler_params=pltpu.CompilerParams(vmem_limit_bytes=VMEM_LIMIT),
        name="plain_attend",
    )(qkv, qkv, qkv, segc)
    return x, cot, w[1:], qkv, wqkv, rows.T, wo, att, lse


def plain_last(layer, gup, gdn, gwo, ghpre, qkv, att, gatt, wqkv, xt, lse, segc, vec):
    axes = ("tensor", "dp")
    nz = lax.axis_size("tensor")
    length, d = att.shape
    pairs, col, seg, lse_spec, wide = plain_specs(length, d)
    f32_wide = pltpu.VMEM((length, LANES), F32)
    grads = pl.pallas_call(
        plain_attend_back_kernel,
        grid=(pairs,),
        out_shape=[jax.ShapeDtypeStruct((length, d), BF)] * 3,
        in_specs=[col(0), col(pairs), col(2 * pairs), col(0), col(0), lse_spec, seg],
        out_specs=[col(0)] * 3,
        scratch_shapes=[
            wide, wide, pltpu.VMEM((LANES, length), BF), pltpu.VMEM((8, length), F32), f32_wide, f32_wide,
        ],
        compiler_params=pltpu.CompilerParams(vmem_limit_bytes=VMEM_LIMIT),
        name="plain_attend_back",
    )(qkv, qkv, qkv, att, gatt, lse, segc)
    g = jnp.concatenate(grads, axis=1)
    gx = (ghpre + dot_nt(g, wqkv)).astype(BF)
    gmix = jnp.concatenate((dot_nn(xt, g).astype(BF), gwo), axis=1)
    gmix = gmix.reshape(d, 4, nz, d // nz).transpose(2, 0, 1, 3).reshape(nz, d, -1)
    split = lambda a: a.reshape(nz, length // nz, d)
    parts = [
        lax.psum_scatter(p.reshape(nz * d, -1), axes, scatter_dimension=0, tiled=True)
        for p in (gmix, gup, gdn)
    ]
    sums = [jnp.sum(grads[j].astype(F32), axis=0, keepdims=True) for j in (0, 2)]
    vec = jnp.concatenate((vec[:-2], *sums), axis=0)
    return (
        lax.all_to_all(split(layer), "tensor", 0, 0),
        lax.all_to_all(split(gx), "tensor", 0, 0),
        jnp.stack(parts).astype(F32),
        lax.psum(vec, axes),
    )


def on_device(
    tokens, segment_ids, drop_flags, qkv_w, qv_b, wo_w, wo_b, gain1, shift1,
    up_w, up_b, dn_w, dn_b, gain2, shift2, cotangent,
):
    me = lax.axis_index("tensor")
    nt, nd = lax.axis_size("tensor"), lax.axis_size("dp")
    d = tokens.shape[2]
    length = segment_ids.shape[1]
    wl = qkv_w.shape[2]
    fl = up_w.shape[1]
    begin, end = (first, last) if (nt, nd) == (4, 8) else (plain_first, plain_last)

    mix = jnp.concatenate((qkv_w[0], qkv_w[1], qkv_w[2], wo_w.T), axis=1)
    shards = jnp.stack((mix, up_w, dn_w.T))
    seg = lax.dynamic_index_in_dim(segment_ids, me, 0, keepdims=False)
    drop = lax.dynamic_slice_in_dim(drop_flags, me, 1)
    segc = jnp.broadcast_to(seg[:, None], (length, LANES))
    bias = jnp.concatenate((qv_b[0], jnp.zeros((d,), F32), qv_b[1]))
    zero_row = jnp.zeros((d,), F32)
    vec = jnp.stack((wo_b, gain1, shift1, dn_b, gain2, shift2, zero_row, zero_row))

    x, cot, wud, qkv, wqkv, xt, wo, att, lse = begin(tokens, cotangent, shards, bias[None], segc)
    layer, g_att, g_hpre, gup, gdn, gwo, vecg, bing = middle(
        drop, att, x.reshape(length, d), cot.reshape(length, d), wo, wud.reshape(2, nt, d, fl), vec,
        up_b.reshape(nt, fl),
    )
    flat = jnp.concatenate((vecg[:6], bing.reshape(-1, d), jnp.zeros((6, d), F32)), axis=0)
    layer_out, rows, grads, total = end(
        layer, gup, gdn, gwo, g_hpre, qkv, att, g_att, wqkv, xt, lse, segc, flat
    )
    g_mix, g_up, g_dn = grads[0], grads[1], grads[2]
    n_bin = nt * fl // d
    return (
        layer_out,
        rows.astype(F32),
        jnp.stack([g_mix[:, j * wl : (j + 1) * wl] for j in range(3)]),
        total[-2:],
        g_mix[:, 3 * wl :].T,
        total[0],
        total[1],
        total[2],
        g_up,
        total[6 : 6 + n_bin].reshape(-1),
        g_dn.T,
        total[3],
        total[4],
        total[5],
    )


def solution(mesh):
    rows = P("dp", "tensor", None)
    return jax.shard_map(
        on_device,
        mesh=mesh,
        in_specs=(
            rows, P("dp", None), P("dp"), P(None, "dp", "tensor"), P(), P("tensor", "dp"), P(), P(), P(),
            P("dp", "tensor"), P(), P("tensor", "dp"), P(), P(), P(), rows,
        ),
        out_specs=(
            rows, rows, P(None, "dp", "tensor"), P(), P("tensor", "dp"), P(), P(), P(),
            P("dp", "tensor"), P(), P("tensor", "dp"), P(), P(), P(),
        ),
        check_vma=False,
    )
```

time: 653 us -> 331 us (0.51)
  waiting for transfers between devices: 255 us -> 0 us
  Pallas kernels: 147 us -> 305 us
  blocking collectives: 64.1 us -> 0 us
  local copies, waits for them, and re-layouts: 73.6 us -> 12.1 us
  starting transfers between devices: 38.3 us -> 0 us
  other arithmetic: 36.5 us -> 6.03 us
  matrix products: 16.9 us -> 0 us
  between operations: 15.4 us -> 1.08 us
    pallas_call x2, Pallas kernels: 89.3 us -> 237 us  [the longest x1 125 us: first(): pl.pallas_call(functools.partial(first_kernel, True), out_shape=(s(tokens...]
    reduce_scatter x1 -> x0, waiting for transfers between devices: 116 us -> none  [on_device(): lax.psum_scatter(gw2, axes, scatter_dimension=0, tiled=True).astype(F32)]
    all_gather x2 -> x0, waiting for transfers between devices: 81 us -> none  [the longest x1 45.1 us: on_device(): lax.all_gather(jnp.transpose(qkv_w, (1, 0, 2)).reshape(rw, 3 * wl), axes,...]
    psum x1 -> x0, blocking collectives: 64.1 us -> none  [on_device(): vecg, bing, qvg = lax.psum((vecg, bing, qvg), axes)]
    all_to_all x4 -> x0, waiting for transfers between devices: 57.9 us -> none  [the longest x2 35.7 us: to_seq(): return lax.all_to_all(a, 'tensor', 0, 1, tiled=True)]
    all_to_all x4 -> x0, starting transfers between devices: 38.1 us -> none  [the longest x2 27.4 us: to_rows(): return lax.all_to_all(a, 'tensor', 1, 0, tiled=True)]
    unnamed x61 -> x29, local copies, waits for them, and re-layouts: 30.3 us -> 3.53 us
    unnamed x2 -> x0, other arithmetic: 23.2 us -> none
  transfers between devices with their start and end apart: 8 -> 0, of which waited for: 5 -> 0; matrix products, arithmetic and copies ran while one was open for 16% -> 0% of each run, Pallas kernels for 6% -> 0%
where the time goes in v3:
time: 331 us; the launch traced here: 324 us
  Pallas kernels  305 us (92%)
  local copies, waits for them, and re-layouts  12.1 us (4%)
  other arithmetic  6.03 us (2%)
    pallas_call x1, Pallas kernels, first(): pl.pallas_call(functools.partial(first_kernel, True), out_shape=(s(tokens...  125 us
    pallas_call x1, Pallas kernels, last(): pl.pallas_call(last_kernel, out_shape=(s((nz, blk, d), BF), s((nz, blk, d...  112 us
    pallas_call x1, Pallas kernels, middle(): pl.pallas_call(functools.partial(middle_kernel, nr), grid=(nr + parts + 1...  68.2 us

profile of v3, /device:TPU:0, one launch (start us, length us, event | category | flops | bytes accessed | tf_op | source)
XLA Modules:
  0.0 324.4 jit_solution(9813277105399296065)
XLA Ops:
  0.7 0.7 copy-done
  1.4 1.0 broadcast_in_dim.20.segc_ref
  2.4 0.9 slice_bitcast_fusion.9
  3.3 0.9 copy.30
  4.2 0.1 maximum_bitcast_fusion
  4.3 1.8 pad_maximum_fusion.sh_ref
  6.1 0.6 broadcast_in_dim.18.bias_ref
  6.8 125.2 %first.1 = (bf16[4,256,768]{2,1,0:T(8,128)(2,1)}, bf16[4,256,768]{2,1,0:T(8,128)(2,1)}, bf16[2,4,4,2,96,768]{5,4,3,2,1,0:T(8,128)(2,1)}, bf16[1024,2304]{1,0:T(8...) custom-call(bf16[4,256,768]{2,1,0:T(8,128)(2,1)} %tok_ref.1, ...), custom_call_target="tpu_custom_call" | custom-call | tf_op jit(solution)/shard_map/first/pallas_call | solution.py:742
  132.0 0.6 dynamic_slice.7.drop_ref
  132.7 0.6 stack.59.vec_ref
  133.4 0.6 reshape.60.bin_ref
  134.0 68.2 %middle.1 = (bf16[1024,768]{1,0:T(8,128)(2,1)}, bf16[1024,768]{1,0:T(8,128)(2,1)}, f32[1024,768]{1,0:T(8,128)}, bf16[4,768,768]{2,1,0:T(8,128)(2,1)}, bf16[4,768...) custom-call(s32[1]{0:T(128)} %dynamic_slice.7.drop_ref, ...), custom_call_target="tpu_custom_call" | custom-call | flops 32614907904 | bytes 28311552 | tf_op jit(solution)/shard_map/middle/pallas_call | solution.py:215
  202.2 0.1 pad.5.clone
  202.3 1.4 maximum_maximum_fusion.vec_ref
  203.8 111.8 %last.1 = (bf16[4,256,768]{2,1,0:T(8,128)(2,1)}, bf16[4,256,768]{2,1,0:T(8,128)(2,1)}, f32[3,96,768]{2,1,0:T(8,128)}, f32[16,768]{1,0:T(8,128)}) custom-call(bf16[4,256,768]{2,1,0:T(8,128)(2,1)} %bitcast.41, bf16[4,4,2,96,768]{4,3,2,1,0:T(8,128)(2,1)} %bitcast.38, bf16[4,4,2,96,768]{4,3,2,1,0:T(8,128)(2,1)} %bitcast.39, ...), custom_call_target="tpu_custom_call" | custom-call | tf_op jit(solution)/shard_map/last/pallas_call | solution.py:964
  315.6 2.1 slice_bitcast_fusion
  317.7 0.1 slice_bitcast_fusion.3
  317.8 0.7 pad_maximum_fusion.1
  318.5 1.9 convert_element_type.3
  320.5 0.7 copy.31
  321.2 0.6 slice_reduce_fusion
  321.9 0.6 reshape.65
  322.5 0.6 slice.73
  323.1 1.1 copy.33
  (38 shorter events, 0.1 us)
Async XLA Ops:
  0.6 0.7 copy-start
  0.7 5.4 %copy-start.5 = (f32[2,768]{1,0:T(2,128)S(1)}, f32[2,768]{1,0:T(2,128)}, u32[]{:S(2)}) copy-start(f32[2,768]{1,0:T(2,128)} %param.20) | copy-start | bytes 18436
  6.7 125.3 %copy-start.12 = (s32[4]{0:T(128)S(1)}, s32[4]{0:T(128)}, u32[]{:S(2)}) copy-start(s32[4]{0:T(128)} %param.18) | copy-start | bytes 52
  6.7 125.9 %copy-start.6 = (f32[768]{0:T(1024)S(1)}, f32[768]{0:T(1024)}, u32[]{:S(2)}) copy-start(f32[768]{0:T(1024)} %param.22) | copy-start | bytes 9220
  6.7 125.9 %copy-start.7 = (f32[768]{0:T(1024)S(1)}, f32[768]{0:T(1024)}, u32[]{:S(2)}) copy-start(f32[768]{0:T(1024)} %param.23) | copy-start | bytes 9220
  6.7 125.9 %copy-start.8 = (f32[768]{0:T(1024)S(1)}, f32[768]{0:T(1024)}, u32[]{:S(2)}) copy-start(f32[768]{0:T(1024)} %param.24) | copy-start | bytes 9220
  6.7 125.9 %copy-start.9 = (f32[768]{0:T(1024)S(1)}, f32[768]{0:T(1024)}, u32[]{:S(2)}) copy-start(f32[768]{0:T(1024)} %param.28) | copy-start | bytes 9220
  6.7 126.0 %copy-start.10 = (f32[768]{0:T(1024)S(1)}, f32[768]{0:T(1024)}, u32[]{:S(2)}) copy-start(f32[768]{0:T(1024)} %param.29) | copy-start | bytes 9220
  6.8 126.0 %copy-start.11 = (f32[768]{0:T(1024)S(1)}, f32[768]{0:T(1024)}, u32[]{:S(2)}) copy-start(f32[768]{0:T(1024)} %param.30) | copy-start | bytes 9220
  6.8 126.6 %copy-start.4 = (f32[3072]{0:T(1024)S(1)}, f32[3072]{0:T(1024)}, u32[]{:S(2)}) copy-start(f32[3072]{0:T(1024)} %param.26) | copy-start | bytes 36868
  315.5 3.0 copy-start.2
  318.5 2.7 copy-start.3
  318.5 4.5 %copy-start.1 = (bf16[4,256,768]{2,1,0:T(8,128)(2,1)S(1)}, bf16[4,256,768]{2,1,0:T(8,128)(2,1)}, u32[]{:S(2)}) copy-start(bf16[4,256,768]{2,1,0:T(8,128)(2,1)} %get-tuple-element.102) | copy-start | bytes 4718596

commit v4 on v3

--- a/solution.py
+++ b/solution.py
@@ -28,9 +28,9 @@
     return lax.dot_general(a, b, (((0,), (0,)), ((), ())), preferred_element_type=F32)
 
 
-def doc_lanes(segc_ref, kx_s, qx_s):
-    lane = lax.broadcasted_iota(jnp.int32, segc_ref.shape, 1)
-    same = (segc_ref[...] == lane).astype(F32)
+def doc_lanes(seg, kx_s, qx_s):
+    lane = lax.broadcasted_iota(jnp.int32, seg.shape, 1)
+    same = (seg == lane).astype(F32)
     kx_s[:, LANES:] = same.astype(BF)
     qx_s[:, LANES:] = ((1.0 - same) * NEG).astype(BF)
 
@@ -102,160 +102,6 @@
 QB = 512
 
 
-def gelu_parts(u):
-    e = jnp.exp(-0.5 * u * u)
-    t = 1.0 / (1.0 + (0.3275911 * 0.7071067811865476) * jnp.abs(u))
-    poly = t * (
-        0.5 * 0.254829592
-        + t * (0.5 * -0.284496736 + t * (0.5 * 1.421413741 + t * (0.5 * -1.453152027 + t * (0.5 * 1.061405429))))
-    )
-    tail = poly * e
-    cdf = jnp.where(u < 0.0, tail, 1.0 - tail)
-    return u * cdf, cdf + u * e * 0.3989422804014327
-
-
-def norm_rows(v):
-    mean = jnp.mean(v, axis=-1, keepdims=True)
-    c = v - mean
-    inv = lax.rsqrt(jnp.mean(c * c, axis=-1, keepdims=True) + EPS)
-    return c * inv, inv
-
-
-def norm_back(g, normed, inv, gain):
-    gn = g * gain
-    return inv * (
-        gn
-        - jnp.mean(gn, axis=-1, keepdims=True)
-        - normed * jnp.mean(gn * normed, axis=-1, keepdims=True)
-    )
-
-
-def middle_kernel(
-    row_steps, drop_ref, att_ref, x_ref, cot_ref, wo_ref, up_ref, dn_ref, vec_ref, bin_ref,
-    lo_ref, gatt_ref, ghpre_ref, gup_ref, gdn_ref, gwo_ref, vecg_ref, bing_ref,
-    att_s, act_s, gpre_s, slope_s, ht_s, gb2t_s, gbt_s,
-):
-    step = pl.program_id(0)
-    parts = up_ref.shape[0]
-
-    @pl.when(step == 0)
-    def _():
-        vecg_ref[...] = jnp.zeros_like(vecg_ref)
-        bing_ref[...] = jnp.zeros_like(bing_ref)
-
-    @pl.when(step < row_steps)
-    def _():
-        at = pl.ds(pl.multiple_of(step * BLK, BLK), BLK)
-        vec = lambda r: vec_ref[r : r + 1, :]
-        dropped = drop_ref[0] == 1
-        att = att_ref[...]
-        att_s[at, :] = att
-        x = x_ref[...].astype(F32)
-        branch = dot_nt(att, wo_ref[...]) + vec(0)
-        n1, inv1 = norm_rows(x + branch)
-        hidden = n1 * vec(1) + vec(2)
-        low = hidden.astype(BF)
-        ht_s[:, at] = jnp.transpose(low)
-        ffn = hidden + vec(3)
-        for t in range(parts):
-            pre = dot_nn(low, up_ref[t]) + bin_ref[t : t + 1, :]
-            act, slope = gelu_parts(pre)
-            act = act.astype(BF)
-            act_s[t, at, :] = act
-            slope_s[t] = slope
-            ffn = ffn + dot_nt(act, dn_ref[t])
-        n2, inv2 = norm_rows(ffn)
-        final = n2 * vec(4) + vec(5)
-        lo_ref[...] = jnp.where(dropped, x, final).astype(BF)
-        g_final = jnp.where(dropped, 0.0, cot_ref[...].astype(F32))
-        g_fpre = norm_back(g_final, n2, inv2, vec(4))
-        gb2 = g_fpre.astype(BF)
-        gb2t_s[:, at] = jnp.transpose(gb2)
-        g_hidden = g_fpre
-        for t in range(parts):
-            gpre = (dot_nn(gb2, dn_ref[t]) * slope_s[t]).astype(BF)
-            gpre_s[t, at, :] = gpre
-            bing_ref[t : t + 1, :] += jnp.sum(gpre.astype(F32), axis=0, keepdims=True)
-            g_hidden = g_hidden + dot_nt(gpre, up_ref[t])
-        g_hpre = norm_back(g_hidden, n1, inv1, vec(1))
-        gb = g_hpre.astype(BF)
-        gbt_s[:, at] = jnp.transpose(gb)
-        gatt_ref[...] = dot_nn(gb, wo_ref[...]).astype(BF)
-        ghpre_ref[...] = g_hpre + jnp.where(dropped, cot_ref[...].astype(F32), 0.0)
-        for r, v in enumerate(
-            (gb.astype(F32), g_hidden * n1, g_hidden, gb2.astype(F32), g_final * n2, g_final)
-        ):
-            vecg_ref[r : r + 1, :] += jnp.sum(v, axis=0, keepdims=True)
-
-    for t in range(parts):
-
-        @pl.when(step == row_steps + t)
-        def _():
-            gup_ref[...] = dot_nn(ht_s[...], gpre_s[t]).astype(BF)
-            gdn_ref[...] = dot_nn(gb2t_s[...], act_s[t]).astype(BF)
-
-    @pl.when(step == row_steps + parts)
-    def _():
-        gwo_ref[...] = dot_nn(gbt_s[...], att_s[...]).astype(BF)
-
-
-def middle(drop, att, x, cot, wo, w, vec, bias_in):
-    length, d = att.shape
-    _, parts, _, fl = w.shape
-    nr = length // BLK
-    rows = pl.BlockSpec((BLK, d), lambda i: (jnp.minimum(i, nr - 1), 0))
-    once = lambda shape: pl.BlockSpec(
-        shape, lambda i: (0,) * len(shape), pipeline_mode=pl.Buffered(1)
-    )
-    weight = lambda a: pl.BlockSpec(
-        (None, parts, d, fl), lambda i: (a, 0, 0, 0), pipeline_mode=pl.Buffered(1)
-    )
-    part = pl.BlockSpec((None, d, fl), lambda i: (jnp.clip(i - nr, 0, parts - 1), 0, 0))
-    whole = lambda shape: pl.BlockSpec(shape, lambda i: (0,) * len(shape))
-    return pl.pallas_call(
-        functools.partial(middle_kernel, nr),
-        grid=(nr + parts + 1,),
-        out_shape=(
-            jax.ShapeDtypeStruct((length, d), BF),
-            jax.ShapeDtypeStruct((length, d), BF),
-            jax.ShapeDtypeStruct((length, d), F32),
-            jax.ShapeDtypeStruct((parts, d, fl), BF),
-            jax.ShapeDtypeStruct((parts, d, fl), BF),
-            jax.ShapeDtypeStruct((d, d), BF),
-            jax.ShapeDtypeStruct((8, d), F32),
-            jax.ShapeDtypeStruct((parts, fl), F32),
-        ),
-        in_specs=[
-            pl.BlockSpec(memory_space=pltpu.SMEM),
-            rows,
-            rows,
-            rows,
-            once((d, d)),
-            weight(0),
-            weight(1),
-            once((8, d)),
-            once((parts, fl)),
-        ],
-        out_specs=(rows, rows, rows, part, part, whole((d, d)), whole((8, d)), whole((parts, fl))),
-        scratch_shapes=[
-            pltpu.VMEM((length, d), BF),
-            pltpu.VMEM((parts, length, fl), BF),
-            pltpu.VMEM((parts, length, fl), BF),
-            pltpu.VMEM((parts, BLK, fl), F32),
-            pltpu.VMEM((d, length), BF),
-            pltpu.VMEM((d, length), BF),
-            pltpu.VMEM((d, length), BF),
-        ],
-        compiler_params=pltpu.CompilerParams(vmem_limit_bytes=VMEM_LIMIT),
-        cost_estimate=pl.CostEstimate(
-            flops=6 * length * d * (d + 2 * parts * fl),
-            bytes_accessed=4 * length * d * 3 + 8 * parts * d * fl,
-            transcendentals=2 * length * parts * fl,
-        ),
-        name="middle",
-    )(drop, att, x, cot, wo, w, w, vec, bias_in)
-
-
 def place(dp):
     yx, core = dp // 2, dp % 2
     y, x = yx // 2, yx % 2
@@ -314,13 +160,17 @@
             body(self.z + s, False)
 
 
+def flip(z, i):
+    return (z % 2 + i % 2) % 2 + 2 * ((z // 2 + i // 2) % 2)
+
+
 class Exchange:
-    def __init__(self, here, src, dst, send, recv):
-        self.here, self.src, self.dst, self.send, self.recv = here, src, dst, send, recv
+    def __init__(self, here, src, dst, send, recv, ks=(1, 2, 3)):
+        self.here, self.src, self.dst, self.send, self.recv, self.ks = here, src, dst, send, recv, ks
 
     def copy(self, k):
         h = self.here
-        to = (h.z + k) % h.nz
+        to = flip(h.z, k)
         return remote(
             self.src.at[to], self.dst.at[h.z], self.send.at[k], self.recv.at[k], h.dp, to
         )
@@ -330,18 +180,20 @@
         return pltpu.make_async_copy(self.src.at[z], self.dst.at[z], self.send.at[0])
 
     def start(self):
+        for k in self.ks:
+            self.copy(k).start()
         self.own().start()
-        for k in range(1, self.here.nz):
-            self.copy(k).start()
+
+    def got(self, k):
+        landed(self.dst.at[flip(self.here.z, k)], self.recv.at[k])
 
     def wait_recv(self):
-        h = self.here
         self.own().wait()
-        for k in range(1, h.nz):
-            landed(self.dst.at[(h.z + h.nz - k) % h.nz], self.recv.at[k])
+        for k in self.ks:
+            self.got(k)
 
     def wait_send(self):
-        for k in range(1, self.here.nz):
+        for k in self.ks:
             self.copy(k).wait_send()
 
 
@@ -633,6 +485,214 @@
     lax.fori_loop(0, pairs, step, 0)
 
 
+def gelu_parts(u):
+    cdf = 0.5 + 0.5 * lax.erf(u * 0.7071067811865476)
+    return u * cdf, cdf + u * jnp.exp(-0.5 * u * u) * 0.3989422804014327
+
+
+def norm_rows(v):
+    mean = jnp.mean(v, axis=-1, keepdims=True)
+    c = v - mean
+    inv = lax.rsqrt(jnp.mean(c * c, axis=-1, keepdims=True) + EPS)
+    return c * inv, inv
+
+
+def norm_back(g, normed, inv, gain):
+    gn = g * gain
+    return inv * (
+        gn
+        - jnp.mean(gn, axis=-1, keepdims=True)
+        - normed * jnp.mean(gn * normed, axis=-1, keepdims=True)
+    )
+
+
+def middle_kernel(comm, row_steps, *refs):
+    drop_ref, att_ref, x_ref, cot_ref, crows_ref, wo_ref, up_ref, dn_ref = refs[:8]
+    vecs, bin_ref = refs[8:14], refs[14]
+    lo_ref, gatt_ref, ghpre_ref, gup_ref, gdn_ref, gwo_ref, vecg_ref, bing_ref = refs[15:23]
+    att_s, act_s, gpre_s, slope_s, ht_s, gb2t_s, gbt_s = refs[23:30]
+    step = pl.program_id(0)
+    parts, _, fl = up_ref.shape
+    vec = lambda r: vecs[r][...][None, :]
+    if comm:
+        cot_s, c3_s, l_s, lsend, lrecv, csend, crecv = refs[30:]
+        here = Here(row_steps)
+        z = here.z
+        layer = Exchange(here, l_s, lo_ref, lsend, lrecv)
+        last_cot = lambda: remote(
+            crows_ref.at[flip(z, 3)], c3_s, csend.at[0], crecv.at[0], here.dp, flip(z, 3)
+        )
+
+    @pl.when(step == 0)
+    def _():
+        if comm:
+            barrier = pltpu.get_barrier_semaphore()
+            for k in range(1, row_steps):
+                pl.semaphore_signal(
+                    barrier, inc=1, device_id=(here.dp, flip(z, k)), device_id_type=pl.DeviceIdType.MESH
+                )
+            pl.semaphore_wait(barrier, row_steps - 1)
+            last_cot().start()
+        vecg_ref[...] = jnp.zeros_like(vecg_ref)
+        bing_ref[...] = jnp.zeros_like(bing_ref)
+
+    if comm:
+
+        @pl.when(step < row_steps - 1)
+        def _():
+            cot_s[...] = cot_ref[...]
+
+        @pl.when(step == row_steps - 1)
+        def _():
+            landed(c3_s, crecv.at[0])
+            cot_s[...] = c3_s[...]
+
+    @pl.when(step < row_steps)
+    def _():
+        at = pl.ds(pl.multiple_of(step * BLK, BLK), BLK)
+        dropped = drop_ref[lax.axis_index("tensor")] == 1
+        cot = (cot_s if comm else cot_ref)[...].astype(F32)
+        att = att_ref[...]
+        att_s[at, :] = att
+        x = x_ref[...].astype(F32)
+        branch = dot_nt(att, wo_ref[...]) + vec(0)
+        n1, inv1 = norm_rows(x + branch)
+        hidden = n1 * vec(1) + vec(2)
+        low = hidden.astype(BF)
+        ht_s[:, at] = jnp.transpose(low)
+        ffn = hidden + vec(3)
+        for t in range(parts):
+            pre = dot_nn(low, up_ref[t]) + bin_ref[t * fl : (t + 1) * fl][None, :]
+            act, slope = gelu_parts(pre)
+            act = act.astype(BF)
+            act_s[t, at, :] = act
+            slope_s[t] = slope
+            ffn = ffn + dot_nt(act, dn_ref[t])
+        n2, inv2 = norm_rows(ffn)
+        final = n2 * vec(4) + vec(5)
+        layer_rows = jnp.where(dropped, x, final).astype(BF)
+        if comm:
+            l_s[flip(z, step)] = layer_rows
+        else:
+            lo_ref[...] = layer_rows
+        g_final = jnp.where(dropped, 0.0, cot)
+        g_fpre = norm_back(g_final, n2, inv2, vec(4))
+        gb2 = g_fpre.astype(BF)
+        gb2t_s[:, at] = jnp.transpose(gb2)
+        g_hidden = g_fpre
+        for t in range(parts):
+            gpre = (dot_nn(gb2, dn_ref[t]) * slope_s[t]).astype(BF)
+            gpre_s[t, at, :] = gpre
+            bing_ref[:, t * fl : (t + 1) * fl] += jnp.sum(gpre.astype(F32), axis=0, keepdims=True)
+            g_hidden = g_hidden + dot_nt(gpre, up_ref[t])
+        g_hpre = norm_back(g_hidden, n1, inv1, vec(1))
+        gb = g_hpre.astype(BF)
+        gbt_s[:, at] = jnp.transpose(gb)
+        gatt_ref[...] = dot_nn(gb, wo_ref[...]).astype(BF)
+        ghpre_ref[...] = g_hpre + jnp.where(dropped, cot, 0.0)
+        for r, v in enumerate(
+            (gb.astype(F32), g_hidden * n1, g_hidden, gb2.astype(F32), g_final * n2, g_final)
+        ):
+            vecg_ref[r : r + 1, :] += jnp.sum(v, axis=0, keepdims=True)
+
+    if comm:
+        for k in range(row_steps):
+
+            @pl.when(step == k)
+            def _():
+                if k == 0:
+                    layer.own().start()
+                else:
+                    layer.copy(k).start()
+
+    @pl.when((step >= row_steps) & (step < row_steps + parts))
+    def _():
+        t = step - row_steps
+        gup_ref[...] = dot_nn(ht_s[...], gpre_s[t]).astype(BF)
+        gdn_ref[...] = dot_nn(gb2t_s[...], act_s[t]).astype(BF)
+
+    @pl.when(step == row_steps + parts)
+    def _():
+        gwo_ref[...] = dot_nn(gbt_s[...], att_s[...]).astype(BF)
+        if comm:
+            last_cot().wait_send()
+            layer.wait_recv()
+            layer.wait_send()
+
+
+def middle(comm, drop, att, x, cot, cot_rows, wo, w, vecs, bias_in):
+    length, d = att.shape
+    _, parts, _, fl = w.shape
+    nr = length // BLK
+
+    def place_of(i):
+        return flip(lax.axis_index("tensor"), i) if comm else i
+
+    rows = pl.BlockSpec((BLK, d), lambda i: (place_of(jnp.minimum(i, nr - 1)), 0))
+    cot_spec = pl.BlockSpec((BLK, d), lambda i: (place_of(jnp.minimum(i, nr - 1 - comm)), 0))
+    any_ = pl.BlockSpec(memory_space=pl.ANY)
+    once = lambda shape: pl.BlockSpec(
+        shape, lambda i: (0,) * len(shape), pipeline_mode=pl.Buffered(1)
+    )
+    weight = lambda a: pl.BlockSpec(
+        (None, parts, d, fl), lambda i: (a, 0, 0, 0), pipeline_mode=pl.Buffered(1)
+    )
+    part = pl.BlockSpec((None, d, fl), lambda i: (jnp.clip(i - nr, 0, parts - 1), 0, 0))
+    whole = lambda shape: pl.BlockSpec(shape, lambda i: (0,) * len(shape))
+    dma = pltpu.SemaphoreType.DMA
+    comm_scratch = [
+        pltpu.VMEM((BLK, d), BF),
+        pltpu.VMEM((BLK, d), BF),
+        pltpu.VMEM((nr, BLK, d), BF),
+        dma((nr,)),
+        dma((nr,)),
+        dma((1,)),
+        dma((1,)),
+    ]
+    extra = dict(collective_id=2, has_side_effects=True) if comm else {}
+    return pl.pallas_call(
+        functools.partial(middle_kernel, comm, nr),
+        grid=(nr + parts + 1,),
+        out_shape=(
+            jax.ShapeDtypeStruct((nr, BLK, d) if comm else (length, d), BF),
+            jax.ShapeDtypeStruct((length, d), BF),
+            jax.ShapeDtypeStruct((length, d), F32),
+            jax.ShapeDtypeStruct((parts, d, fl), BF),
+            jax.ShapeDtypeStruct((parts, d, fl), BF),
+            jax.ShapeDtypeStruct((d, d), BF),
+            jax.ShapeDtypeStruct((8, d), F32),
+            jax.ShapeDtypeStruct((1, parts * fl), F32),
+        ),
+        in_specs=[
+            pl.BlockSpec(memory_space=pltpu.SMEM),
+            rows,
+            rows,
+            cot_spec,
+            any_,
+            once((d, d)),
+            weight(0),
+            weight(1),
+            *[once((d,))] * 6,
+            once((parts * fl,)),
+        ],
+        out_specs=(
+            any_ if comm else rows, rows, rows, part, part, whole((d, d)), whole((8, d)), whole((1, parts * fl)),
+        ),
+        scratch_shapes=[
+            pltpu.VMEM((length, d), BF),
+            pltpu.VMEM((parts, length, fl), BF),
+            pltpu.VMEM((parts, length, fl), BF),
+            pltpu.VMEM((parts, BLK, fl), F32),
+            pltpu.VMEM((d, length), BF),
+            pltpu.VMEM((d, length), BF),
+            pltpu.VMEM((d, length), BF),
+            *(comm_scratch if comm else []),
+        ],
+        compiler_params=pltpu.CompilerParams(vmem_limit_bytes=VMEM_LIMIT, **extra),
+        name="middle",
+    )(drop, att, x, cot, cot_rows, wo, w, w, *vecs, bias_in)
+
+
 def columns(p, start=0):
     return pl.ds(pl.multiple_of(start + p * LANES, LANES), LANES)
 
@@ -649,61 +709,73 @@
 
 
 def first_kernel(
-    comm, tok_ref, cot_ref, sh_ref, bias_ref, segc_ref,
-    x_out, cot_out, wud_out, qkv_out, wqkv_out, xt_out, wo_ref, att_ref, lse_ref,
-    mix_s, x_s, qkv_s, wqkv_s, xt_s, kx_s, qx_s, vt_s, out_sem, *sems,
+    tok_ref, cot_ref, qkvw_ref, wow_ref, upw_ref, dnw_ref, bias_ref, seg_ref,
+    x_out, cot_out, wud_out, qkv_out, wqkv_out, xt_out, wo_ref, att_ref, lse_ref, ext_ref,
+    sh_ref, mix_s, x_s, qkv_s, wqkv_s, xt_s, kx_s, qx_s, vt_s,
+    out_sem, send, recv, local, tsend, trecv, csend, crecv,
 ):
     nz = mix_s.shape[1]
     length, d = att_ref.shape
     pairs = d // LANES
     blk = length // nz
-    if comm:
-        send, recv, local, tsend, trecv, csend, crecv = sems
-        here = Here(nz)
-        here.greet()
-        mix = Gather(here, mix_s, sh_ref, 0, 1, send, recv, local)
-        rest = Gather(here, wud_out, sh_ref, 1, 2, send, recv, local)
-        tokens = Exchange(here, tok_ref, x_s, tsend, trecv)
-        cots = Exchange(here, cot_ref, cot_out, csend, crecv)
-        mix.stage1(0)
-        tokens.start()
-        doc_lanes(segc_ref, kx_s, qx_s)
-        vt_s[:, HD:, :] = jnp.ones((2, vt_s.shape[1] - HD, length), BF)
-        mix.stage1(1)
-        mix.stage2(0)
-        mix.stage1(2)
-        mix.stage2(1)
-        mix.stage3(0)
-        rest.stage1(0)
-        mix.stage1(3)
-        mix.stage2(2)
-        mix.stage3(1)
-        mix.stage2(3)
-        mix.stage3(2)
-        mix.stage3(3)
-        tokens.wait_recv()
-        cots.start()
-        rest.stage1(1)
-        mix.drain()
-        between = [
-            [lambda: rest.stage2(0), lambda: rest.stage1(2)],
-            [lambda: rest.stage3(0), lambda: rest.stage2(1), lambda: rest.stage1(3)],
-            [lambda: rest.stage3(1), lambda: rest.stage2(2)],
-            [lambda: rest.stage3(2), lambda: rest.stage2(3)],
-            [lambda: rest.stage3(3)],
-            [],
-        ]
+    here = Here(nz)
+    mix = Gather(here, mix_s, sh_ref, 0, 1, send, recv, local)
+    rest = Gather(here, wud_out, sh_ref, 1, 2, send, recv, local)
+    tokens = Exchange(here, tok_ref, x_s, tsend, trecv)
+    cots = Exchange(here, cot_ref, cot_out, csend, crecv, (1, 2))
+    sh_ref[0] = jnp.concatenate(
+        (qkvw_ref[0], qkvw_ref[1], qkvw_ref[2], wow_ref[...]), axis=1
+    )
+    here.greet()
+    mix.stage1(0)
+    sh_ref[1] = upw_ref[...]
+    sh_ref[2] = dnw_ref[...]
+    seg = jnp.transpose(jnp.broadcast_to(seg_ref[pl.ds(here.z, 1), :], (LANES, length)))
+    doc_lanes(seg, kx_s, qx_s)
+    ext_ref[:, :LANES] = kx_s[:, LANES:]
+    ext_ref[:, LANES:] = qx_s[:, LANES:]
+    vt_s[:, HD:, :] = jnp.ones((2, vt_s.shape[1] - HD, length), BF)
+    rest.stage1(0)
+    mix.stage1(1)
+    mix.stage1(2)
+    rest.stage1(1)
+    mix.stage1(3)
+    tokens.start()
+    mix.stage2(0)
+    mix.stage2(1)
+    mix.stage3(0)
+    mix.stage2(2)
+    mix.stage3(1)
+    mix.stage2(3)
+    mix.stage3(2)
+    mix.stage3(3)
+    rest.stage2(0)
+    rest.stage1(2)
+    mix.drain()
+    assemble(lambda t: mix_s[0, t].reshape(d, -1), nz, wqkv_s, wo_ref)
+    rest.stage2(1)
+    rest.stage3(0)
+    tokens.wait_recv()
+    rest.stage1(3)
+    cots.start()
+    between = [
+        [lambda: rest.stage2(2), lambda: rest.stage3(1)],
+        [lambda: rest.stage2(3), lambda: rest.stage3(2)],
+        [lambda: rest.stage3(3)],
+    ]
     out_x = pltpu.make_async_copy(x_s, x_out, out_sem.at[0])
     out_qkv = pltpu.make_async_copy(qkv_s, qkv_out, out_sem.at[1])
     out_w = pltpu.make_async_copy(wqkv_s, wqkv_out, out_sem.at[2])
     out_xt = pltpu.make_async_copy(xt_s, xt_out, out_sem.at[3])
     out_x.start()
-    assemble(lambda t: mix_s[0, t].reshape(d, -1), nz, wqkv_s, wo_ref)
     out_w.start()
+    bias = jnp.concatenate(
+        (bias_ref[0:1, :], jnp.zeros((1, d), F32), bias_ref[1:2, :]), axis=1
+    )
 
     def body(i, carry):
         at = pl.ds(pl.multiple_of(i * blk, blk), blk)
-        qkv_s[at, :] = (dot_nn(x_s[i], wqkv_s[...]) + bias_ref[...]).astype(BF)
+        qkv_s[at, :] = (dot_nn(x_s[i], wqkv_s[...]) + bias).astype(BF)
         return carry
 
     lax.fori_loop(0, nz, body, 0)
@@ -728,11 +800,11 @@
         copy.wait()
 
 
-def first(tokens, cot, shards, bias, segc):
+def first(tokens, cot, qkv_w, wo_w, up_w, dn_w, qv_b, segment_ids):
     nz, nd = lax.axis_size("tensor"), lax.axis_size("dp")
-    na, rw, wide = shards.shape
+    na, (rw, wide) = 3, up_w.shape
     _, blk, d = tokens.shape
-    length = segc.shape[0]
+    length = segment_ids.shape[1]
     pairs = d // LANES
     any_ = pl.BlockSpec(memory_space=pl.ANY)
     vmem = pl.BlockSpec(memory_space=pltpu.VMEM)
@@ -740,7 +812,7 @@
     s = jax.ShapeDtypeStruct
     unit = (nz, nd // 2, 2, rw, wide)
     return pl.pallas_call(
-        functools.partial(first_kernel, True),
+        first_kernel,
         out_shape=(
             s(tokens.shape, BF),
             s(tokens.shape, BF),
@@ -751,10 +823,12 @@
             s((d, d), BF),
             s((length, d), BF),
             s((pairs, 2, length), F32),
+            s((length, 2 * LANES), BF),
         ),
-        in_specs=[any_, any_, any_, vmem, vmem],
-        out_specs=(any_,) * 6 + (vmem,) * 3,
+        in_specs=[any_, any_] + [vmem] * 6,
+        out_specs=(any_,) * 6 + (vmem,) * 4,
         scratch_shapes=[
+            pltpu.VMEM((na, rw, wide), BF),
             pltpu.VMEM((1,) + unit, BF),
             pltpu.VMEM((nz, blk, d), BF),
             pltpu.VMEM((length, 3 * d), BF),
@@ -776,16 +850,16 @@
             collective_id=0, has_side_effects=True, vmem_limit_bytes=VMEM_LIMIT
         ),
         name="first",
-    )(tokens, cot, shards, bias, segc)
+    )(tokens, cot, qkv_w, wo_w, up_w, dn_w, qv_b, segment_ids)
 
 
 def last_kernel(
-    layer_ref, gup_ref, gdn_ref, gwo_ref, ghpre_ref, qkv_ref, att_ref, gatt_ref, wqkv_ref, xt_ref,
-    lse_ref, segc_ref, vec_ref,
-    lrows_ref, grows_ref, out_ref, vsum_ref,
+    gup_ref, gdn_ref, gwo_ref, ghpre_ref, qkv_ref, att_ref, gatt_ref, wqkv_ref, xt_ref,
+    lse_ref, ext_ref, vecg_ref, bing_ref,
+    grows_ref, out_ref, vsum_ref,
     pair_s, g_s, w_s, xt_s, hpre_s, gwo_s, gx_s, kx_s, qx_s, kt_s, delta_s, dk_s, dv_s, vbuf,
     u0, u1, u2, u3, u4, u5, u6, m0, m1, m2, m3, m4, m5, m6,
-    psem, hsem, load, uload, send, recv, lsend, lrecv, xsend, xrecv, vsend, vrecv,
+    psem, hsem, load, uload, send, recv, xsend, xrecv, vsend, vrecv,
 ):
     nz = u0.shape[1]
     length, d = g_s.shape[1:]
@@ -796,7 +870,6 @@
     z = here.z
     ud = Scatter(here, u0, u1, u2, u3, u4, u5, u6, 1, send, recv)
     mx = Scatter(here, m0, m1, m2, m3, m4, m5, m6, 0, send, recv)
-    layer = Exchange(here, layer_ref, lrows_ref, lsend, lrecv)
     rows = Exchange(here, gx_s, grows_ref, xsend, xrecv)
 
     def pair_loads(p, slot):
@@ -830,8 +903,12 @@
         for copy in ud_loads(k):
             copy.start()
     here.greet()
-    layer.start()
-    doc_lanes(segc_ref, kx_s, qx_s)
+    kx_s[:, LANES:] = ext_ref[:, :LANES]
+    qx_s[:, LANES:] = ext_ref[:, LANES:]
+    for k in range(nz):
+        for copy in ud_loads(k):
+            copy.wait()
+        ud.stage1(k)
 
     def work(p):
         slot = p % 2
@@ -852,12 +929,6 @@
         g_s[1, :, columns(p)] = dk_s[...].astype(BF)
         g_s[2, :, columns(p)] = dv_s[...].astype(BF)
 
-    def cores():
-        for k in range(nz):
-            for copy in ud_loads(k):
-                copy.wait()
-            ud.stage1(k)
-
     def start_later():
         for copy in later:
             copy.start()
@@ -866,16 +937,15 @@
         return [lambda name=name, k=k: getattr(ud, name)(k) for name, k in names]
 
     between = [
-        [cores],
         run(("stage2", 0), ("stage2", 1)),
-        run(("stage3", 0), ("stage2", 2), ("stage3", 1), ("stage2", 3)),
-        run(("stage4", 0), ("stage5", 0), ("stage3", 2)) + [start_later],
+        run(("stage2", 2), ("stage3", 0), ("stage2", 3)),
+        run(("stage3", 1),) + [start_later],
+        run(("stage4", 0), ("stage5", 0), ("stage3", 2)),
         run(("stage3", 3), ("stage4", 1), ("stage5", 1)),
-        run(("stage4", 2), ("stage5", 2), ("stage4", 3)),
     ]
     every_pair(pairs, work, between)
 
-    place_of = [(z + k) % nz for k in (1, 2, 3, 0)]
+    place_of = [flip(z, k) for k in (2, 3, 1, 0)]
     hpre_load(place_of[0], 0).start()
     for copy in later:
         copy.wait()
@@ -889,11 +959,17 @@
             total = total + dot_nt(g_s[j, at, :], w_s[:, j * d : (j + 1) * d])
         gx_s[to] = total.astype(BF)
         if i + 1 < nz:
-            rows.copy(i + 1).start()
+            rows.copy((2, 3, 1)[i]).start()
         else:
             rows.own().start()
 
-    vsum_ref[...] = vec_ref[...]
+    ud.stage4(2)
+    ud.stage5(2)
+
+    vsum_ref[...] = jnp.zeros_like(vsum_ref)
+    vsum_ref[0:8, :] = vecg_ref[...]
+    for i in range(bing_ref.shape[1] // d):
+        vsum_ref[8 + i : 9 + i, :] = bing_ref[:, i * d : (i + 1) * d]
     xt = xt_s[...]
     for j in range(3):
         grad = dot_nn(xt, g_s[j]).astype(BF)
@@ -902,7 +978,7 @@
             m0[0, t, :, :, :, j * wl : (j + 1) * wl] = part.reshape(m0.shape[2:5] + (wl,))
         if j != 1:
             sums = jnp.sum(g_s[j].astype(F32), axis=0, keepdims=True)
-            r = vec_ref.shape[0] - 2 + j // 2
+            r = vsum_ref.shape[0] - 2 + j // 2
             vsum_ref[r : r + 1, :] = sums
     for t in range(nz):
         part = gwo_s[:, t * wl : (t + 1) * wl]
@@ -938,19 +1014,18 @@
             mx.stage4(k - 2)
         if 3 <= k <= nz + 1:
             mx.stage5(k - 3)
+    ud.stage4(3)
     ud.finish(out_ref)
     mx.finish(out_ref)
     ud.drain()
     mx.drain()
     for k in range(len(partners)):
         vec_copy(k).wait_send()
-    layer.wait_recv()
-    layer.wait_send()
     rows.wait_recv()
     rows.wait_send()
 
 
-def last(layer, gup, gdn, gwo, ghpre, qkv, att, gatt, wqkv, xt, lse, segc, vec):
+def last(gup, gdn, gwo, ghpre, qkv, att, gatt, wqkv, xt, lse, ext, vecg, bing):
     nz, nd = lax.axis_size("tensor"), lax.axis_size("dp")
     length, d = att.shape
     rw, wide = d // nd, gup.shape[2]
@@ -961,16 +1036,16 @@
     dma = pltpu.SemaphoreType.DMA
     s = jax.ShapeDtypeStruct
     steps = 5
+    vec_shape = (16, d)
     return pl.pallas_call(
         last_kernel,
         out_shape=(
             s((nz, blk, d), BF),
-            s((nz, blk, d), BF),
             s((3, rw, wide), F32),
-            s(vec.shape, F32),
+            s(vec_shape, F32),
         ),
-        in_specs=[any_] * 10 + [vmem] * 3,
-        out_specs=(any_, any_, vmem, vmem),
+        in_specs=[any_] * 9 + [vmem] * 4,
+        out_specs=(any_, vmem, vmem),
         scratch_shapes=[
             pltpu.VMEM((2, 5, length, LANES), BF),
             pltpu.VMEM((3, length, d), BF),
@@ -985,7 +1060,7 @@
             pltpu.VMEM((8, length), F32),
             pltpu.VMEM((length, LANES), F32),
             pltpu.VMEM((length, LANES), F32),
-            pltpu.VMEM((2, steps) + vec.shape, F32),
+            pltpu.VMEM((2, steps) + vec_shape, F32),
         ]
         + scatter_scratch(2, nz, nd, rw, wide)
         + scatter_scratch(1, nz, nd, rw, wide)
@@ -998,8 +1073,6 @@
             dma((3, nz, 7)),
             dma((nz,)),
             dma((nz,)),
-            dma((nz,)),
-            dma((nz,)),
             dma((steps,)),
             dma((steps,)),
         ],
@@ -1008,8 +1081,8 @@
         ),
         name="last",
     )(
-        layer.reshape(nz, blk, d), gup.reshape(unit), gdn.reshape(unit), gwo,
-        ghpre.reshape(nz, blk, d), qkv, att, gatt, wqkv, xt, lse, segc, vec,
+        gup.reshape(unit), gdn.reshape(unit), gwo, ghpre.reshape(nz, blk, d),
+        qkv, att, gatt, wqkv, xt, lse, ext, vecg, bing,
     )
 
 
@@ -1017,7 +1090,7 @@
 
 
 def plain_attend_kernel(q_ref, k_ref, v_ref, segc_ref, o_ref, lse_ref, kx_s, qx_s, vt_s):
-    doc_lanes(segc_ref, kx_s, qx_s)
+    doc_lanes(segc_ref[...], kx_s, qx_s)
     vt_s[:, HD:, :] = jnp.ones((2, vt_s.shape[1] - HD, vt_s.shape[2]), BF)
     o_ref[...], lse_ref[...] = attend_pair(q_ref[...], k_ref[...], v_ref[...], kx_s, qx_s, vt_s)
 
@@ -1026,7 +1099,7 @@
     q_ref, k_ref, v_ref, att_ref, g_ref, lse_ref, segc_ref, gq_ref, gk_ref, gv_ref,
     kx_s, qx_s, kt_s, delta_s, dk_s, dv_s,
 ):
-    doc_lanes(segc_ref, kx_s, qx_s)
+    doc_lanes(segc_ref[...], kx_s, qx_s)
 
     def put_q(at, value):
         gq_ref[at, :] = value
@@ -1046,11 +1119,16 @@
     return d // LANES, col, seg, lse, wide
 
 
-def plain_first(tokens, cot, shards, bias, segc):
+def plain_first(tokens, cot, qkv_w, wo_w, up_w, dn_w, qv_b, segment_ids):
     axes = ("tensor", "dp")
     nz = lax.axis_size("tensor")
-    length, d = segc.shape[0], tokens.shape[2]
+    length, d = segment_ids.shape[1], tokens.shape[2]
     pairs, col, seg, lse_spec, wide = plain_specs(length, d)
+    mix = jnp.concatenate((qkv_w[0], qkv_w[1], qkv_w[2], wo_w), axis=1)
+    shards = jnp.stack((mix, up_w, dn_w))
+    ids = lax.dynamic_index_in_dim(segment_ids, lax.axis_index("tensor"), 0, keepdims=False)
+    segc = jnp.broadcast_to(ids[:, None], (length, LANES))
+    bias = jnp.concatenate((qv_b[0], jnp.zeros((d,), F32), qv_b[1]))
     x = lax.all_to_all(tokens, "tensor", 0, 0)
     cot = lax.all_to_all(cot, "tensor", 0, 0)
     w = lax.all_gather(shards, axes, axis=1, tiled=True).reshape(3, nz, d, shards.shape[2])
@@ -1071,10 +1149,10 @@
         compiler_params=pltpu.CompilerParams(vmem_limit_bytes=VMEM_LIMIT),
         name="plain_attend",
     )(qkv, qkv, qkv, segc)
-    return x, cot, w[1:], qkv, wqkv, rows.T, wo, att, lse
-
-
-def plain_last(layer, gup, gdn, gwo, ghpre, qkv, att, gatt, wqkv, xt, lse, segc, vec):
+    return x, cot, w[1:], qkv, wqkv, rows.T, wo, att, lse, segc
+
+
+def plain_last(gup, gdn, gwo, ghpre, qkv, att, gatt, wqkv, xt, lse, segc, vecg, bing):
     axes = ("tensor", "dp")
     nz = lax.axis_size("tensor")
     length, d = att.shape
@@ -1102,9 +1180,10 @@
         for p in (gmix, gup, gdn)
     ]
     sums = [jnp.sum(grads[j].astype(F32), axis=0, keepdims=True) for j in (0, 2)]
-    vec = jnp.concatenate((vec[:-2], *sums), axis=0)
+    bing = bing.reshape(-1, d)
+    gap = jnp.zeros((6 - bing.shape[0], d), F32)
+    vec = jnp.concatenate((vecg, bing, gap, *sums), axis=0)
     return (
-        lax.all_to_all(split(layer), "tensor", 0, 0),
         lax.all_to_all(split(gx), "tensor", 0, 0),
         jnp.stack(parts).astype(F32),
         lax.psum(vec, axes),
@@ -1115,31 +1194,25 @@
     tokens, segment_ids, drop_flags, qkv_w, qv_b, wo_w, wo_b, gain1, shift1,
     up_w, up_b, dn_w, dn_b, gain2, shift2, cotangent,
 ):
-    me = lax.axis_index("tensor")
     nt, nd = lax.axis_size("tensor"), lax.axis_size("dp")
     d = tokens.shape[2]
     length = segment_ids.shape[1]
     wl = qkv_w.shape[2]
     fl = up_w.shape[1]
-    begin, end = (first, last) if (nt, nd) == (4, 8) else (plain_first, plain_last)
-
-    mix = jnp.concatenate((qkv_w[0], qkv_w[1], qkv_w[2], wo_w.T), axis=1)
-    shards = jnp.stack((mix, up_w, dn_w.T))
-    seg = lax.dynamic_index_in_dim(segment_ids, me, 0, keepdims=False)
-    drop = lax.dynamic_slice_in_dim(drop_flags, me, 1)
-    segc = jnp.broadcast_to(seg[:, None], (length, LANES))
-    bias = jnp.concatenate((qv_b[0], jnp.zeros((d,), F32), qv_b[1]))
-    zero_row = jnp.zeros((d,), F32)
-    vec = jnp.stack((wo_b, gain1, shift1, dn_b, gain2, shift2, zero_row, zero_row))
-
-    x, cot, wud, qkv, wqkv, xt, wo, att, lse = begin(tokens, cotangent, shards, bias[None], segc)
-    layer, g_att, g_hpre, gup, gdn, gwo, vecg, bing = middle(
-        drop, att, x.reshape(length, d), cot.reshape(length, d), wo, wud.reshape(2, nt, d, fl), vec,
-        up_b.reshape(nt, fl),
-    )
-    flat = jnp.concatenate((vecg[:6], bing.reshape(-1, d), jnp.zeros((6, d), F32)), axis=0)
-    layer_out, rows, grads, total = end(
-        layer, gup, gdn, gwo, g_hpre, qkv, att, g_att, wqkv, xt, lse, segc, flat
+    comm = (nt, nd) == (4, 8)
+    begin, end = (first, last) if comm else (plain_first, plain_last)
+    x, cot, wud, qkv, wqkv, xt, wo, att, lse, ext = begin(
+        tokens, cotangent, qkv_w, wo_w.T, up_w, dn_w.T, qv_b, segment_ids
+    )
+    vecs = (wo_b, gain1, shift1, dn_b, gain2, shift2)
+    layer_out, g_att, g_hpre, gup, gdn, gwo, vecg, bing = middle(
+        comm, drop_flags, att, x.reshape(length, d), cot.reshape(length, d), cotangent, wo,
+        wud.reshape(2, nt, d, fl), vecs, up_b,
+    )
+    if not comm:
+        layer_out = lax.all_to_all(layer_out.reshape(nt, length // nt, d), "tensor", 0, 0)
+    rows, grads, total = end(
+        gup, gdn, gwo, g_hpre, qkv, att, g_att, wqkv, xt, lse, ext, vecg, bing
     )
     g_mix, g_up, g_dn = grads[0], grads[1], grads[2]
     n_bin = nt * fl // d
@@ -1153,7 +1226,7 @@
         total[1],
         total[2],
         g_up,
-        total[6 : 6 + n_bin].reshape(-1),
+        total[8 : 8 + n_bin].reshape(-1),
         g_dn.T,
         total[3],
         total[4],

time: 331 us -> 272 us (0.82); the launches traced: 324 us -> 271 us
  Pallas kernels: 305 us -> 258 us
  other arithmetic: 6.03 us -> 2.66 us
    pallas_call x3, Pallas kernels: 305 us -> 258 us  [the longest x1 102 us: last(): pl.pallas_call(last_kernel, out_shape=(s((nz, blk, d), BF), s((3, rw, wid...]
where the time goes in v4:
time: 272 us; the launch traced here: 271 us
  Pallas kernels  258 us (95%)
  local copies, waits for them, and re-layouts  9.94 us (4%)
    pallas_call x1, Pallas kernels, last(): pl.pallas_call(last_kernel, out_shape=(s((nz, blk, d), BF), s((3, rw, wid...  102 us
    pallas_call x1, Pallas kernels, first(): pl.pallas_call(first_kernel, out_shape=(s(tokens.shape, BF), s(tokens.sha...  91.1 us
    pallas_call x1, Pallas kernels, middle(): pl.pallas_call(functools.partial(middle_kernel, comm, nr), grid=(nr + par...  64.4 us

profile of v4, /device:TPU:0, one launch (start us, length us, event | category | flops | bytes accessed | tf_op | source)
XLA Modules:
  0.0 271.1 jit_solution(16214765849826479327)
XLA Ops:
  0.6 1.5 copy.30
  2.2 91.1 %first.1 = (bf16[4,256,768]{2,1,0:T(8,128)(2,1)}, bf16[4,256,768]{2,1,0:T(8,128)(2,1)}, bf16[2,4,4,2,96,768]{5,4,3,2,1,0:T(8,128)(2,1)}, bf16[1024,2304]{1,0:T(8...) custom-call(bf16[4,256,768]{2,1,0:T(8,128)(2,1)} %tok_ref.1, ...), custom_call_target="tpu_custom_call" | custom-call | tf_op jit(solution)/shard_map/first/pallas_call | solution.py:814
  93.2 64.4 %middle.1 = (bf16[4,256,768]{2,1,0:T(8,128)(2,1)}, bf16[1024,768]{1,0:T(8,128)(2,1)}, f32[1024,768]{1,0:T(8,128)}, bf16[4,768,768]{2,1,0:T(8,128)(2,1)}, bf16[4,...) custom-call(s32[4]{0:T(128)} %refs_0_.1, ...), custom_call_target="tpu_custom_call" | custom-call | tf_op jit(solution)/shard_map/middle/pallas_call | solution.py:653
  157.6 102.3 %last.1 = (bf16[4,256,768]{2,1,0:T(8,128)(2,1)}, f32[3,96,768]{2,1,0:T(8,128)}, f32[16,768]{1,0:T(8,128)}) custom-call(bf16[4,4,2,96,768]{4,3,2,1,0:T(8,128)(2,1)} %bitcast.26, bf16[4,4,2,96,768]{4,3,2,1,0:T(8,128)(2,1)} %bitcast.27, bf16[768,768]{1,0:T(8,128)(2,1)} %get-tuple-element.43.gwo_ref, f32[4,256,768]{2,1,0:T(8,128)} %bitcast.28, ...), custom_call_target="tpu_custom_call" | custom-call | tf_op jit(solution)/shard_map/last/pallas_call | solution.py:1040
  260.0 1.3 slice.49
  261.3 0.7 slice.55
  262.0 1.6 slice_reduce_fusion
  263.6 0.6 reshape.55
  264.3 0.0 copy-start.1
  264.3 2.1 slice_bitcast_fusion
  266.4 0.1 slice_bitcast_fusion.3
  266.5 0.7 copy.31
  267.2 0.7 pad_maximum_fusion
  268.0 0.0 copy-done.1
  268.0 0.0 copy-start
  268.0 1.9 convert_element_type.3
  269.9 0.0 copy-done
  269.9 1.1 copy.33
Async XLA Ops:
  264.3 3.7 %copy-start.1 = (bf16[4,256,768]{2,1,0:T(8,128)(2,1)S(1)}, bf16[4,256,768]{2,1,0:T(8,128)(2,1)}, u32[]{:S(2)}) copy-start(bf16[4,256,768]{2,1,0:T(8,128)(2,1)} %get-tuple-element.53) | copy-start | bytes 4718596
  268.0 1.9 copy-start

commit v5 on v4

--- a/solution.py
+++ b/solution.py
@@ -198,275 +198,234 @@
 
 
 class Gather:
-    def __init__(self, here, w_ref, sh_ref, first, count, send, recv, local):
-        self.here, self.w, self.sh, self.first, self.count = here, w_ref, sh_ref, first, count
-        self.send, self.recv, self.local = send, recv, local
-
-    def blk(self, a, t, yx):
-        return self.w.at[a, t, yx, self.here.core]
-
-    def copy(self, src, dst, a, t, sender, receiver, dp, z):
-        f = self.first + a
-        return remote(src, dst, self.send.at[f, t, sender], self.recv.at[f, t, receiver], dp, z)
-
-    def firsts(self, a, t, own):
+    def __init__(self, here, w_ref, sh_ref, group, send, recv, line, local):
+        self.here, self.w, self.sh = here, w_ref, sh_ref
+        self.send = lambda kind: send.at[group, kind]
+        self.recv = lambda t, kind: recv.at[group, t, kind]
+        self.line = lambda t, kind: line.at[group, t, kind]
+        self.all_cores = recv.at[group, 0, 5]
+        self.local = local.at[group]
+        half = w_ref.shape[4] // 2
+        self.low, self.high = pl.ds(0, half), pl.ds(half, half)
+
+    def blk(self, t, yx):
+        return self.w.at[t, yx, self.here.core]
+
+    def to_plane(self, t, own, kind):
         h = self.here
-        dst = self.blk(a, t, h.yx)
-        src = self.sh.at[self.first + a] if own else dst
-        return (
-            lambda: self.copy(src, dst, a, t, 0, 0, h.dev_x, h.z),
-            lambda: self.copy(src, dst, a, t, 1, 1, h.dev_y, h.z),
-            lambda: self.copy(src, dst, a, t, 2, 5, h.dev_c, h.z),
-            lambda: self.copy(src, dst, a, t, 8, 4, h.dp, (h.z + 1) % h.nz),
-            lambda: self.copy(src, dst, a, t, 9, 4, h.dp, (h.z + h.nz - 1) % h.nz),
-        )
-
-    def own_copy(self, a, t):
-        return pltpu.make_async_copy(
-            self.sh.at[self.first + a], self.blk(a, t, self.here.yx), self.local.at[self.first + a]
-        )
-
-    def halves(self, a, t):
+        dst = self.blk(t, h.yx)
+        dev = (h.dev_x, h.dev_y, h.dev_c)[kind]
+        arrived = self.all_cores if kind == 2 else self.recv(t, kind)
+        return remote(self.sh if own else dst, dst, self.send(kind), arrived, dev, h.z)
+
+    def to_line(self, t, own, kind):
         h = self.here
-        half = self.w.shape[4] // 2
-        to_y = self.blk(a, t, h.yx_x).at[pl.ds(0, half)]
-        to_x = self.blk(a, t, h.yx_y).at[pl.ds(half, half)]
-        return (
-            self.copy(to_y, to_y, a, t, 3, 2, h.dev_y, h.z),
-            self.copy(to_x, to_x, a, t, 4, 3, h.dev_x, h.z),
-        )
-
-    def to_core(self, a, t, yx, kind):
-        b = self.blk(a, t, yx)
-        return self.copy(b, b, a, t, kind, 5, self.here.dev_c, self.here.z)
-
-    def each(self, s, body):
-        def run(a, carry):
-            self.here.sides(s, lambda t, from_left: body(a, t, from_left))
-            return carry
-
-        lax.fori_loop(0, self.count, run, 0)
-
-    def along(self, own, from_left, right, left):
+        dst = self.blk(t, h.yx)
+        to = (h.z + 1) % h.nz if kind == 0 else (h.z + h.nz - 1) % h.nz
+        return remote(self.sh if own else dst, dst, self.line(t, kind), self.recv(t, 4), h.dp, to)
+
+    def own_copy(self):
+        return pltpu.make_async_copy(self.sh, self.blk(self.here.z, self.here.yx), self.local)
+
+    def half_y(self, t):
+        b = self.w.at[t, self.here.yx_x, self.here.core, :, self.low]
+        return remote(b, b, self.send(3), self.recv(t, 2), self.here.dev_y, self.here.z)
+
+    def half_x(self, t):
+        b = self.w.at[t, self.here.yx_y, self.here.core, :, self.high]
+        return remote(b, b, self.send(4), self.recv(t, 3), self.here.dev_x, self.here.z)
+
+    def to_core(self, t, yx, kind):
+        b = self.blk(t, yx)
+        return remote(b, b, self.send(kind), self.all_cores, self.here.dev_c, self.here.z)
+
+    def along(self, s, from_left, right, left):
         h = self.here
-        if own or from_left:
+        if s == 0 or from_left:
             pl.when(h.z < h.nz - 1)(right)
-        if own or not from_left:
+        if s == 0 or not from_left:
             pl.when(h.z > 0)(left)
 
     def stage1(self, s):
-        h, own = self.here, s == 0
-
-        def body(a, t, from_left):
+        own = s == 0
+
+        def body(t, from_left):
             if own:
-                self.own_copy(a, t).start()
+                self.own_copy().start()
             else:
-                landed(self.blk(a, t, h.yx), self.recv.at[self.first + a, t, 4])
-            x, y, c, right, left = self.firsts(a, t, own)
-            self.along(own, from_left, lambda: right().start(), lambda: left().start())
-            x().start()
-            y().start()
-            c().start()
-
-        self.each(s, body)
+                landed(self.blk(t, self.here.yx), self.recv(t, 4))
+            self.along(
+                s, from_left,
+                lambda: self.to_line(t, own, 0).start(), lambda: self.to_line(t, own, 1).start(),
+            )
+            for kind in range(3):
+                self.to_plane(t, own, kind).start()
+
+        self.here.sides(s, body)
 
     def stage2(self, s):
         h = self.here
 
-        def body(a, t, from_left):
-            f = self.first + a
-            to_y, to_x = self.halves(a, t)
-            landed(self.blk(a, t, h.yx_x), self.recv.at[f, t, 0])
-            to_y.start()
-            self.to_core(a, t, h.yx_x, 5).start()
-            landed(self.blk(a, t, h.yx_y), self.recv.at[f, t, 1])
-            to_x.start()
-            self.to_core(a, t, h.yx_y, 6).start()
-
-        self.each(s, body)
+        def body(t, from_left):
+            landed(self.blk(t, h.yx_x), self.recv(t, 0))
+            self.half_y(t).start()
+            self.to_core(t, h.yx_x, 5).start()
+            landed(self.blk(t, h.yx_y), self.recv(t, 1))
+            self.half_x(t).start()
+            self.to_core(t, h.yx_y, 6).start()
+
+        h.sides(s, body)
 
     def stage3(self, s):
         h = self.here
-        half = self.w.shape[4] // 2
-
-        def body(a, t, from_left):
-            f = self.first + a
-            b = self.blk(a, t, h.yx_d)
-            landed(b.at[pl.ds(0, half)], self.recv.at[f, t, 2])
-            landed(b.at[pl.ds(half, half)], self.recv.at[f, t, 3])
-            self.to_core(a, t, h.yx_d, 7).start()
-
-        self.each(s, body)
+
+        def body(t, from_left):
+            landed(self.w.at[t, h.yx_d, h.core, :, self.low], self.recv(t, 2))
+            landed(self.w.at[t, h.yx_d, h.core, :, self.high], self.recv(t, 3))
+            self.to_core(t, h.yx_d, 7).start()
+
+        h.sides(s, body)
 
     def drain(self):
-        h = self.here
+        h, w = self.here, self.w
+        landed(w.at[:, :, 1 - h.core], self.all_cores)
+        self.own_copy().wait()
+        for kind in (0, 1, 2, 5, 6, 7):
+            landed(w.at[:, h.yx, h.core], self.send(kind))
+        landed(w.at[:, h.yx_x, h.core, :, self.low], self.send(3))
+        landed(w.at[:, h.yx_y, h.core, :, self.high], self.send(4))
         for s in range(h.nz):
-            own = s == 0
-
-            def body(a, t, from_left):
-                landed(self.w.at[a, t, :, 1 - h.core], self.recv.at[self.first + a, t, 5])
-                if own:
-                    self.own_copy(a, t).wait()
-                x, y, c, right, left = self.firsts(a, t, own)
-                self.along(own, from_left, lambda: right().wait_send(), lambda: left().wait_send())
-                for copy in (x(), y(), c(), *self.halves(a, t)):
-                    copy.wait_send()
-                for yx, kind in ((h.yx_x, 5), (h.yx_y, 6), (h.yx_d, 7)):
-                    self.to_core(a, t, yx, kind).wait_send()
-
-            self.each(s, body)
+
+            def body(t, from_left):
+                self.along(
+                    s, from_left,
+                    lambda: self.to_line(t, s == 0, 0).wait_send(),
+                    lambda: self.to_line(t, s == 0, 1).wait_send(),
+                )
+
+            h.sides(s, body)
 
 
 class Scatter:
-    def __init__(self, here, own, rc, rda, rdb, rx, ry, rz, first, send, recv):
-        self.here, self.own, self.first, self.count = here, own, first, own.shape[0]
+    def __init__(self, here, own, rc, rda, rdb, rx, ry, rz, group, send, recv, order=None):
+        self.here, self.own = here, own
         self.rc, self.rda, self.rdb, self.rx, self.ry, self.rz = rc, rda, rdb, rx, ry, rz
-        self.send, self.recv = send, recv
+        self.send = lambda kind: send.at[group, kind]
+        self.recv = lambda t, kind: recv.at[group, t, kind]
+        half = own.shape[4] // 2
+        self.low, self.high = pl.ds(0, half), pl.ds(half, half)
         z = here.z
-        self.order = [3 * (1 - z // 2), (2 + 3 * z) % 5, 1 + z % 2, z]
-
-    def copies(self, a, t):
-        h, own, f = self.here, self.own, self.first + a
-        half = own.shape[4] // 2
-        d = own.at[a, t, h.yx_d, h.core]
-        mine = own.at[a, t, h.yx, h.core]
-        sem = lambda k: (self.send.at[f, t, k], self.recv.at[f, t, k])
-        return (
-            lambda: remote(own.at[a, t, :, 1 - h.core], self.rc.at[a, t], *sem(0), h.dev_c, h.z),
-            lambda: remote(d.at[pl.ds(0, half)], self.rda.at[a, t], *sem(1), h.dev_x, h.z),
-            lambda: remote(d.at[pl.ds(half, half)], self.rdb.at[a, t], *sem(2), h.dev_y, h.z),
-            lambda: remote(own.at[a, t, h.yx_x, h.core], self.rx.at[a, t], *sem(3), h.dev_x, h.z),
-            lambda: remote(own.at[a, t, h.yx_y, h.core], self.ry.at[a, t], *sem(4), h.dev_y, h.z),
-            lambda: remote(mine, self.rz.at[0, a, t], *sem(5), h.dp, (h.z + 1) % h.nz),
-            lambda: remote(mine, self.rz.at[1, a, t], *sem(6), h.dp, (h.z + h.nz - 1) % h.nz),
-        )
-
-    def each(self, k, body):
-        t = self.order[k]
-
-        def run(a, carry):
-            body(a, t, self.copies(a, t))
-            return carry
-
-        lax.fori_loop(0, self.count, run, 0)
-
-    def got(self, ref, a, t, kind):
-        landed(ref, self.recv.at[self.first + a, t, kind])
-
-    def add(self, dst, src):
-        dst[...] = (dst[...].astype(F32) + src[...].astype(F32)).astype(BF)
+        self.order = order or [3 * (1 - z // 2), (2 + 3 * z) % 5, 1 + z % 2, z]
+
+    def copy(self, t, kind):
+        h, own = self.here, self.own
+        src, dst, dev, z = (
+            lambda: (own.at[t, :, 1 - h.core], self.rc.at[t], h.dev_c, h.z),
+            lambda: (own.at[t, h.yx_d, h.core, :, self.low], self.rda.at[t], h.dev_x, h.z),
+            lambda: (own.at[t, h.yx_d, h.core, :, self.high], self.rdb.at[t], h.dev_y, h.z),
+            lambda: (own.at[t, h.yx_x, h.core], self.rx.at[t], h.dev_x, h.z),
+            lambda: (own.at[t, h.yx_y, h.core], self.ry.at[t], h.dev_y, h.z),
+            lambda: (own.at[t, h.yx, h.core], self.rz.at[0, t], h.dp, (h.z + 1) % h.nz),
+            lambda: (own.at[t, h.yx, h.core], self.rz.at[1, t], h.dp, (h.z + h.nz - 1) % h.nz),
+        )[kind]()
+        return remote(src, dst, self.send(min(kind, 5)), self.recv(t, kind), dev, z)
+
+    def add(self, dst, *srcs):
+        total = dst[...].astype(F32)
+        for src in srcs:
+            total = total + src[...].astype(F32)
+        dst[...] = total.astype(BF)
 
     def stage1(self, k):
-        self.each(k, lambda a, t, copies: copies[0]().start())
+        self.copy(self.order[k], 0).start()
 
     def stage2(self, k):
-        h = self.here
-
-        def body(a, t, copies):
-            self.got(self.rc.at[a, t], a, t, 0)
-            for q in range(4):
-                self.add(self.own.at[a, t, q, h.core], self.rc.at[a, t, q])
-            copies[1]().start()
-            copies[2]().start()
-
-        self.each(k, body)
+        h, t = self.here, self.order[k]
+        landed(self.rc.at[t], self.recv(t, 0))
+        self.add(self.own.at[t, h.yx_d, h.core], self.rc.at[t, h.yx_d])
+        self.copy(t, 1).start()
+        self.copy(t, 2).start()
+        for yx in (h.yx_x, h.yx_y, h.yx):
+            self.add(self.own.at[t, yx, h.core], self.rc.at[t, yx])
 
     def stage3(self, k):
-        h = self.here
-        half = self.own.shape[4] // 2
-
-        def body(a, t, copies):
-            self.got(self.rda.at[a, t], a, t, 1)
-            self.add(self.own.at[a, t, h.yx_y, h.core, pl.ds(0, half)], self.rda.at[a, t])
-            copies[4]().start()
-            self.got(self.rdb.at[a, t], a, t, 2)
-            self.add(self.own.at[a, t, h.yx_x, h.core, pl.ds(half, half)], self.rdb.at[a, t])
-            copies[3]().start()
-
-        self.each(k, body)
+        h, t = self.here, self.order[k]
+        landed(self.rda.at[t], self.recv(t, 1))
+        self.add(self.own.at[t, h.yx_y, h.core, :, self.low], self.rda.at[t])
+        self.copy(t, 4).start()
+        landed(self.rdb.at[t], self.recv(t, 2))
+        self.add(self.own.at[t, h.yx_x, h.core, :, self.high], self.rdb.at[t])
+        self.copy(t, 3).start()
 
     def stage4(self, k):
-        h = self.here
-
-        def body(a, t, copies):
-            mine = self.own.at[a, t, h.yx, h.core]
-            self.got(self.rx.at[a, t], a, t, 3)
-            self.got(self.ry.at[a, t], a, t, 4)
-            mine[...] = (
-                mine[...].astype(F32) + self.rx[a, t].astype(F32) + self.ry[a, t].astype(F32)
-            ).astype(BF)
-
-        self.each(k, body)
+        h, t = self.here, self.order[k]
+        landed(self.rx.at[t], self.recv(t, 3))
+        landed(self.ry.at[t], self.recv(t, 4))
+        self.add(self.own.at[t, h.yx, h.core], self.rx.at[t], self.ry.at[t])
 
     def stage5(self, k):
-        h = self.here
-
-        def body(a, t, copies):
-            mine = self.own.at[a, t, h.yx, h.core]
-
-            @pl.when(t > h.z)
+        h, t = self.here, self.order[k]
+        mine = self.own.at[t, h.yx, h.core]
+
+        @pl.when(t > h.z)
+        def _():
+            @pl.when(h.z > 0)
             def _():
-                @pl.when(h.z > 0)
-                def _():
-                    self.got(self.rz.at[0, a, t], a, t, 5)
-                    self.add(mine, self.rz.at[0, a, t])
-
-                copies[5]().start()
-
-            @pl.when(t < h.z)
+                landed(self.rz.at[0, t], self.recv(t, 5))
+                self.add(mine, self.rz.at[0, t])
+
+            self.copy(t, 5).start()
+
+        @pl.when(t < h.z)
+        def _():
+            @pl.when(h.z < h.nz - 1)
             def _():
-                @pl.when(h.z < h.nz - 1)
-                def _():
-                    self.got(self.rz.at[1, a, t], a, t, 6)
-                    self.add(mine, self.rz.at[1, a, t])
-
-                copies[6]().start()
-
-        self.each(k, body)
-
-    def finish(self, out_ref):
-        h = self.here
-
-        def run(a, carry):
-            f, z = self.first + a, h.z
-            out_ref[f] = self.own[a, z, h.yx, h.core].astype(F32)
-
-            @pl.when(z > 0)
-            def _():
-                self.got(self.rz.at[0, a, z], a, z, 5)
-                out_ref[f] += self.rz[0, a, z].astype(F32)
-
-            @pl.when(z < h.nz - 1)
-            def _():
-                self.got(self.rz.at[1, a, z], a, z, 6)
-                out_ref[f] += self.rz[1, a, z].astype(F32)
-
-            return carry
-
-        lax.fori_loop(0, self.count, run, 0)
+                landed(self.rz.at[1, t], self.recv(t, 6))
+                self.add(mine, self.rz.at[1, t])
+
+            self.copy(t, 6).start()
+
+    def total(self):
+        h, z = self.here, self.here.z
+        mine = self.own.at[z, h.yx, h.core]
+
+        @pl.when((z > 0) & (z < h.nz - 1))
+        def _():
+            landed(self.rz.at[0, z], self.recv(z, 5))
+            landed(self.rz.at[1, z], self.recv(z, 6))
+            self.add(mine, self.rz.at[0, z], self.rz.at[1, z])
+
+        @pl.when(z == 0)
+        def _():
+            landed(self.rz.at[1, z], self.recv(z, 6))
+            self.add(mine, self.rz.at[1, z])
+
+        @pl.when(z == h.nz - 1)
+        def _():
+            landed(self.rz.at[0, z], self.recv(z, 5))
+            self.add(mine, self.rz.at[0, z])
+
+        return [mine[a].astype(F32) for a in range(mine.shape[0])]
 
     def drain(self):
-        h = self.here
-
-        def body(a, t, copies):
-            for copy in copies[:5]:
-                copy().wait_send()
-            pl.when(t > h.z)(lambda: copies[5]().wait_send())
-            pl.when(t < h.z)(lambda: copies[6]().wait_send())
-
-        for k in range(h.nz):
-            self.each(k, body)
+        h, own = self.here, self.own
+        landed(own.at[:, :, 1 - h.core], self.send(0))
+        landed(own.at[:, h.yx_d, h.core, :, self.low], self.send(1))
+        landed(own.at[:, h.yx_d, h.core, :, self.high], self.send(2))
+        landed(own.at[:, h.yx_x, h.core], self.send(3))
+        landed(own.at[:, h.yx_y, h.core], self.send(4))
+        landed(self.rz.at[0, pl.ds(0, h.nz - 1)], self.send(5))
 
 
 def scatter_scratch(na, nz, nd, rw, wide):
     return [
-        pltpu.VMEM((na, nz, nd // 2, 2, rw, wide), BF),
-        pltpu.VMEM((na, nz, nd // 2, rw, wide), BF),
-        pltpu.VMEM((na, nz, rw // 2, wide), BF),
-        pltpu.VMEM((na, nz, rw // 2, wide), BF),
-        pltpu.VMEM((na, nz, rw, wide), BF),
-        pltpu.VMEM((na, nz, rw, wide), BF),
-        pltpu.VMEM((2, na, nz, rw, wide), BF),
+        pltpu.VMEM((nz, nd // 2, 2, na, rw, wide), BF),
+        pltpu.VMEM((nz, nd // 2, na, rw, wide), BF),
+        pltpu.VMEM((nz, na, rw // 2, wide), BF),
+        pltpu.VMEM((nz, na, rw // 2, wide), BF),
+        pltpu.VMEM((nz, na, rw, wide), BF),
+        pltpu.VMEM((nz, na, rw, wide), BF),
+        pltpu.VMEM((2, nz, na, rw, wide), BF),
     ]
 
 
@@ -506,13 +465,19 @@
     )
 
 
+def partner_at(step):
+    return (6 - step) % 4
+
+
 def middle_kernel(comm, row_steps, *refs):
     drop_ref, att_ref, x_ref, cot_ref, crows_ref, wo_ref, up_ref, dn_ref = refs[:8]
     vecs, bin_ref = refs[8:14], refs[14]
     lo_ref, gatt_ref, ghpre_ref, gup_ref, gdn_ref, gwo_ref, vecg_ref, bing_ref = refs[15:23]
     att_s, act_s, gpre_s, slope_s, ht_s, gb2t_s, gbt_s = refs[23:30]
     step = pl.program_id(0)
-    parts, _, fl = up_ref.shape
+    parts, d, fl = up_ref.shape[0], att_ref.shape[1], up_ref.shape[3]
+    up = lambda t: up_ref[t].reshape(d, fl)
+    dn = lambda t: dn_ref[t].reshape(d, fl)
     vec = lambda r: vecs[r][...][None, :]
     if comm:
         cot_s, c3_s, l_s, lsend, lrecv, csend, crecv = refs[30:]
@@ -562,17 +527,17 @@
         ht_s[:, at] = jnp.transpose(low)
         ffn = hidden + vec(3)
         for t in range(parts):
-            pre = dot_nn(low, up_ref[t]) + bin_ref[t * fl : (t + 1) * fl][None, :]
+            pre = dot_nn(low, up(t)) + bin_ref[t * fl : (t + 1) * fl][None, :]
             act, slope = gelu_parts(pre)
             act = act.astype(BF)
             act_s[t, at, :] = act
             slope_s[t] = slope
-            ffn = ffn + dot_nt(act, dn_ref[t])
+            ffn = ffn + dot_nt(act, dn(t))
         n2, inv2 = norm_rows(ffn)
         final = n2 * vec(4) + vec(5)
         layer_rows = jnp.where(dropped, x, final).astype(BF)
         if comm:
-            l_s[flip(z, step)] = layer_rows
+            l_s[flip(z, partner_at(step))] = layer_rows
         else:
             lo_ref[...] = layer_rows
         g_final = jnp.where(dropped, 0.0, cot)
@@ -581,10 +546,10 @@
         gb2t_s[:, at] = jnp.transpose(gb2)
         g_hidden = g_fpre
         for t in range(parts):
-            gpre = (dot_nn(gb2, dn_ref[t]) * slope_s[t]).astype(BF)
+            gpre = (dot_nn(gb2, dn(t)) * slope_s[t]).astype(BF)
             gpre_s[t, at, :] = gpre
             bing_ref[:, t * fl : (t + 1) * fl] += jnp.sum(gpre.astype(F32), axis=0, keepdims=True)
-            g_hidden = g_hidden + dot_nt(gpre, up_ref[t])
+            g_hidden = g_hidden + dot_nt(gpre, up(t))
         g_hpre = norm_back(g_hidden, n1, inv1, vec(1))
         gb = g_hpre.astype(BF)
         gbt_s[:, at] = jnp.transpose(gb)
@@ -600,10 +565,10 @@
 
             @pl.when(step == k)
             def _():
-                if k == 0:
+                if partner_at(k) == 0:
                     layer.own().start()
                 else:
-                    layer.copy(k).start()
+                    layer.copy(partner_at(k)).start()
 
     @pl.when((step >= row_steps) & (step < row_steps + parts))
     def _():
@@ -622,11 +587,11 @@
 
 def middle(comm, drop, att, x, cot, cot_rows, wo, w, vecs, bias_in):
     length, d = att.shape
-    _, parts, _, fl = w.shape
+    parts, groups, _, group, fl = w.shape
     nr = length // BLK
 
     def place_of(i):
-        return flip(lax.axis_index("tensor"), i) if comm else i
+        return flip(lax.axis_index("tensor"), partner_at(i)) if comm else i
 
     rows = pl.BlockSpec((BLK, d), lambda i: (place_of(jnp.minimum(i, nr - 1)), 0))
     cot_spec = pl.BlockSpec((BLK, d), lambda i: (place_of(jnp.minimum(i, nr - 1 - comm)), 0))
@@ -635,7 +600,7 @@
         shape, lambda i: (0,) * len(shape), pipeline_mode=pl.Buffered(1)
     )
     weight = lambda a: pl.BlockSpec(
-        (None, parts, d, fl), lambda i: (a, 0, 0, 0), pipeline_mode=pl.Buffered(1)
+        (parts, groups, None, group, fl), lambda i: (0, 0, a, 0, 0), pipeline_mode=pl.Buffered(1)
     )
     part = pl.BlockSpec((None, d, fl), lambda i: (jnp.clip(i - nr, 0, parts - 1), 0, 0))
     whole = lambda shape: pl.BlockSpec(shape, lambda i: (0,) * len(shape))
@@ -712,20 +677,24 @@
     tok_ref, cot_ref, qkvw_ref, wow_ref, upw_ref, dnw_ref, bias_ref, seg_ref,
     x_out, cot_out, wud_out, qkv_out, wqkv_out, xt_out, wo_ref, att_ref, lse_ref, ext_ref,
     sh_ref, mix_s, x_s, qkv_s, wqkv_s, xt_s, kx_s, qx_s, vt_s,
-    out_sem, send, recv, local, tsend, trecv, csend, crecv,
+    out_sem, send, recv, line, local, tsend, trecv, csend, crecv,
 ):
-    nz = mix_s.shape[1]
+    nz = mix_s.shape[0]
     length, d = att_ref.shape
     pairs = d // LANES
     blk = length // nz
     here = Here(nz)
-    mix = Gather(here, mix_s, sh_ref, 0, 1, send, recv, local)
-    rest = Gather(here, wud_out, sh_ref, 1, 2, send, recv, local)
+    mix = Gather(here, mix_s, sh_ref.at[0:1], 0, send, recv, line, local)
+    rest = Gather(here, wud_out, sh_ref.at[1:3], 1, send, recv, line, local)
     tokens = Exchange(here, tok_ref, x_s, tsend, trecv)
     cots = Exchange(here, cot_ref, cot_out, csend, crecv, (1, 2))
     sh_ref[0] = jnp.concatenate(
-        (qkvw_ref[0], qkvw_ref[1], qkvw_ref[2], wow_ref[...]), axis=1
-    )
+        (qkvw_ref[0], qkvw_ref[1], qkvw_ref[2], jnp.transpose(wow_ref[...])), axis=1
+    )
+    out_x = pltpu.make_async_copy(x_s, x_out, out_sem.at[0])
+    out_qkv = pltpu.make_async_copy(qkv_s, qkv_out, out_sem.at[1])
+    out_w = pltpu.make_async_copy(wqkv_s, wqkv_out, out_sem.at[2])
+    out_xt = pltpu.make_async_copy(xt_s, xt_out, out_sem.at[3])
     here.greet()
     mix.stage1(0)
     sh_ref[1] = upw_ref[...]
@@ -752,37 +721,44 @@
     rest.stage2(0)
     rest.stage1(2)
     mix.drain()
-    assemble(lambda t: mix_s[0, t].reshape(d, -1), nz, wqkv_s, wo_ref)
-    rest.stage2(1)
-    rest.stage3(0)
-    tokens.wait_recv()
-    rest.stage1(3)
+    assemble(lambda t: mix_s[t].reshape(d, -1), nz, wqkv_s, wo_ref)
+    out_w.start()
+    bias = jnp.concatenate(
+        (bias_ref[0:1, :], jnp.zeros((1, d), F32), bias_ref[1:2, :]), axis=1
+    )
+    tokens.own().wait()
+
+    def project(k, carry):
+        @pl.when(k > 0)
+        def _():
+            tokens.got(k)
+
+        block = flip(here.z, k)
+        at = pl.ds(pl.multiple_of(block * blk, blk), blk)
+        qkv_s[at, :] = (dot_nn(x_s[block], wqkv_s[...]) + bias).astype(BF)
+        xt_s[:, at] = jnp.transpose(x_s[block])
+
+        @pl.when(k == 0)
+        def _():
+            rest.stage2(1)
+            rest.stage3(0)
+
+        @pl.when(k == 2)
+        def _():
+            rest.stage1(3)
+
+        return carry
+
+    lax.fori_loop(0, nz, project, 0)
+    out_x.start()
+    out_qkv.start()
+    out_xt.start()
     cots.start()
     between = [
         [lambda: rest.stage2(2), lambda: rest.stage3(1)],
         [lambda: rest.stage2(3), lambda: rest.stage3(2)],
         [lambda: rest.stage3(3)],
     ]
-    out_x = pltpu.make_async_copy(x_s, x_out, out_sem.at[0])
-    out_qkv = pltpu.make_async_copy(qkv_s, qkv_out, out_sem.at[1])
-    out_w = pltpu.make_async_copy(wqkv_s, wqkv_out, out_sem.at[2])
-    out_xt = pltpu.make_async_copy(xt_s, xt_out, out_sem.at[3])
-    out_x.start()
-    out_w.start()
-    bias = jnp.concatenate(
-        (bias_ref[0:1, :], jnp.zeros((1, d), F32), bias_ref[1:2, :]), axis=1
-    )
-
-    def body(i, carry):
-        at = pl.ds(pl.multiple_of(i * blk, blk), blk)
-        qkv_s[at, :] = (dot_nn(x_s[i], wqkv_s[...]) + bias).astype(BF)
-        return carry
-
-    lax.fori_loop(0, nz, body, 0)
-    out_qkv.start()
-    for i in range(nz):
-        xt_s[:, i * blk : (i + 1) * blk] = jnp.transpose(x_s[i])
-    out_xt.start()
 
     def work(p):
         o, lse = attend_pair(
@@ -810,13 +786,13 @@
     vmem = pl.BlockSpec(memory_space=pltpu.VMEM)
     dma = pltpu.SemaphoreType.DMA
     s = jax.ShapeDtypeStruct
-    unit = (nz, nd // 2, 2, rw, wide)
+    unit = lambda count: (nz, nd // 2, 2, count, rw, wide)
     return pl.pallas_call(
         first_kernel,
         out_shape=(
             s(tokens.shape, BF),
             s(tokens.shape, BF),
-            s((na - 1,) + unit, BF),
+            s(unit(na - 1), BF),
             s((length, 3 * d), BF),
             s((d, 3 * d), BF),
             s((d, length), BF),
@@ -829,7 +805,7 @@
         out_specs=(any_,) * 6 + (vmem,) * 4,
         scratch_shapes=[
             pltpu.VMEM((na, rw, wide), BF),
-            pltpu.VMEM((1,) + unit, BF),
+            pltpu.VMEM(unit(1), BF),
             pltpu.VMEM((nz, blk, d), BF),
             pltpu.VMEM((length, 3 * d), BF),
             pltpu.VMEM((d, 3 * d), BF),
@@ -838,9 +814,10 @@
             pltpu.VMEM((length, 2 * LANES), BF),
             pltpu.VMEM((2, HD + 16, length), BF),
             dma((4,)),
-            dma((na, nz, 10)),
-            dma((na, nz, 6)),
-            dma((na,)),
+            dma((2, 8)),
+            dma((2, nz, 6)),
+            dma((2, nz, 2)),
+            dma((2,)),
             dma((nz,)),
             dma((nz,)),
             dma((nz,)),
@@ -856,12 +833,12 @@
 def last_kernel(
     gup_ref, gdn_ref, gwo_ref, ghpre_ref, qkv_ref, att_ref, gatt_ref, wqkv_ref, xt_ref,
     lse_ref, ext_ref, vecg_ref, bing_ref,
-    grows_ref, out_ref, vsum_ref,
+    grows_ref, gqkv_ref, gout_ref, gup_out, gdn_out, vsum_ref,
     pair_s, g_s, w_s, xt_s, hpre_s, gwo_s, gx_s, kx_s, qx_s, kt_s, delta_s, dk_s, dv_s, vbuf,
     u0, u1, u2, u3, u4, u5, u6, m0, m1, m2, m3, m4, m5, m6,
     psem, hsem, load, uload, send, recv, xsend, xrecv, vsend, vrecv,
 ):
-    nz = u0.shape[1]
+    nz = u0.shape[0]
     length, d = g_s.shape[1:]
     pairs = d // LANES
     blk = length // nz
@@ -885,9 +862,18 @@
     def ud_loads(k):
         t = ud.order[k]
         return [
-            pltpu.make_async_copy(g.at[t], u0.at[a, t], uload.at[a, t])
+            pltpu.make_async_copy(
+                g.at[t, :, here.core], u0.at[t, :, here.core, a], uload.at[a, t]
+            )
             for a, g in enumerate((gup_ref, gdn_ref))
         ]
+
+    def ud_core(k):
+        t = ud.order[k]
+        for a, g in enumerate((gup_ref, gdn_ref)):
+            remote(
+                g.at[t, :, 1 - here.core], u1.at[t, :, a], ud.send(0), ud.recv(t, 0), here.dev_c, z
+            ).start()
 
     later = [
         pltpu.make_async_copy(src, dst, load.at[i])
@@ -903,12 +889,10 @@
         for copy in ud_loads(k):
             copy.start()
     here.greet()
+    for k in range(nz):
+        ud_core(k)
     kx_s[:, LANES:] = ext_ref[:, :LANES]
     qx_s[:, LANES:] = ext_ref[:, LANES:]
-    for k in range(nz):
-        for copy in ud_loads(k):
-            copy.wait()
-        ud.stage1(k)
 
     def work(p):
         slot = p % 2
@@ -936,8 +920,13 @@
     def run(*names):
         return [lambda name=name, k=k: getattr(ud, name)(k) for name, k in names]
 
+    def halves_here():
+        for k in range(nz):
+            for copy in ud_loads(k):
+                copy.wait()
+
     between = [
-        run(("stage2", 0), ("stage2", 1)),
+        [halves_here] + run(("stage2", 0), ("stage2", 1)),
         run(("stage2", 2), ("stage3", 0), ("stage2", 3)),
         run(("stage3", 1),) + [start_later],
         run(("stage4", 0), ("stage5", 0), ("stage3", 2)),
@@ -975,14 +964,14 @@
         grad = dot_nn(xt, g_s[j]).astype(BF)
         for t in range(nz):
             part = grad[:, t * wl : (t + 1) * wl]
-            m0[0, t, :, :, :, j * wl : (j + 1) * wl] = part.reshape(m0.shape[2:5] + (wl,))
+            m0[t, :, :, 0, :, j * wl : (j + 1) * wl] = part.reshape(m0.shape[1:3] + (m0.shape[4], wl))
         if j != 1:
             sums = jnp.sum(g_s[j].astype(F32), axis=0, keepdims=True)
             r = vsum_ref.shape[0] - 2 + j // 2
             vsum_ref[r : r + 1, :] = sums
     for t in range(nz):
         part = gwo_s[:, t * wl : (t + 1) * wl]
-        m0[0, t, :, :, :, 3 * wl :] = part.reshape(m0.shape[2:5] + (wl,))
+        m0[t, :, :, 0, :, 3 * wl :] = part.reshape(m0.shape[1:3] + (m0.shape[4], wl))
 
     partners = [(here.dev_c, z), (here.dev_x, z), (here.dev_y, z)]
     partners += [(here.dp, z + 1 - 2 * (z % 2)), (here.dp, (z + 2) % nz)]
@@ -1015,8 +1004,13 @@
         if 3 <= k <= nz + 1:
             mx.stage5(k - 3)
     ud.stage4(3)
-    ud.finish(out_ref)
-    mx.finish(out_ref)
+    up_sum, dn_sum = ud.total()
+    gup_out[...] = up_sum
+    gdn_out[...] = dn_sum
+    (mix_sum,) = mx.total()
+    for j in range(3):
+        gqkv_ref[j] = mix_sum[:, j * wl : (j + 1) * wl]
+    gout_ref[...] = jnp.transpose(mix_sum[:, 3 * wl :])
     ud.drain()
     mx.drain()
     for k in range(len(partners)):
@@ -1028,7 +1022,7 @@
 def last(gup, gdn, gwo, ghpre, qkv, att, gatt, wqkv, xt, lse, ext, vecg, bing):
     nz, nd = lax.axis_size("tensor"), lax.axis_size("dp")
     length, d = att.shape
-    rw, wide = d // nd, gup.shape[2]
+    rw, wide, wl = d // nd, gup.shape[2], d // nz
     blk = length // nz
     unit = (nz, nd // 2, 2, rw, wide)
     any_ = pl.BlockSpec(memory_space=pl.ANY)
@@ -1041,11 +1035,14 @@
         last_kernel,
         out_shape=(
             s((nz, blk, d), BF),
-            s((3, rw, wide), F32),
+            s((3, rw, wl), F32),
+            s((wl, rw), F32),
+            s((rw, wide), F32),
+            s((rw, wide), F32),
             s(vec_shape, F32),
         ),
         in_specs=[any_] * 9 + [vmem] * 4,
-        out_specs=(any_, vmem, vmem),
+        out_specs=(any_,) + (vmem,) * 5,
         scratch_shapes=[
             pltpu.VMEM((2, 5, length, LANES), BF),
             pltpu.VMEM((3, length, d), BF),
@@ -1069,8 +1066,8 @@
             dma((2,)),
             dma((3,)),
             dma((2, nz)),
-            dma((3, nz, 7)),
-            dma((3, nz, 7)),
+            dma((2, 6)),
+            dma((2, nz, 7)),
             dma((nz,)),
             dma((nz,)),
             dma((steps,)),
@@ -1089,6 +1086,48 @@
 LAST_LIMIT = 61 * 1024 * 1024
 
 
+def finish_kernel(lrows, grows, gqkv, gout, gup, gdn, sums, *outs):
+    (
+        layer_out, grad_tokens, o_qkv, o_qvb, o_out, o_outb, o_gain1, o_shift1,
+        o_up, o_upb, o_dn, o_dnb, o_gain2, o_shift2,
+    ) = outs
+    layer_out[...] = lrows[...]
+    grad_tokens[...] = grows[...].astype(F32)
+
+    @pl.when(pl.program_id(0) == 0)
+    def _():
+        d = sums.shape[1]
+        for dst, src in ((o_qkv, gqkv), (o_out, gout), (o_up, gup), (o_dn, gdn)):
+            dst[...] = src[...]
+        for r, dst in enumerate((o_outb, o_gain1, o_shift1, o_dnb, o_gain2, o_shift2)):
+            dst[...] = sums[r, :]
+        for r in range(o_upb.shape[0] // d):
+            o_upb[r * d : (r + 1) * d] = sums[8 + r, :]
+        o_qvb[...] = sums[sums.shape[0] - 2 :, :]
+
+
+def finish(lrows, grows, gqkv, gout, gup, gdn, sums, hidden):
+    nz, blk, d = lrows.shape
+    rows = pl.BlockSpec((1, blk, d), lambda i: (i, 0, 0))
+    s = jax.ShapeDtypeStruct
+    same = lambda a: s(a.shape, a.dtype)
+    vector = s((d,), F32)
+    outs = (
+        same(lrows), s(grows.shape, F32), same(gqkv), s((2, d), F32), same(gout), vector, vector, vector,
+        same(gup), s((hidden,), F32), same(gdn), vector, vector, vector,
+    )
+    whole = lambda a: pl.BlockSpec(a.shape, lambda i: (0,) * len(a.shape))
+    return pl.pallas_call(
+        finish_kernel,
+        grid=(nz,),
+        out_shape=outs,
+        in_specs=[rows, rows] + [whole(a) for a in (gqkv, gout, gup, gdn, sums)],
+        out_specs=[rows, rows] + [whole(a) for a in outs[2:]],
+        compiler_params=pltpu.CompilerParams(vmem_limit_bytes=VMEM_LIMIT),
+        name="finish",
+    )(lrows, grows, gqkv, gout, gup, gdn, sums)
+
+
 def plain_attend_kernel(q_ref, k_ref, v_ref, segc_ref, o_ref, lse_ref, kx_s, qx_s, vt_s):
     doc_lanes(segc_ref[...], kx_s, qx_s)
     vt_s[:, HD:, :] = jnp.ones((2, vt_s.shape[1] - HD, vt_s.shape[2]), BF)
@@ -1124,7 +1163,7 @@
     nz = lax.axis_size("tensor")
     length, d = segment_ids.shape[1], tokens.shape[2]
     pairs, col, seg, lse_spec, wide = plain_specs(length, d)
-    mix = jnp.concatenate((qkv_w[0], qkv_w[1], qkv_w[2], wo_w), axis=1)
+    mix = jnp.concatenate((qkv_w[0], qkv_w[1], qkv_w[2], wo_w.T), axis=1)
     shards = jnp.stack((mix, up_w, dn_w))
     ids = lax.dynamic_index_in_dim(segment_ids, lax.axis_index("tensor"), 0, keepdims=False)
     segc = jnp.broadcast_to(ids[:, None], (length, LANES))
@@ -1149,7 +1188,8 @@
         compiler_params=pltpu.CompilerParams(vmem_limit_bytes=VMEM_LIMIT),
         name="plain_attend",
     )(qkv, qkv, qkv, segc)
-    return x, cot, w[1:], qkv, wqkv, rows.T, wo, att, lse, segc
+    wud = w[1:].reshape(2, nz, 8, d // 8, -1).transpose(1, 2, 0, 3, 4)
+    return x, cot, wud, qkv, wqkv, rows.T, wo, att, lse, segc
 
 
 def plain_last(gup, gdn, gwo, ghpre, qkv, att, gatt, wqkv, xt, lse, segc, vecg, bing):
@@ -1179,13 +1219,18 @@
         lax.psum_scatter(p.reshape(nz * d, -1), axes, scatter_dimension=0, tiled=True)
         for p in (gmix, gup, gdn)
     ]
+    mix_sum, up_sum, dn_sum = [p.astype(F32) for p in parts]
+    wl = d // nz
     sums = [jnp.sum(grads[j].astype(F32), axis=0, keepdims=True) for j in (0, 2)]
     bing = bing.reshape(-1, d)
     gap = jnp.zeros((6 - bing.shape[0], d), F32)
     vec = jnp.concatenate((vecg, bing, gap, *sums), axis=0)
     return (
         lax.all_to_all(split(gx), "tensor", 0, 0),
-        jnp.stack(parts).astype(F32),
+        jnp.stack([mix_sum[:, j * wl : (j + 1) * wl] for j in range(3)]),
+        mix_sum[:, 3 * wl :].T,
+        up_sum,
+        dn_sum,
         lax.psum(vec, axes),
     )
 
@@ -1202,36 +1247,20 @@
     comm = (nt, nd) == (4, 8)
     begin, end = (first, last) if comm else (plain_first, plain_last)
     x, cot, wud, qkv, wqkv, xt, wo, att, lse, ext = begin(
-        tokens, cotangent, qkv_w, wo_w.T, up_w, dn_w.T, qv_b, segment_ids
+        tokens, cotangent, qkv_w, wo_w, up_w, dn_w.T, qv_b, segment_ids
     )
     vecs = (wo_b, gain1, shift1, dn_b, gain2, shift2)
     layer_out, g_att, g_hpre, gup, gdn, gwo, vecg, bing = middle(
         comm, drop_flags, att, x.reshape(length, d), cot.reshape(length, d), cotangent, wo,
-        wud.reshape(2, nt, d, fl), vecs, up_b,
+        wud.reshape(nt, -1, 2, *wud.shape[-2:]), vecs, up_b,
     )
     if not comm:
         layer_out = lax.all_to_all(layer_out.reshape(nt, length // nt, d), "tensor", 0, 0)
-    rows, grads, total = end(
+    rows, g_qkv, g_out, g_up, g_dn, total = end(
         gup, gdn, gwo, g_hpre, qkv, att, g_att, wqkv, xt, lse, ext, vecg, bing
     )
-    g_mix, g_up, g_dn = grads[0], grads[1], grads[2]
-    n_bin = nt * fl // d
-    return (
-        layer_out,
-        rows.astype(F32),
-        jnp.stack([g_mix[:, j * wl : (j + 1) * wl] for j in range(3)]),
-        total[-2:],
-        g_mix[:, 3 * wl :].T,
-        total[0],
-        total[1],
-        total[2],
-        g_up,
-        total[8 : 8 + n_bin].reshape(-1),
-        g_dn.T,
-        total[3],
-        total[4],
-        total[5],
-    )
+    outs = finish(layer_out, rows, g_qkv, g_out, g_up, g_dn, total, nt * fl)
+    return (*outs[:10], outs[10].T, *outs[11:])
 
 
 def solution(mesh):

time: 272 us -> 258 us (0.949)
  the two profiles are of different devices: /device:TPU:0 before, /device:TPU:8 now
where the time goes in v5:
time: 258 us; the launch traced here: 253 us
  Pallas kernels  252 us (98%)
    pallas_call x1, Pallas kernels, last(): pl.pallas_call(last_kernel, out_shape=(s((nz, blk, d), BF), s((3, rw, wl)...  103 us
    pallas_call x1, Pallas kernels, first(): pl.pallas_call(first_kernel, out_shape=(s(tokens.shape, BF), s(tokens.sha...  82.7 us
    pallas_call x1, Pallas kernels, middle(): pl.pallas_call(functools.partial(middle_kernel, comm, nr), grid=(nr + par...  61.4 us
    pallas_call x1, Pallas kernels, finish(): pl.pallas_call(finish_kernel, grid=(nz,), out_shape=outs, in_specs=[rows,...  5.32 us

profile of v5, /device:TPU:8, one launch (start us, length us, event | category | flops | bytes accessed | tf_op | source)
XLA Modules:
  0.0 253.4 jit_solution(16697889056370536009)
XLA Ops:
  0.6 82.7 %first.1 = (bf16[4,256,768]{2,1,0:T(8,128)(2,1)}, bf16[4,256,768]{2,1,0:T(8,128)(2,1)}, bf16[4,4,2,2,96,768]{5,4,3,2,1,0:T(8,128)(2,1)}, bf16[1024,2304]{1,0:T(8...) custom-call(bf16[4,256,768]{2,1,0:T(8,128)(2,1)} %tok_ref.1, ...), custom_call_target="tpu_custom_call" | custom-call | tf_op jit(solution)/shard_map/first/pallas_call | solution.py:790
  83.4 61.4 %middle.1 = (bf16[4,256,768]{2,1,0:T(8,128)(2,1)}, bf16[1024,768]{1,0:T(8,128)(2,1)}, f32[1024,768]{1,0:T(8,128)}, bf16[4,768,768]{2,1,0:T(8,128)(2,1)}, bf16[4,...) custom-call(s32[4]{0:T(128)} %refs_0_.1, ...), custom_call_target="tpu_custom_call" | custom-call | tf_op jit(solution)/shard_map/middle/pallas_call | solution.py:618
  144.8 102.8 %last.1 = (bf16[4,256,768]{2,1,0:T(8,128)(2,1)}, f32[3,96,192]{2,1,0:T(8,128)}, f32[192,96]{1,0:T(8,128)}, f32[96,768]{1,0:T(8,128)}, f32[96,768]{1,0:T(8,128)}, /*index=5*/f32[16,768]{1,0:T(8,128)}) custom-call(bf16[4,4,2,96,768]{4,3,2,1,0:T(8,128)(2,1)} %bitcast.10, bf16[4,4,2,96,768]{4,3,2,1,0:T(8,128)(2,1)} %bitcast.11, ...), custom_call_target="tpu_custom_call" | custom-call | tf_op jit(solution)/shard_map/last/pallas_call | solution.py:1034
  247.6 5.3 %finish.1 = (bf16[4,256,768]{2,1,0:T(8,128)(2,1)}, f32[4,256,768]{2,1,0:T(8,128)}, f32[3,96,192]{2,1,0:T(8,128)}, f32[2,768]{1,0:T(2,128)}, f32[192,96]{1,0:T(8,...) custom-call(bf16[4,256,768]{2,1,0:T(8,128)(2,1)} %get-tuple-element., ...), custom_call_target="tpu_custom_call" | custom-call | tf_op jit(solution)/shard_map/finish/pallas_call | solution.py:1120

commit v6 on v5

--- a/solution.py
+++ b/solution.py
@@ -70,12 +70,11 @@
     kt_s[...] = jnp.transpose(k_ref[...])
     sub = lax.broadcasted_iota(jnp.int32, (8, LANES), 0)
     lane = lax.broadcasted_iota(jnp.int32, (8, LANES), 1)
-    pick = jnp.where(lane // HD == sub, 1.0, 0.0).astype(F32)
+    pick = jnp.where(lane // HD == sub, 1.0, 0.0).astype(BF)
     prod = g_ref[...].astype(F32) * att_ref[...].astype(F32)
-    delta_s[...] = lax.dot_general(
-        pick, prod, (((1,), (1,)), ((), ())),
-        preferred_element_type=F32, precision=lax.Precision.HIGHEST,
-    )
+    upper = prod.astype(BF)
+    lower = (prod - upper.astype(F32)).astype(BF)
+    delta_s[...] = dot_nt(pick, upper) + dot_nt(pick, lower)
     for i in range(length // QB):
         at = slice(i * QB, (i + 1) * QB)
         kx = kx_s[...]
@@ -1108,7 +1107,7 @@
 
 def finish(lrows, grows, gqkv, gout, gup, gdn, sums, hidden):
     nz, blk, d = lrows.shape
-    rows = pl.BlockSpec((1, blk, d), lambda i: (i, 0, 0))
+    rows = pl.BlockSpec((nz // 2, blk, d), lambda i: (i, 0, 0))
     s = jax.ShapeDtypeStruct
     same = lambda a: s(a.shape, a.dtype)
     vector = s((d,), F32)
@@ -1119,7 +1118,7 @@
     whole = lambda a: pl.BlockSpec(a.shape, lambda i: (0,) * len(a.shape))
     return pl.pallas_call(
         finish_kernel,
-        grid=(nz,),
+        grid=(2,),
         out_shape=outs,
         in_specs=[rows, rows] + [whole(a) for a in (gqkv, gout, gup, gdn, sums)],
         out_specs=[rows, rows] + [whole(a) for a in outs[2:]],

time: 258 us -> 252 us (0.977)
  the two profiles are of different devices: /device:TPU:8 before, /device:TPU:0 now
where the time goes in v6:
time: 252 us; the launch traced here: 250 us
  Pallas kernels  249 us (99%)
    pallas_call x1, Pallas kernels, last(): pl.pallas_call(last_kernel, out_shape=(s((nz, blk, d), BF), s((3, rw, wl)...  100 us
    pallas_call x1, Pallas kernels, first(): pl.pallas_call(first_kernel, out_shape=(s(tokens.shape, BF), s(tokens.sha...  88.5 us
    pallas_call x1, Pallas kernels, middle(): pl.pallas_call(functools.partial(middle_kernel, comm, nr), grid=(nr + par...  56.2 us

profile of v6, /device:TPU:0, one launch (start us, length us, event | category | flops | bytes accessed | tf_op | source)
XLA Modules:
  0.0 250.0 jit_solution(12690592896563740235)
XLA Ops:
  0.6 88.5 %first.1 = (bf16[4,256,768]{2,1,0:T(8,128)(2,1)}, bf16[4,256,768]{2,1,0:T(8,128)(2,1)}, bf16[4,4,2,2,96,768]{5,4,3,2,1,0:T(8,128)(2,1)}, bf16[1024,2304]{1,0:T(8...) custom-call(bf16[4,256,768]{2,1,0:T(8,128)(2,1)} %tok_ref.1, ...), custom_call_target="tpu_custom_call" | custom-call | tf_op jit(solution)/shard_map/first/pallas_call | solution.py:789
  89.1 56.2 %middle.1 = (bf16[4,256,768]{2,1,0:T(8,128)(2,1)}, bf16[1024,768]{1,0:T(8,128)(2,1)}, f32[1024,768]{1,0:T(8,128)}, bf16[4,768,768]{2,1,0:T(8,128)(2,1)}, bf16[4,...) custom-call(s32[4]{0:T(128)} %refs_0_.1, ...), custom_call_target="tpu_custom_call" | custom-call | tf_op jit(solution)/shard_map/middle/pallas_call | solution.py:617
  145.3 100.0 %last.1 = (bf16[4,256,768]{2,1,0:T(8,128)(2,1)}, f32[3,96,192]{2,1,0:T(8,128)}, f32[192,96]{1,0:T(8,128)}, f32[96,768]{1,0:T(8,128)}, f32[96,768]{1,0:T(8,128)}, /*index=5*/f32[16,768]{1,0:T(8,128)}) custom-call(bf16[4,4,2,96,768]{4,3,2,1,0:T(8,128)(2,1)} %bitcast.10, bf16[4,4,2,96,768]{4,3,2,1,0:T(8,128)(2,1)} %bitcast.11, ...), custom_call_target="tpu_custom_call" | custom-call | tf_op jit(solution)/shard_map/last/pallas_call | solution.py:1033
  245.3 4.4 %finish.1 = (bf16[4,256,768]{2,1,0:T(8,128)(2,1)}, f32[4,256,768]{2,1,0:T(8,128)}, f32[3,96,192]{2,1,0:T(8,128)}, f32[2,768]{1,0:T(2,128)}, f32[192,96]{1,0:T(8,...) custom-call(bf16[4,256,768]{2,1,0:T(8,128)(2,1)} %get-tuple-element., ...), custom_call_target="tpu_custom_call" | custom-call | tf_op jit(solution)/shard_map/finish/pallas_call | solution.py:1119

commit v7 on v6

--- a/solution.py
+++ b/solution.py
@@ -285,10 +285,12 @@
 
         h.sides(s, body)
 
-    def drain(self):
+    def arrive(self):
+        landed(self.w.at[:, :, 1 - self.here.core], self.all_cores)
+        self.own_copy().wait()
+
+    def sent(self):
         h, w = self.here, self.w
-        landed(w.at[:, :, 1 - h.core], self.all_cores)
-        self.own_copy().wait()
         for kind in (0, 1, 2, 5, 6, 7):
             landed(w.at[:, h.yx, h.core], self.send(kind))
         landed(w.at[:, h.yx_x, h.core, :, self.low], self.send(3))
@@ -698,17 +700,17 @@
     mix.stage1(0)
     sh_ref[1] = upw_ref[...]
     sh_ref[2] = dnw_ref[...]
-    seg = jnp.transpose(jnp.broadcast_to(seg_ref[pl.ds(here.z, 1), :], (LANES, length)))
-    doc_lanes(seg, kx_s, qx_s)
-    ext_ref[:, :LANES] = kx_s[:, LANES:]
-    ext_ref[:, LANES:] = qx_s[:, LANES:]
-    vt_s[:, HD:, :] = jnp.ones((2, vt_s.shape[1] - HD, length), BF)
     rest.stage1(0)
     mix.stage1(1)
     mix.stage1(2)
     rest.stage1(1)
     mix.stage1(3)
     tokens.start()
+    seg = jnp.transpose(jnp.broadcast_to(seg_ref[pl.ds(here.z, 1), :], (LANES, length)))
+    doc_lanes(seg, kx_s, qx_s)
+    ext_ref[:, :LANES] = kx_s[:, LANES:]
+    ext_ref[:, LANES:] = qx_s[:, LANES:]
+    vt_s[:, HD:, :] = jnp.ones((2, vt_s.shape[1] - HD, length), BF)
     mix.stage2(0)
     mix.stage2(1)
     mix.stage3(0)
@@ -719,7 +721,7 @@
     mix.stage3(3)
     rest.stage2(0)
     rest.stage1(2)
-    mix.drain()
+    mix.arrive()
     assemble(lambda t: mix_s[t].reshape(d, -1), nz, wqkv_s, wo_ref)
     out_w.start()
     bias = jnp.concatenate(
@@ -767,7 +769,9 @@
         lse_ref[p] = lse
 
     every_pair(pairs, work, between)
-    rest.drain()
+    rest.arrive()
+    rest.sent()
+    mix.sent()
     tokens.wait_send()
     cots.wait_recv()
     cots.wait_send()
@@ -942,10 +946,8 @@
             hpre_load(place_of[i + 1], (i + 1) % 2).start()
         hpre_load(to, i % 2).wait()
         at = pl.ds(pl.multiple_of(to * blk, blk), blk)
-        total = hpre_s[i % 2]
-        for j in range(3):
-            total = total + dot_nt(g_s[j, at, :], w_s[:, j * d : (j + 1) * d])
-        gx_s[to] = total.astype(BF)
+        g_rows = jnp.concatenate([g_s[j, at, :] for j in range(3)], axis=1)
+        gx_s[to] = (hpre_s[i % 2] + dot_nt(g_rows, w_s[...])).astype(BF)
         if i + 1 < nz:
             rows.copy((2, 3, 1)[i]).start()
         else:

time: 252 us -> 252 us (level)
  no operation moved by 1% of the time
where the time goes in v7:
time: 252 us; the launch traced here: 251 us
  Pallas kernels  250 us (99%)
    pallas_call x1, Pallas kernels, last(): pl.pallas_call(last_kernel, out_shape=(s((nz, blk, d), BF), s((3, rw, wl)...  101 us
    pallas_call x1, Pallas kernels, first(): pl.pallas_call(first_kernel, out_shape=(s(tokens.shape, BF), s(tokens.sha...  88.5 us
    pallas_call x1, Pallas kernels, middle(): pl.pallas_call(functools.partial(middle_kernel, comm, nr), grid=(nr + par...  56.2 us

profile of v7, /device:TPU:0, one launch (start us, length us, event | category | flops | bytes accessed | tf_op | source)
XLA Modules:
  0.0 250.9 jit_solution(11192137068175317989)
XLA Ops:
  0.6 88.5 %first.1 = (bf16[4,256,768]{2,1,0:T(8,128)(2,1)}, bf16[4,256,768]{2,1,0:T(8,128)(2,1)}, bf16[4,4,2,2,96,768]{5,4,3,2,1,0:T(8,128)(2,1)}, bf16[1024,2304]{1,0:T(8...) custom-call(bf16[4,256,768]{2,1,0:T(8,128)(2,1)} %tok_ref.1, ...), custom_call_target="tpu_custom_call" | custom-call | tf_op jit(solution)/shard_map/first/pallas_call | solution.py:793
  89.2 56.2 %middle.1 = (bf16[4,256,768]{2,1,0:T(8,128)(2,1)}, bf16[1024,768]{1,0:T(8,128)(2,1)}, f32[1024,768]{1,0:T(8,128)}, bf16[4,768,768]{2,1,0:T(8,128)(2,1)}, bf16[4,...) custom-call(s32[4]{0:T(128)} %refs_0_.1, ...), custom_call_target="tpu_custom_call" | custom-call | tf_op jit(solution)/shard_map/middle/pallas_call | solution.py:619
  145.3 100.9 %last.1 = (bf16[4,256,768]{2,1,0:T(8,128)(2,1)}, f32[3,96,192]{2,1,0:T(8,128)}, f32[192,96]{1,0:T(8,128)}, f32[96,768]{1,0:T(8,128)}, f32[96,768]{1,0:T(8,128)}, /*index=5*/f32[16,768]{1,0:T(8,128)}) custom-call(bf16[4,4,2,96,768]{4,3,2,1,0:T(8,128)(2,1)} %bitcast.10, bf16[4,4,2,96,768]{4,3,2,1,0:T(8,128)(2,1)} %bitcast.11, ...), custom_call_target="tpu_custom_call" | custom-call | tf_op jit(solution)/shard_map/last/pallas_call | solution.py:1035
  246.3 4.4 %finish.1 = (bf16[4,256,768]{2,1,0:T(8,128)(2,1)}, f32[4,256,768]{2,1,0:T(8,128)}, f32[3,96,192]{2,1,0:T(8,128)}, f32[2,768]{1,0:T(2,128)}, f32[192,96]{1,0:T(8,...) custom-call(bf16[4,256,768]{2,1,0:T(8,128)(2,1)} %get-tuple-element., ...), custom_call_target="tpu_custom_call" | custom-call | tf_op jit(solution)/shard_map/finish/pallas_call | solution.py:1121
